TPU v7x, 32 devices: a whole 2x2x4 slice. The times are simulated.
32 devices in a mesh: ctx: 4 (over y, x), fsdp: 8 (over z, core).
Axes of the slice: x: 2, y: 2, z: 4, core: 2. Of those that a mesh axis runs over, the one named last changes fastest.
Arguments:
- tokens: bfloat16 [8, 512, 2048], P('fsdp', 'ctx'), may hold values from -6 to 6
- cotangent: bfloat16 [8, 512, 2048], P('fsdp', 'ctx'), may hold values from -6 to 6
- block_ids: int32 [8, 512], P('fsdp', 'ctx'), may hold values from 0 to 2, as said below
- span_order: int32 [8, 8], P('fsdp'), may hold values from 0 to 7, as said below
- attn_gain: bfloat16 [2048], P('fsdp'), may hold values from 0.099609375 to 1.8984375
- w_qkv: bfloat16 [2048, 3, 2048], P('fsdp'), may hold values from -0.125 to 0.125
- w_out: bfloat16 [2048, 2048], P('fsdp'), may hold values from -0.75 to 0.75
- ffn_gain: bfloat16 [2048], P('fsdp'), may hold values from 0.099609375 to 1.8984375
- w_gate_up: bfloat16 [2048, 2, 8192], P('fsdp'), may hold values from -0.125 to 0.125
- w_down: bfloat16 [8192, 2048], P('fsdp'), may hold values from -0.0625 to 0.0625
Outputs:
- layer_out: bfloat16 [8, 512, 2048], P('fsdp', 'ctx')
- input_grad: bfloat16 [8, 512, 2048], P('fsdp', 'ctx')
- grad_attn_gain: float32 [2048], P('fsdp')
- grad_qkv: float32 [2048, 3, 2048], P('fsdp')
- grad_out: float32 [2048, 2048], P('fsdp')
- grad_ffn_gain: float32 [2048], P('fsdp')
- grad_gate_up: float32 [2048, 2, 8192], P('fsdp')
- grad_down: float32 [8192, 2048], P('fsdp')
Inputs may be any that keep to these rules, and one draw needn't show every extreme that they name: Each row is an ordering of 0 to 7; stored row i of a sequence holds position span_order[s, i // 64] * 64 + i % 64. `block_ids`: in order of positions the block numbers of a sequence start at 0, never fall and rise by one at a time; every sequence has exactly 3 blocks, each covering 1 to 256 consecutive positions, and one block of every sequence covers exactly 256.
All inputs are finite; a program needn't handle non-finite values.
Results may differ from a plain program's by a relative error of at most 0.023.
Values may be sent and summed in bfloat16 or wider, within the bound.
No kernel may reach another device: no remote copies, remote signals or barrier semaphores. Data moves between devices by JAX's collectives and lax.ppermute only.
A program may use at most 576 MiB of HBM per device.

v0:
```python
import jax
import jax.numpy as jnp
from jax import lax
from jax.sharding import PartitionSpec as P

HD = 64


rope_theta = 130000.0
norm_eps = 1e-05
score_scale = 0.125
masked_score = -1e30


def shifted(array, axis, by):
    size = lax.axis_size(axis)
    return lax.ppermute(array, axis, [(i, (i + by) % size) for i in range(size)])


def angles(positions, width):
    half_width = width // 2
    frequency = rope_theta ** (-2.0 * jnp.arange(half_width, dtype=jnp.float32) / width)
    phases = positions.astype(jnp.float32)[:, None] * frequency[None, :]
    return (jnp.cos(phases)[:, None, :], jnp.sin(phases)[:, None, :])


def rotate(values, cosine, sine):
    half_width = values.shape[-1] // 2
    leading = values[..., :half_width]
    trailing = values[..., half_width:]
    return jnp.concatenate(
        [leading * cosine - trailing * sine, trailing * cosine + leading * sine], -1
    )


def inverse_rms(values):
    return lax.rsqrt(jnp.mean(values * values, -1, keepdims=True) + norm_eps)


def norm_back(grad_normed, normed, gain, inverse):
    scaled = grad_normed * gain
    return inverse * (scaled - normed * jnp.mean(scaled * normed, -1, keepdims=True))


def contract_rows(picked, right):
    return lax.dot_general(
        picked, right, (((0,), (0,)), ((), ())), preferred_element_type=jnp.float32
    )


def sectioned_rows(left, right):
    return lax.psum_scatter(
        contract_rows(left, right).astype(jnp.bfloat16), "fsdp", scatter_dimension=0, tiled=True
    ).astype(jnp.float32)


def per_device(
    tokens, cotangent, block_ids, span_order, attn_gain, w_qkv, w_out, ffn_gain, w_gate_up, w_down
):
    local_rows = tokens.shape[1]
    width = tokens.shape[2]
    heads = width // HD
    ctx_count = lax.axis_size("ctx")
    inputs = tokens[0].astype(jnp.float32)
    query_blocks = block_ids[0]
    half_rows = local_rows // 2
    row_ids = jnp.arange(local_rows, dtype=jnp.int32)
    slots = 2 * lax.axis_index("ctx") + row_ids // half_rows
    order_row = span_order[0]
    matches = slots[:, None] == jnp.arange(order_row.shape[0], dtype=jnp.int32)[None, :]
    picked = jnp.sum(jnp.where(matches, order_row[None, :], 0), axis=1)
    positions = picked * half_rows + row_ids % half_rows
    cosine, sine = angles(positions, HD)
    inverse_one = inverse_rms(inputs)
    normed_one = inputs * inverse_one
    gain_one, qkv_full, out_full = (
        lax.all_gather(attn_gain, "fsdp", axis=0, tiled=True),
        lax.all_gather(w_qkv, "fsdp", axis=0, tiled=True),
        lax.all_gather(w_out, "fsdp", axis=0, tiled=True),
    )
    gain_one = gain_one.astype(jnp.float32)
    act_one = (normed_one * gain_one).astype(jnp.bfloat16)
    qkv = jnp.einsum("td,dke->tke", act_one, qkv_full, preferred_element_type=jnp.float32)
    query = rotate(qkv[:, 0].reshape(local_rows, heads, HD), cosine, sine).astype(jnp.bfloat16)
    key_own = rotate(qkv[:, 1].reshape(local_rows, heads, HD), cosine, sine).astype(jnp.bfloat16)
    value_own = qkv[:, 2].reshape(local_rows, heads, HD).astype(jnp.bfloat16)
    all_blocks = lax.all_gather(query_blocks, "ctx", axis=0, tiled=True)

    def visible(start, count):
        key_blocks = lax.dynamic_slice_in_dim(all_blocks, start, count)
        return key_blocks[None, None, :] <= query_blocks[:, None, None]

    running_top = jnp.full((local_rows, heads), masked_score, jnp.float32)
    key_part = lax.all_gather(key_own, "ctx", axis=0, tiled=True)
    value_part = lax.all_gather(value_own, "ctx", axis=0, tiled=True)
    allowed = visible(jnp.int32(0), key_part.shape[0])
    scores = (
        jnp.einsum("qhe,khe->qhk", query, key_part, preferred_element_type=jnp.float32)
        * score_scale
    )
    scores = jnp.where(allowed, scores, masked_score)
    new_top = jnp.maximum(running_top, jnp.max(scores, -1))
    weights = jnp.where(allowed, jnp.exp(scores - new_top[..., None]), 0.0)
    accum = jnp.einsum(
        "qhk,khe->qhe", weights.astype(jnp.bfloat16), value_part, preferred_element_type=jnp.float32
    )
    running_top, running_total, accum = (new_top, jnp.sum(weights, -1), accum)
    attended = accum / running_total[..., None]
    log_total = running_top + jnp.log(running_total)
    attn_b = attended.reshape(local_rows, width).astype(jnp.bfloat16)
    resid = inputs + jnp.dot(attn_b, out_full, preferred_element_type=jnp.float32)
    inverse_two = inverse_rms(resid)
    normed_two = resid * inverse_two
    gain_two, gate_up_full, down_full = (
        lax.all_gather(ffn_gain, "fsdp", axis=0, tiled=True),
        lax.all_gather(w_gate_up, "fsdp", axis=0, tiled=True),
        lax.all_gather(w_down, "fsdp", axis=0, tiled=True),
    )
    gain_two = gain_two.astype(jnp.float32)
    act_two = (normed_two * gain_two).astype(jnp.bfloat16)
    gate_up = jnp.einsum("td,dkf->tkf", act_two, gate_up_full, preferred_element_type=jnp.float32)
    gate = gate_up[:, 0]
    upward = gate_up[:, 1]
    sigma = jax.nn.sigmoid(gate)
    swish = gate * sigma
    hidden = (swish * upward).astype(jnp.bfloat16)
    output = resid + jnp.dot(hidden, down_full, preferred_element_type=jnp.float32)
    layer_out = output.astype(jnp.bfloat16)[None]
    grad_out_rows = cotangent[0]
    grad_hidden = lax.dot_general(
        grad_out_rows, down_full, (((1,), (1,)), ((), ())), preferred_element_type=jnp.float32
    )
    grad_gate = grad_hidden * upward * sigma * (1.0 + gate * (1.0 - sigma))
    grad_up = grad_hidden * swish
    grad_gu = jnp.stack([grad_gate, grad_up], 1).astype(jnp.bfloat16)
    grad_act_two = jnp.einsum(
        "tkf,dkf->td", grad_gu, gate_up_full, preferred_element_type=jnp.float32
    )
    grad_gain_two = jnp.sum(grad_act_two * normed_two, 0)
    grad_resid = grad_out_rows.astype(jnp.float32) + norm_back(
        grad_act_two, normed_two, gain_two, inverse_two
    )
    grad_branch = grad_resid.astype(jnp.bfloat16)
    grad_attended = lax.dot_general(
        grad_branch, out_full, (((1,), (1,)), ((), ())), preferred_element_type=jnp.float32
    )
    grad_attended = grad_attended.astype(jnp.bfloat16).reshape(local_rows, heads, HD)
    delta = jnp.sum(grad_attended.astype(jnp.float32) * attended, -1)

    def key_terms(key_part, value_part, start):
        allowed = visible(start, key_part.shape[0])
        scores = (
            jnp.einsum("qhe,khe->qhk", query, key_part, preferred_element_type=jnp.float32)
            * score_scale
        )
        probs = jnp.where(allowed, jnp.exp(scores - log_total[..., None]), 0.0)
        grad_value = jnp.einsum(
            "qhk,qhe->khe",
            probs.astype(jnp.bfloat16),
            grad_attended,
            preferred_element_type=jnp.float32,
        )
        grad_probs = jnp.einsum(
            "qhe,khe->qhk", grad_attended, value_part, preferred_element_type=jnp.float32
        )
        grad_scores = (probs * (grad_probs - delta[..., None])).astype(jnp.bfloat16)
        grad_query = (
            jnp.einsum("qhk,khe->qhe", grad_scores, key_part, preferred_element_type=jnp.float32)
            * score_scale
        )
        grad_key = (
            jnp.einsum("qhk,qhe->khe", grad_scores, query, preferred_element_type=jnp.float32)
            * score_scale
        )
        return (grad_query, grad_key, grad_value)

    def pass_step(step, carry):
        key_part, value_part, grad_key, grad_value, grad_query = carry
        owner = (lax.axis_index("ctx") - step) % ctx_count
        query_add, key_add, value_add = key_terms(key_part, value_part, owner * local_rows)
        key_part, value_part = shifted((key_part, value_part), "ctx", 1)
        grad_key, grad_value = (
            shifted((grad_key + key_add).astype(jnp.bfloat16), "ctx", 1).astype(jnp.float32),
            shifted((grad_value + value_add).astype(jnp.bfloat16), "ctx", 1).astype(jnp.float32),
        )
        return (key_part, value_part, grad_key, grad_value, grad_query + query_add)

    empty = jnp.zeros((local_rows, heads, HD), jnp.float32)
    final = lax.fori_loop(0, ctx_count, pass_step, (key_own, value_own, empty, empty, empty))
    grad_query, grad_key, grad_value = (final[4], final[2], final[3])
    grad_qkv_rows = jnp.stack(
        [
            rotate(grad_query, cosine, -sine).reshape(local_rows, width),
            rotate(grad_key, cosine, -sine).reshape(local_rows, width),
            grad_value.reshape(local_rows, width),
        ],
        1,
    ).astype(jnp.bfloat16)
    grad_act_one = jnp.einsum(
        "tke,dke->td", grad_qkv_rows, qkv_full, preferred_element_type=jnp.float32
    )
    grad_gain_one = jnp.sum(grad_act_one * normed_one, 0)
    grad_inputs = grad_resid + norm_back(grad_act_one, normed_one, gain_one, inverse_one)
    input_grad = grad_inputs.astype(jnp.bfloat16)[None]
    part_qkv = sectioned_rows(act_one, grad_qkv_rows)
    part_out = sectioned_rows(attn_b, grad_branch)
    part_gate_up = sectioned_rows(act_two, grad_gu)
    part_down = sectioned_rows(hidden, grad_out_rows)
    gain_parts = (
        lax.psum_scatter(grad_gain_one, "fsdp", scatter_dimension=0, tiled=True),
        lax.psum_scatter(grad_gain_two, "fsdp", scatter_dimension=0, tiled=True),
    )
    summed = (
        lax.psum(gain_parts[0].astype(jnp.bfloat16), "ctx").astype(jnp.float32),
        lax.psum(part_qkv.astype(jnp.bfloat16), "ctx").astype(jnp.float32),
        lax.psum(part_out.astype(jnp.bfloat16), "ctx").astype(jnp.float32),
        lax.psum(gain_parts[1].astype(jnp.bfloat16), "ctx").astype(jnp.float32),
        lax.psum(part_gate_up.astype(jnp.bfloat16), "ctx").astype(jnp.float32),
        lax.psum(part_down.astype(jnp.bfloat16), "ctx").astype(jnp.float32),
    )
    return (layer_out, input_grad, summed[0], summed[1], summed[2], summed[3], summed[4], summed[5])


def solution(mesh):
    return jax.shard_map(
        per_device,
        mesh=mesh,
        in_specs=(
            P("fsdp", "ctx", None),
            P("fsdp", "ctx", None),
            P("fsdp", "ctx"),
            P("fsdp", None),
            P("fsdp"),
            P("fsdp", None, None),
            P("fsdp", None),
            P("fsdp"),
            P("fsdp", None, None),
            P("fsdp", None),
        ),
        out_specs=(
            P("fsdp", "ctx", None),
            P("fsdp", "ctx", None),
            P("fsdp"),
            P("fsdp", None, None),
            P("fsdp", None),
            P("fsdp"),
            P("fsdp", None, None),
            P("fsdp", None),
        ),
        check_vma=False,
    )
```

profile of v0, /device:TPU:0, one launch (start us, length us, event | category | flops | bytes accessed | tf_op | source)
XLA Modules:
  0.0 3121.6 jit_solution(10979373377277663653)
XLA Ops:
  8.6 13.4 all-gather.1
  24.9 207.3 %all-gather.10.cloned.1.call-done = bf16[2048,3,2048]{2,0,1:T(8,128)(2,1)} async-done(((bf16[256,3,2048]{2,0,1:T(8,128)(2,1)}), bf16[2048,3,2048]{2,0,1:T(8,128)(2,1)}) %all-gather.10.cloned.1.call-update) | async-done | bytes 25165840 | tf_op jit(solution)/shard_map/all_gather | solution.py:78
  232.2 10.2 fusion.61
  255.9 13.1 copy.73
  295.8 27.1 all-gather.12.cloned.1.call-done
  330.4 76.1 %all-gather.16.cloned.1.call-done = bf16[2048,2048]{1,0:T(8,128)(2,1)} async-done(((bf16[256,2048]{1,0:T(8,128)(2,1)}), bf16[2048,2048]{1,0:T(8,128)(2,1)}) %all-gather.16.cloned.1.call-update) | async-done | bytes 8388624 | tf_op jit(solution)/shard_map/all_gather | solution.py:79
  411.3 559.8 %all-gather.18.cloned.1.call-done = bf16[2048,2,8192]{2,0,1:T(8,128)(2,1)} async-done(((bf16[256,2,8192]{2,0,1:T(8,128)(2,1)}), bf16[2048,2,8192]{2,0,1:T(8,128)(2,1)}) %all-gather.18.cloned.1.call-update) | async-done | bytes 67108880 | tf_op jit(solution)/shard_map/all_gather | solution.py:116
  971.1 31.7 %fusion.64 = f32[128,2,8192]{2,0,1:T(8,128)} fusion(bf16[2048,2,8192]{2,0,1:T(8,128)(2,1)} %all-gather.18.cloned.1.call-done, f32[128,2048]{1,0:T(8,128)S(1)} %get-tuple-element.443, f32[2048]{0:T(1024)S(1)} %bitcast.209, f32[128]{0:T(128)S(1)} %add_rsqrt_fusion), kind=kOutput, calls=%fused_computation.105 | convolution fusion | flops 8590721024 | bytes 76554752 | tf_op jit(solution)/shard_map/td,dkf->tkf/dot_general | solution.py:121
  1002.8 256.6 %all-gather.20.cloned.1.call-done = bf16[8192,2048]{1,0:T(8,128)(2,1)} async-done(((bf16[1024,2048]{1,0:T(8,128)(2,1)}), bf16[8192,2048]{1,0:T(8,128)(2,1)}) %all-gather.20.cloned.1.call-update) | async-done | bytes 33554448 | tf_op jit(solution)/shard_map/all_gather | solution.py:117
  1259.4 19.2 fusion.33
  1278.5 30.5 multiply_reduce_fusion
  1327.1 217.0 %while.24 = (s32[]{:T(128)}, bf16[128,32,64]{0,2,1:T(8,128)(2,1)S(1)}, bf16[128,32,64]{0,2,1:T(8,128)(2,1)}, f32[128,32,64]{0,2,1:T(8,128)}, f32[128,32,64]{0,2,...) while((s32[]{:T(128)}, ...), condition=%wide.region_8.9_spmd.clone, body=%wide.region_7.8_spmd.clone.sunk | while | flops 342376448 | bytes 36244028 | solution.py:189
  1351.7 9.1 collective-permute-done.3
  1362.9 9.0 collective-permute-done
  1371.9 10.7 collective-permute-done.1
  1407.3 9.1 collective-permute-done.3
  1418.6 9.0 collective-permute-done
  1427.6 9.8 collective-permute-done.1
  1462.1 9.1 collective-permute-done.3
  1516.0 9.1 collective-permute-done.3
  1548.2 11.9 convolution_convert_fusion.2
  1561.1 18.5 convolution_convert_fusion.1
  1580.8 28.1 convolution_convert_fusion
  1609.0 195.7 %reduce-scatter.5.cloned.1.call-done = bf16[256,3,2048]{2,0,1:T(8,128)(2,1)} async-done(((bf16[2048,3,2048]{2,0,1:T(8,128)(2,1)}), bf16[256,3,2048]{2,0,1:T(8,128)(2,1)}) %reduce-scatter.5.cloned.1.call-update) | async-done | bytes 3145744 | tf_op jit(solution)/shard_map/reduce_scatter | solution.py:52
  1804.8 326.3 %reduce-scatter.11.cloned.1.call-done = bf16[1024,2048]{1,0:T(8,128)(2,1)} async-done(((bf16[8192,2048]{1,0:T(8,128)(2,1)}), bf16[1024,2048]{1,0:T(8,128)(2,1)}) %reduce-scatter.11.cloned.1.call-update) | async-done | bytes 4194320 | tf_op jit(solution)/shard_map/reduce_scatter | solution.py:52
  2131.1 640.8 %reduce-scatter.9.cloned.1.call-done = bf16[256,2,8192]{2,0,1:T(8,128)(2,1)} async-done(((bf16[2048,2,8192]{2,0,1:T(8,128)(2,1)}), bf16[256,2,8192]{2,0,1:T(8,128)(2,1)}) %reduce-scatter.9.cloned.1.call-update) | async-done | bytes 8388624 | tf_op jit(solution)/shard_map/reduce_scatter | solution.py:52
  2773.8 14.8 fusion.47
  2788.6 25.9 all-reduce.2
  2814.6 10.3 all-reduce.3
  2828.5 19.9 fusion.29
  2848.4 236.1 %all-reduce.7.cloned.1.call-done = (bf16[256,2,8192]{2,0,1:T(8,128)(2,1)}, bf16[256,3,2048]{2,0,1:T(8,128)(2,1)}, bf16[256,2048]{1,0:T(8,128)(2,1)}, bf16[1024,2048]{1,0:T(8,128)(2,1)}) async-done(((bf16[256,2,8192]{2,0,1:T(8,128)(2,1)}, bf16[256,3,2048]{2,0,1:T(8,128)(2,1)}, bf16[256,2048]{1,0:T(8,128)(2,1)}, bf16[1024,2048]{1,0:T(8,128)(2,1)}), (bf16[256,2,8192]{2,0,1:T(8,128)(2,1)}, ...) | async-done | bytes 16777232 | tf_op jit(solution)/shard_map/psum | solution.py:218
  3092.0 18.2 copy.80
  (200 shorter events, 239.3 us)
Async XLA Ops:
  7.2 225.0 %all-gather.10.cloned.1.call-start = ((), (), s32[]{:S(2)}) async-start(), calls=%async_computation.4 | async-start | bytes 28311552 | tf_op jit(solution)/shard_map/all_gather | solution.py:78
  7.9 279.0 %all-gather.14.cloned.1.call-start = ((), (), s32[]{:S(2)}) async-start(), calls=%async_computation.6 | async-start | bytes 2621440 | tf_op jit(solution)/shard_map/all_gather | solution.py:94
  252.3 70.6 %all-gather.12.cloned.1.call-start = ((), (), s32[]{:S(2)}) async-start(), calls=%async_computation.5 | async-start | bytes 2621440 | tf_op jit(solution)/shard_map/all_gather | solution.py:95
  255.3 151.2 %all-gather.16.cloned.1.call-start = ((), (), s32[]{:S(2)}) async-start(), calls=%async_computation.7 | async-start | bytes 9437184 | tf_op jit(solution)/shard_map/all_gather | solution.py:79
  255.9 715.2 %all-gather.18.cloned.1.call-start = ((), (), s32[]{:S(2)}) async-start(), calls=%async_computation.8 | async-start | bytes 75497472 | tf_op jit(solution)/shard_map/all_gather | solution.py:116
  269.1 990.2 %all-gather.20.cloned.1.call-start = ((), (), s32[]{:S(2)}) async-start(), calls=%async_computation.9 | async-start | bytes 37748736 | tf_op jit(solution)/shard_map/all_gather | solution.py:117
  269.7 1339.3 %reduce-scatter.7.cloned.1.call-start = ((), (), s32[]{:S(2)}) async-start(), calls=%async_computation.11 | async-start | bytes 9437184 | tf_op jit(solution)/shard_map/reduce_scatter | solution.py:52
  295.8 110.7 %copy-start.7 = (bf16[1,128,2048]{2,1,0:T(8,128)(2,1)S(1)}, bf16[1,128,2048]{2,1,0:T(8,128)(2,1)}, u32[]{:S(2)}) copy-start(bf16[1,128,2048]{2,1,0:T(8,128)(2,1)} %param.12) | copy-start | bytes 1572868
  330.4 80.9 %copy-start.11 = (bf16[128,32,64]{0,2,1:T(8,128)(2,1)}, bf16[128,32,64]{0,2,1:T(8,128)(2,1)S(1)}, u32[]{:S(2)}) copy-start(bf16[128,32,64]{0,2,1:T(8,128)(2,1)S(1)} %get-tuple-element.440) | copy-start | bytes 1572868
  411.2 897.8 %copy-start.2 = (f32[128,2048]{1,0:T(8,128)}, f32[128,2048]{1,0:T(8,128)S(1)}, u32[]{:S(2)}) copy-start(f32[128,2048]{1,0:T(8,128)S(1)} %get-tuple-element.443) | copy-start | bytes 3145732
  1316.5 488.2 %reduce-scatter.5.cloned.1.call-start = ((), (), s32[]{:S(2)}) async-start(), calls=%async_computation.10 | async-start | bytes 28311552 | tf_op jit(solution)/shard_map/reduce_scatter | solution.py:52
  1327.1 218.6 %copy-start.20 = (f32[128,32]{0,1:T(8,128)S(1)}, f32[128,32]{0,1:T(8,128)}, u32[]{:S(2)}) copy-start(f32[128,32]{0,1:T(8,128)} %get-tuple-element.435) | copy-start | bytes 49156
  1333.6 16.0 collective-permute-start.2
  1336.5 24.2 collective-permute-start.3
  1338.0 33.9 %collective-permute-start = (bf16[128,32,64]{0,2,1:T(8,128)(2,1)S(1)}, bf16[128,32,64]{0,2,1:T(8,128)(2,1)S(1)}, u32[]{:S(2)}, u32[]{:S(2)}) collective-permute-start(bf16[128,32,64]{0,2,1:T(8,128)(2,1)S(1)} %copy.96), channel_id=1, source_target_pairs={{0,8},{8,16},{16,24},{24,0},{1,9},{9,17},{17,25},{25,1},{2,10},{10... | collective-permute-start | bytes 1572872 | tf_op jit(solution)/shard_map/while/body/eval_jaxpr/ppermute | solution.py:17
  1339.5 43.1 %collective-permute-start.1 = (bf16[128,32,64]{0,2,1:T(8,128)(2,1)S(1)}, bf16[128,32,64]{0,2,1:T(8,128)(2,1)}, u32[]{:S(2)}, u32[]{:S(2)}) collective-permute-start(bf16[128,32,64]{0,2,1:T(8,128)(2,1)S(1)} %copy.97), channel_id=1, source_target_pairs={{0,8},{8,16},{16,24},{24,0},{1,9},{9,17},{17,25},{25,1},{2,10},{10... | collective-permute-start | bytes 1572872 | tf_op jit(solution)/shard_map/while/body/eval_jaxpr/ppermute | solution.py:17
  1389.1 16.1 collective-permute-start.2
  1391.3 25.2 collective-permute-start.3
  1393.6 33.9 %collective-permute-start = (bf16[128,32,64]{0,2,1:T(8,128)(2,1)S(1)}, bf16[128,32,64]{0,2,1:T(8,128)(2,1)S(1)}, u32[]{:S(2)}, u32[]{:S(2)}) collective-permute-start(bf16[128,32,64]{0,2,1:T(8,128)(2,1)S(1)} %copy.96), channel_id=1, source_target_pairs={{0,8},{8,16},{16,24},{24,0},{1,9},{9,17},{17,25},{25,1},{2,10},{10... | collective-permute-start | bytes 1572872 | tf_op jit(solution)/shard_map/while/body/eval_jaxpr/ppermute | solution.py:17
  1394.2 43.2 %collective-permute-start.1 = (bf16[128,32,64]{0,2,1:T(8,128)(2,1)S(1)}, bf16[128,32,64]{0,2,1:T(8,128)(2,1)}, u32[]{:S(2)}, u32[]{:S(2)}) collective-permute-start(bf16[128,32,64]{0,2,1:T(8,128)(2,1)S(1)} %copy.97), channel_id=1, source_target_pairs={{0,8},{8,16},{16,24},{24,0},{1,9},{9,17},{17,25},{25,1},{2,10},{10... | collective-permute-start | bytes 1572872 | tf_op jit(solution)/shard_map/while/body/eval_jaxpr/ppermute | solution.py:17
  1443.9 16.1 collective-permute-start.2
  1445.6 25.6 collective-permute-start.3
  1448.5 33.9 %collective-permute-start = (bf16[128,32,64]{0,2,1:T(8,128)(2,1)S(1)}, bf16[128,32,64]{0,2,1:T(8,128)(2,1)S(1)}, u32[]{:S(2)}, u32[]{:S(2)}) collective-permute-start(bf16[128,32,64]{0,2,1:T(8,128)(2,1)S(1)} %copy.96), channel_id=1, source_target_pairs={{0,8},{8,16},{16,24},{24,0},{1,9},{9,17},{17,25},{25,1},{2,10},{10... | collective-permute-start | bytes 1572872 | tf_op jit(solution)/shard_map/while/body/eval_jaxpr/ppermute | solution.py:17
  1448.5 42.7 %collective-permute-start.1 = (bf16[128,32,64]{0,2,1:T(8,128)(2,1)S(1)}, bf16[128,32,64]{0,2,1:T(8,128)(2,1)}, u32[]{:S(2)}, u32[]{:S(2)}) collective-permute-start(bf16[128,32,64]{0,2,1:T(8,128)(2,1)S(1)} %copy.97), channel_id=1, source_target_pairs={{0,8},{8,16},{16,24},{24,0},{1,9},{9,17},{17,25},{25,1},{2,10},{10... | collective-permute-start | bytes 1572872 | tf_op jit(solution)/shard_map/while/body/eval_jaxpr/ppermute | solution.py:17
  1497.8 16.1 collective-permute-start.2
  1499.4 25.6 collective-permute-start.3
  1502.4 33.8 %collective-permute-start = (bf16[128,32,64]{0,2,1:T(8,128)(2,1)S(1)}, bf16[128,32,64]{0,2,1:T(8,128)(2,1)S(1)}, u32[]{:S(2)}, u32[]{:S(2)}) collective-permute-start(bf16[128,32,64]{0,2,1:T(8,128)(2,1)S(1)} %copy.96), channel_id=1, source_target_pairs={{0,8},{8,16},{16,24},{24,0},{1,9},{9,17},{17,25},{25,1},{2,10},{10... | collective-permute-start | bytes 1572872 | tf_op jit(solution)/shard_map/while/body/eval_jaxpr/ppermute | solution.py:17
  1502.4 41.7 %collective-permute-start.1 = (bf16[128,32,64]{0,2,1:T(8,128)(2,1)S(1)}, bf16[128,32,64]{0,2,1:T(8,128)(2,1)}, u32[]{:S(2)}, u32[]{:S(2)}) collective-permute-start(bf16[128,32,64]{0,2,1:T(8,128)(2,1)S(1)} %copy.97), channel_id=1, source_target_pairs={{0,8},{8,16},{16,24},{24,0},{1,9},{9,17},{17,25},{25,1},{2,10},{10... | collective-permute-start | bytes 1572872 | tf_op jit(solution)/shard_map/while/body/eval_jaxpr/ppermute | solution.py:17
  1560.1 571.0 %reduce-scatter.11.cloned.1.call-start = ((), (), s32[]{:S(2)}) async-start(), calls=%async_computation.13 | async-start | bytes 37748736 | tf_op jit(solution)/shard_map/reduce_scatter | solution.py:52
  1579.6 1192.3 %reduce-scatter.9.cloned.1.call-start = ((), (), s32[]{:S(2)}) async-start(), calls=%async_computation.12 | async-start | bytes 75497472 | tf_op jit(solution)/shard_map/reduce_scatter | solution.py:52
  1608.9 1475.6 %all-reduce.7.cloned.1.call-start = ((), (), s32[]{:S(2)}) async-start(), calls=%async_computation.14 | async-start | bytes 33554432 | tf_op jit(solution)/shard_map/psum | solution.py:218
  2773.8 52.3 %copy-start.6 = (f32[128,2048]{1,0:T(8,128)S(1)}, f32[128,2048]{1,0:T(8,128)}, u32[]{:S(2)}) copy-start(f32[128,2048]{1,0:T(8,128)} %copy-done.5) | copy-start | bytes 3145732
  (22 other events, 157.6 us)
Sparse Core Ops, SparseCore 0:
  9.6 222.5 all-gather.9
  252.5 33.3 all-gather.13
  287.7 35.1 all-gather.11
  324.4 82.0 all-gather.15
  408.5 562.5 all-gather.17
  972.5 286.8 all-gather.19
  1316.7 87.7 reduce-scatter.6
  1560.2 244.5 reduce-scatter.4
  1807.1 323.8 reduce-scatter.10
  2133.4 638.4 reduce-scatter.8
  2775.9 308.5 all-reduce.6
where the time goes:
time: 3130 us; the launch traced here: 3120 us
  waiting for transfers between devices  2670 us (85%)
  matrix products  250 us (8%)
  blocking collectives  66.6 us (2%)
  local copies, waits for them, and re-layouts  54.7 us (2%)
  other arithmetic  48.7 us (2%)
    reduce_scatter x4, waiting for transfers between devices, sectioned_rows(): lax.psum_scatter(contract_rows(left, right).astype(jnp.bfloat16), 'fsdp',...  1160 us
    all_gather x1, waiting for transfers between devices, per_device(): lax.all_gather(w_gate_up, 'fsdp', axis=0, tiled=True)  560 us
    all_gather x1, waiting for transfers between devices, per_device(): lax.all_gather(w_down, 'fsdp', axis=0, tiled=True)  257 us
    psum x1, waiting for transfers between devices, per_device(): lax.psum(part_gate_up.astype(jnp.bfloat16), 'ctx').astype(jnp.float32)  236 us
    all_gather x1, waiting for transfers between devices, per_device(): lax.all_gather(w_qkv, 'fsdp', axis=0, tiled=True)  207 us
    ppermute x16, waiting for transfers between devices, shifted(): lax.ppermute(array, axis, [(i, (i + by) % size) for i in range(size)])  138 us
    all_gather x1, waiting for transfers between devices, per_device(): lax.all_gather(w_out, 'fsdp', axis=0, tiled=True)  76.1 us
    dot_general x4, matrix products, contract_rows(): lax.dot_general(picked, right, (((0,), (0,)), ((), ())), preferred_elemen...  64.2 us
  transfers between devices with their start and end apart: 27, of which 25 were waited for; matrix products, arithmetic and copies ran while one was open for 8% of the time, Pallas kernels for 0%

commit v1 on v0

v1 whole, which is shorter than its diff:
```python
import jax
import jax.numpy as jnp
from jax import lax
from jax.sharding import PartitionSpec as P

HD = 64

rope_theta = 130000.0
norm_eps = 1e-05
score_scale = 0.125
masked_score = -1e30


def swapped(array, axis, by):
    size = lax.axis_size(axis)
    return lax.ppermute(array, axis, [(i, i ^ by) for i in range(size)])


def gathered(array, axis):
    return [array] + [swapped(array, axis, k) for k in range(1, lax.axis_size(axis))]


def scattered(parts, axis):
    total = parts[0].astype(jnp.float32)
    for k in range(1, lax.axis_size(axis)):
        total = total + swapped(parts[k].astype(jnp.bfloat16), axis, k).astype(jnp.float32)
    return total


def exchanged(blocks, axis):
    size = lax.axis_size(axis)
    own = lax.axis_index(axis)
    result = blocks
    for k in range(1, size):
        other = own ^ k
        block = lax.dynamic_index_in_dim(blocks, other, 0, keepdims=True)
        result = lax.dynamic_update_slice_in_dim(result, swapped(block, axis, k), other, 0)
    return result


def angles(positions, width):
    half_width = width // 2
    frequency = rope_theta ** (-2.0 * jnp.arange(half_width, dtype=jnp.float32) / width)
    phases = positions.astype(jnp.float32)[:, None] * frequency[None, :]
    return (jnp.cos(phases)[:, None, :], jnp.sin(phases)[:, None, :])


def rotate(values, cosine, sine):
    half_width = values.shape[-1] // 2
    leading = values[..., :half_width]
    trailing = values[..., half_width:]
    return jnp.concatenate(
        [leading * cosine - trailing * sine, trailing * cosine + leading * sine], -1
    )


def inverse_rms(values):
    return lax.rsqrt(jnp.mean(values * values, -1, keepdims=True) + norm_eps)


def norm_back(grad_normed, normed, gain, inverse):
    scaled = grad_normed * gain
    return inverse * (scaled - normed * jnp.mean(scaled * normed, -1, keepdims=True))


def product(left, right, left_dim, right_dim):
    return lax.dot_general(
        left, right, (((left_dim,), (right_dim,)), ((), ())), preferred_element_type=jnp.float32
    )


def low(values):
    return values.astype(jnp.bfloat16)


def gather_rows(array, axis):
    return lax.all_gather(array, axis, axis=0, tiled=True)


def scatter_rows(array, axis):
    return lax.psum_scatter(low(array), axis, scatter_dimension=0, tiled=True)


def per_device(
    tokens, cotangent, block_ids, span_order, attn_gain, w_qkv, w_out, ffn_gain, w_gate_up, w_down
):
    ctx_count = lax.axis_size("ctx")
    fsdp_count = lax.axis_size("fsdp")
    ctx = lax.axis_index("ctx")
    rows = tokens.shape[1]
    width = tokens.shape[2]
    shard = w_qkv.shape[0]
    length = rows * ctx_count
    heads = width // HD // ctx_count
    own_width = heads * HD
    inputs = tokens[0].astype(jnp.float32)
    strided = (shard // HD) % ctx_count == 0

    chunks = jnp.bitwise_xor(ctx, jnp.arange(ctx_count, dtype=jnp.int32))
    order_row = span_order[0]
    spans = order_row.shape[0]
    half = length // spans
    local = jnp.arange(rows, dtype=jnp.int32)
    slots = (chunks[:, None] * (rows // half) + (local // half)[None, :]).reshape(length)
    matches = slots[:, None] == jnp.arange(spans, dtype=jnp.int32)[None, :]
    picked = jnp.sum(jnp.where(matches, order_row[None, :], 0), axis=1)
    positions = picked * half + jnp.tile(local % half, ctx_count)
    cosine, sine = angles(positions, HD)
    blocks = jnp.concatenate(gathered(block_ids[0], "ctx"), 0)
    allowed = (blocks[None, :] <= blocks[:, None])[None]

    if strided:
        per = heads // fsdp_count
        qkv_own = lax.dynamic_index_in_dim(
            w_qkv.reshape(shard, 3, fsdp_count, ctx_count, per * HD), ctx, 3, keepdims=False
        ).reshape(shard, 3 * own_width)
        out_own = lax.dynamic_slice_in_dim(w_out, ctx * (per * HD), per * HD, 0)
        qkv_weight = gather_rows(qkv_own, "fsdp")
        out_weight = gather_rows(out_own, "fsdp")
    else:
        qkv_own = lax.dynamic_slice_in_dim(w_qkv, ctx * own_width, own_width, 2)
        qkv_weight = gather_rows(qkv_own.reshape(shard, 3 * own_width), "fsdp")
        out_weight = lax.dynamic_slice_in_dim(
            gather_rows(w_out, "fsdp"), ctx * own_width, own_width, 0
        )
    gains = lax.all_gather(
        jnp.stack([attn_gain, ffn_gain]), "fsdp", axis=1, tiled=True
    ).astype(jnp.float32)
    gain_one, gain_two = gains[0], gains[1]

    hidden_own = w_down.shape[0]
    block = hidden_own // ctx_count
    gate_up_own = lax.dynamic_index_in_dim(
        w_gate_up.reshape(shard, 2, fsdp_count, ctx_count, block), ctx, 3, keepdims=False
    )
    gate_up_mine = exchanged(jnp.transpose(gate_up_own, (2, 0, 1, 3)), "fsdp")
    gate_up_mine = gate_up_mine.reshape(width, 2, block)
    gate_up_weight = jnp.stack(gathered(gate_up_mine, "ctx"), 2).reshape(width, 2 * hidden_own)
    down_weight = jnp.concatenate(
        [
            lax.dynamic_slice_in_dim(w_down, (ctx ^ k) * block, block, 0)
            for k in range(ctx_count)
        ],
        0,
    )

    inverse_one = inverse_rms(inputs)
    normed_one = inputs * inverse_one
    act_one = low(normed_one * gain_one)
    act_seq = jnp.concatenate(gathered(act_one, "ctx"), 0)
    qkv = product(act_seq, qkv_weight, 1, 0).reshape(length, 3, heads, HD)
    query = low(rotate(qkv[:, 0], cosine, sine))
    keys = low(rotate(qkv[:, 1], cosine, sine))
    values = low(qkv[:, 2])
    scores = (
        jnp.einsum("qhe,khe->hqk", query, keys, preferred_element_type=jnp.float32) * score_scale
    )
    scores = jnp.where(allowed, scores, masked_score)
    top = jnp.max(scores, -1, keepdims=True)
    weights = jnp.where(allowed, jnp.exp(scores - top), 0.0)
    total = jnp.sum(weights, -1, keepdims=True)
    probs = weights / total
    probs_b = low(probs)
    attended = jnp.einsum("hqk,khe->qhe", probs_b, values, preferred_element_type=jnp.float32)
    attn_b = low(attended).reshape(length, own_width)
    branch = product(attn_b, out_weight, 1, 0).reshape(ctx_count, rows, width)
    resid = inputs + scattered([branch[k] for k in range(ctx_count)], "ctx")

    inverse_two = inverse_rms(resid)
    normed_two = resid * inverse_two
    act_two = gather_rows(low(normed_two * gain_two), "fsdp")
    cot = gather_rows(cotangent[0], "fsdp")
    gate_up = product(act_two, gate_up_weight, 1, 0)
    gate = gate_up[:, :hidden_own]
    upward = gate_up[:, hidden_own:]
    sigma = jax.nn.sigmoid(gate)
    swish = gate * sigma
    hidden = low(swish * upward)
    layer_out = resid + scatter_rows(product(hidden, down_weight, 1, 0), "fsdp").astype(jnp.float32)
    grad_hidden = product(cot, down_weight, 1, 1)
    grad_gate = grad_hidden * upward * sigma * (1.0 + gate * (1.0 - sigma))
    grad_up = grad_hidden * swish
    grad_gu = low(jnp.concatenate([grad_gate, grad_up], 1))
    grad_act_two = scatter_rows(product(grad_gu, gate_up_weight, 1, 1), "fsdp").astype(jnp.float32)
    grad_gain_two = jnp.sum(grad_act_two * normed_two, 0)
    grad_resid = cotangent[0].astype(jnp.float32) + norm_back(
        grad_act_two, normed_two, gain_two, inverse_two
    )

    grad_branch = jnp.concatenate(gathered(low(grad_resid), "ctx"), 0)
    grad_att = low(product(grad_branch, out_weight, 1, 1)).reshape(length, heads, HD)
    delta = jnp.sum(grad_att.astype(jnp.float32) * attended, -1)
    grad_values = jnp.einsum("hqk,qhe->khe", probs_b, grad_att, preferred_element_type=jnp.float32)
    grad_probs = jnp.einsum("qhe,khe->hqk", grad_att, values, preferred_element_type=jnp.float32)
    grad_scores = low(probs * (grad_probs - delta.T[..., None]))
    grad_query = (
        jnp.einsum("hqk,khe->qhe", grad_scores, keys, preferred_element_type=jnp.float32)
        * score_scale
    )
    grad_keys = (
        jnp.einsum("hqk,qhe->khe", grad_scores, query, preferred_element_type=jnp.float32)
        * score_scale
    )
    grad_qkv = low(
        jnp.stack(
            [rotate(grad_query, cosine, -sine), rotate(grad_keys, cosine, -sine), grad_values], 1
        )
    ).reshape(length, 3 * own_width)
    back = product(grad_qkv, qkv_weight, 1, 1).reshape(ctx_count, rows, width)
    grad_act_one = scattered([back[k] for k in range(ctx_count)], "ctx")
    grad_gain_one = jnp.sum(grad_act_one * normed_one, 0)
    input_grad = low(grad_resid + norm_back(grad_act_one, normed_one, gain_one, inverse_one))

    part_down = product(hidden, cot, 0, 0).reshape(ctx_count, block, width)
    part_down = low(scattered([part_down[k] for k in range(ctx_count)], "ctx"))
    grad_down = gather_rows(part_down, "ctx").astype(jnp.float32)
    part_gu = product(act_two, grad_gu, 0, 0).reshape(width, 2, ctx_count, block)
    part_gu = low(scattered([part_gu[:, :, k] for k in range(ctx_count)], "ctx"))
    part_gu = exchanged(part_gu.reshape(fsdp_count, shard, 2, block), "fsdp")
    part_gu = lax.all_gather(part_gu, "ctx", axis=0)
    grad_gate_up = jnp.transpose(part_gu, (2, 3, 1, 0, 4)).reshape(w_gate_up.shape)
    part_out = product(attn_b, grad_branch, 0, 0)
    if strided:
        part_out = scatter_rows(part_out, "fsdp")
        grad_out = gather_rows(part_out, "ctx").astype(jnp.float32)
    else:
        part_out = gather_rows(low(part_out), "ctx")
        grad_out = scatter_rows(part_out, "fsdp").astype(jnp.float32)
    part_qkv = scatter_rows(product(act_seq, grad_qkv, 0, 0), "fsdp")
    part_qkv = lax.all_gather(part_qkv, "ctx", axis=0)
    if strided:
        part_qkv = part_qkv.reshape(ctx_count, shard, 3, fsdp_count, own_width // fsdp_count)
        part_qkv = jnp.transpose(part_qkv, (1, 2, 3, 0, 4))
    else:
        part_qkv = jnp.transpose(part_qkv.reshape(ctx_count, shard, 3, own_width), (1, 2, 0, 3))
    grad_w_qkv = part_qkv.reshape(w_qkv.shape)
    grad_gains = lax.psum(jnp.stack([grad_gain_one, grad_gain_two]), "ctx")
    grad_gains = lax.psum_scatter(grad_gains, "fsdp", scatter_dimension=1, tiled=True)
    return (
        low(layer_out)[None],
        input_grad[None],
        grad_gains[0],
        grad_w_qkv.astype(jnp.float32),
        grad_out,
        grad_gains[1],
        grad_gate_up.astype(jnp.float32),
        grad_down,
    )


def solution(mesh):
    return jax.shard_map(
        per_device,
        mesh=mesh,
        in_specs=(
            P("fsdp", "ctx", None),
            P("fsdp", "ctx", None),
            P("fsdp", "ctx"),
            P("fsdp", None),
            P("fsdp"),
            P("fsdp", None, None),
            P("fsdp", None),
            P("fsdp"),
            P("fsdp", None, None),
            P("fsdp", None),
        ),
        out_specs=(
            P("fsdp", "ctx", None),
            P("fsdp", "ctx", None),
            P("fsdp"),
            P("fsdp", None, None),
            P("fsdp", None),
            P("fsdp"),
            P("fsdp", None, None),
            P("fsdp", None),
        ),
        check_vma=False,
    )
```

time: 3130 us -> 1090 us (0.35)
  waiting for transfers between devices: 2670 us -> 580 us
  local copies, waits for them, and re-layouts: 54.7 us -> 255 us
  matrix products: 250 us -> 110 us
  blocking collectives: 66.6 us -> 21.2 us
    reduce_scatter x4, waiting for transfers between devices: 1160 us -> 60.1 us  [scatter_rows(): return lax.psum_scatter(low(array), axis, scatter_dimension=0, tiled=True)]
    all_gather x6 -> x8, waiting for transfers between devices: 1130 us -> 113 us  [the longest x1 82.2 us: per_device(): part_gu = lax.all_gather(part_gu, 'ctx', axis=0)]
    ppermute x16 -> x38, waiting for transfers between devices: 138 us -> 405 us  [swapped(): return lax.ppermute(array, axis, [(i, i ^ by) for i in range(size)])]
    psum x1 -> x0, waiting for transfers between devices: 236 us -> none  [per_device(): lax.psum(part_gate_up.astype(jnp.bfloat16), 'ctx').astype(jnp.float32)]
    dot_general x34 -> x17, matrix products: 250 us -> 105 us  [the longest x12 92.9 us: product(): lax.dot_general(left, right, (((left_dim,), (right_dim,)), ((), ())), pre...]
    dynamic_update_slice x0 -> x15, local copies, waits for them, and re-layouts: none -> 94.6 us  [exchanged(): lax.dynamic_update_slice_in_dim(result, swapped(block, axis, k), other, 0)]
    unnamed x53 -> x116, local copies, waits for them, and re-layouts: 39.8 us -> 73.3 us
  transfers between devices with their start and end apart: 27 -> 51, of which waited for: 25 -> 26; matrix products, arithmetic and copies ran while one was open for 8% -> 31% of each run, Pallas kernels for 0% -> 0%
where the time goes in v1:
time: 1090 us; the launch traced here: 1080 us
  waiting for transfers between devices  580 us (53%)
  local copies, waits for them, and re-layouts  255 us (23%)
  matrix products  110 us (10%)
  other arithmetic  54.9 us (5%)
  starting transfers between devices  46.3 us (4%)
  blocking collectives  21.2 us (2%)
  between operations  15.2 us (1%)
    ppermute x38, waiting for transfers between devices, swapped(): return lax.ppermute(array, axis, [(i, i ^ by) for i in range(size)])  405 us
    dynamic_update_slice x15, local copies, waits for them, and re-layouts, exchanged(): lax.dynamic_update_slice_in_dim(result, swapped(block, axis, k), other, 0)  94.6 us
    dot_general x12, matrix products, product(): lax.dot_general(left, right, (((left_dim,), (right_dim,)), ((), ())), pre...  92.9 us
    all_gather x1, waiting for transfers between devices, per_device(): part_gu = lax.all_gather(part_gu, 'ctx', axis=0)  82.2 us
    unnamed x116, local copies, waits for them, and re-layouts  73.3 us
    reduce_scatter x4, waiting for transfers between devices, scatter_rows(): return lax.psum_scatter(low(array), axis, scatter_dimension=0, tiled=True)  60.1 us
    ppermute x38, starting transfers between devices, swapped(): return lax.ppermute(array, axis, [(i, i ^ by) for i in range(size)])  45.3 us
    all_gather x6, waiting for transfers between devices, gather_rows(): return lax.all_gather(array, axis, axis=0, tiled=True)  30.6 us
  transfers between devices with their start and end apart: 51, of which 26 were waited for; matrix products, arithmetic and copies ran while one was open for 31% of the time, Pallas kernels for 0%

profile of v1, /device:TPU:0, one launch (start us, length us, event | category | flops | bytes accessed | tf_op | source)
XLA Modules:
  0.0 1082.1 jit_solution(16234305393839408432)
XLA Ops:
  18.8 12.5 %all_gather.47 = bf16[2,2048]{1,0:T(2,128)(2,1)S(1)} all-gather(bf16[2,256]{1,0:T(2,128)(2,1)S(1)} %pad_maximum_fusion.29), channel_id=1, replica_groups=mesh['ctx'=4,'fsdp'=8] {'fsdp'}, dimensions={1}, use_global_device_ids=true | all-gather | bytes 9216 | tf_op jit(solution)/shard_map/all_gather | solution.py:126
  58.3 23.9 %all-gather.11.cloned.1.call-done = bf16[2048,1536]{0,1:T(8,128)(2,1)} async-done(((bf16[256,1536]{0,1:T(8,128)(2,1)}), bf16[2048,1536]{0,1:T(8,128)(2,1)}) %all-gather.11.cloned.1.call-update) | async-done | bytes 6291472 | tf_op jit(solution)/shard_map/all_gather | solution.py:77
  118.3 11.3 %collective-permute-done.6 = bf16[128,2048]{1,0:T(8,128)(2,1)S(1)} collective-permute-done((bf16[128,2048]{1,0:T(8,128)(2,1)S(1)}, bf16[128,2048]{1,0:T(8,128)(2,1)S(1)}, u32[]{:S(2)}, u32[]{:S(2)}) %collective-permute-start.6) | collective-permute-done | bytes 524320 | tf_op jit(solution)/shard_map/ppermute | solution.py:16
  129.5 11.6 %collective-permute-done.8 = bf16[128,2048]{1,0:T(8,128)(2,1)S(1)} collective-permute-done((bf16[128,2048]{1,0:T(8,128)(2,1)S(1)}, bf16[128,2048]{1,0:T(8,128)(2,1)S(1)}, u32[]{:S(2)}, u32[]{:S(2)}) %collective-permute-start.8) | collective-permute-done | bytes 524320 | tf_op jit(solution)/shard_map/ppermute | solution.py:16
  145.4 21.0 %copy.201 = bf16[256,2,8192]{0,2,1:T(8,128)(2,1)} copy(bf16[256,2,8192]{2,1,0:T(2,128)(2,1)} %param.18) | data formatting | bytes 16777216 | tf_op args[8]
  181.6 39.7 %collective-permute-done.10 = bf16[1,256,2,256]{3,0,2,1:T(2,128)(2,1)} collective-permute-done((bf16[1,256,2,256]{3,0,2,1:T(2,128)(2,1)S(1)}, bf16[1,256,2,256]{3,0,2,1:T(2,128)(2,1)}, u32[]{:S(2)}, u32[]{:S(2)}) %collective-permute-start.10) | collective-permute-done | bytes 262176 | tf_op jit(solution)/shard_map/ppermute | solution.py:16
  227.9 11.9 %dynamic_update_slice.49 = bf16[8,256,2,256]{3,0,2,1:T(8,128)(2,1)} dynamic-update-slice(bf16[8,256,2,256]{3,0,2,1:T(8,128)(2,1)} %bitcast.188, bf16[1,256,2,256]{3,0,2,1:T(2,128)(2,1)} %collective-permute-done.9, s32[]{:T(128)S(6)} %select_n.118, s32[]{:T(128)} %constant.277.clone.1, s32[]{:T(128)} %constant.277.clone.1, s32[]{:T(128)} %constant.277.clone.1) | dynamic-update-slice | bytes 524292 | tf_op jit(solution)/shard_map/dynamic_update_slice | solution.py:37
  239.9 11.9 %dynamic_update_slice.50 = bf16[8,256,2,256]{3,0,2,1:T(8,128)(2,1)} dynamic-update-slice(bf16[8,256,2,256]{3,0,2,1:T(8,128)(2,1)} %dynamic_update_slice.49, bf16[1,256,2,256]{3,0,2,1:T(2,128)(2,1)} %collective-permute-done.10, s32[]{:T(128)S(6)} %select_n.121, s32[]{:T(128)} %constant.277.clone.1, s32[]{:T(128)} %constant.277.clone.1, s32[]{:T(128)} %constant.277.clone.1) | dynamic-update-slice | bytes 524292 | tf_op jit(solution)/shard_map/dynamic_update_slice | solution.py:37
  251.8 11.9 %dynamic_update_slice.51 = bf16[8,256,2,256]{3,0,2,1:T(8,128)(2,1)} dynamic-update-slice(bf16[8,256,2,256]{3,0,2,1:T(8,128)(2,1)} %dynamic_update_slice.50, bf16[1,256,2,256]{3,0,2,1:T(2,128)(2,1)} %collective-permute-done.11, s32[]{:T(128)S(6)} %select_n.123, s32[]{:T(128)} %constant.277.clone.1, s32[]{:T(128)} %constant.277.clone.1, s32[]{:T(128)} %constant.277.clone.1) | dynamic-update-slice | bytes 524292 | tf_op jit(solution)/shard_map/dynamic_update_slice | solution.py:37
  263.7 11.9 %dynamic_update_slice.52 = bf16[8,256,2,256]{3,0,2,1:T(8,128)(2,1)} dynamic-update-slice(bf16[8,256,2,256]{3,0,2,1:T(8,128)(2,1)} %dynamic_update_slice.51, bf16[1,256,2,256]{3,0,2,1:T(2,128)(2,1)} %collective-permute-done.12, s32[]{:T(128)S(6)} %select_n.125, s32[]{:T(128)} %constant.277.clone.1, s32[]{:T(128)} %constant.277.clone.1, s32[]{:T(128)} %constant.277.clone.1) | dynamic-update-slice | bytes 524292 | tf_op jit(solution)/shard_map/dynamic_update_slice | solution.py:37
  275.6 11.9 %dynamic_update_slice.53 = bf16[8,256,2,256]{3,0,2,1:T(8,128)(2,1)} dynamic-update-slice(bf16[8,256,2,256]{3,0,2,1:T(8,128)(2,1)} %dynamic_update_slice.52, bf16[1,256,2,256]{3,0,2,1:T(2,128)(2,1)} %collective-permute-done.13, s32[]{:T(128)S(6)} %select_n.127, s32[]{:T(128)} %constant.277.clone.1, s32[]{:T(128)} %constant.277.clone.1, s32[]{:T(128)} %constant.277.clone.1) | dynamic-update-slice | bytes 524292 | tf_op jit(solution)/shard_map/dynamic_update_slice | solution.py:37
  287.5 11.9 %dynamic_update_slice.54 = bf16[8,256,2,256]{3,0,2,1:T(8,128)(2,1)} dynamic-update-slice(bf16[8,256,2,256]{3,0,2,1:T(8,128)(2,1)} %dynamic_update_slice.53, bf16[1,256,2,256]{3,0,2,1:T(2,128)(2,1)} %collective-permute-done.14, s32[]{:T(128)S(6)} %select_n.129, s32[]{:T(128)} %constant.277.clone.1, s32[]{:T(128)} %constant.277.clone.1, s32[]{:T(128)} %constant.277.clone.1) | dynamic-update-slice | bytes 524292 | tf_op jit(solution)/shard_map/dynamic_update_slice | solution.py:37
  299.5 11.9 %dynamic_update_slice.55 = bf16[8,256,2,256]{3,0,2,1:T(8,128)(2,1)} dynamic-update-slice(bf16[8,256,2,256]{3,0,2,1:T(8,128)(2,1)} %dynamic_update_slice.54, bf16[1,256,2,256]{3,0,2,1:T(2,128)(2,1)} %collective-permute-done.15, s32[]{:T(128)S(6)} %select_n.131, s32[]{:T(128)} %constant.277.clone.1, s32[]{:T(128)} %constant.277.clone.1, s32[]{:T(128)} %constant.277.clone.1) | dynamic-update-slice | bytes 524292 | tf_op jit(solution)/shard_map/dynamic_update_slice | solution.py:37
  321.6 41.6 %collective-permute-done.18 = bf16[2048,2,256]{2,0,1:T(8,128)(2,1)} collective-permute-done((bf16[2048,2,256]{2,0,1:T(8,128)(2,1)S(1)}, bf16[2048,2,256]{2,0,1:T(8,128)(2,1)}, u32[]{:S(2)}, u32[]{:S(2)}) %collective-permute-start.18) | collective-permute-done | bytes 2097184 | tf_op jit(solution)/shard_map/ppermute | solution.py:16
  363.3 44.3 %collective-permute-done.17 = bf16[2048,2,256]{2,0,1:T(8,128)(2,1)} collective-permute-done((bf16[2048,2,256]{2,0,1:T(8,128)(2,1)S(1)}, bf16[2048,2,256]{2,0,1:T(8,128)(2,1)}, u32[]{:S(2)}, u32[]{:S(2)}) %collective-permute-start.17) | collective-permute-done | bytes 2097184 | tf_op jit(solution)/shard_map/ppermute | solution.py:16
  414.4 11.5 %copy.220 = bf16[2048,2,4,256]{0,3,2,1:T(8,128)(2,1)} copy(bf16[2048,2,4,256]{3,0,1,2:T(8,128)(2,1)} %pad_maximum_fusion) | data formatting | bytes 16777216 | tf_op jit(solution)/shard_map/stack | solution.py:138
  425.9 14.7 %fusion.87 = f32[1024,2048]{1,0:T(8,128)} fusion(bf16[1024,2048]{1,0:T(8,128)(2,1)} %all-gather.15.cloned.1.call-done, bf16[2048,2048]{0,1:T(8,128)(2,1)} %bitcast.186), kind=kOutput, calls=%fused_computation.184 | convolution fusion | flops 8589934592 | bytes 20971520 | tf_op jit(solution)/shard_map/dot_general | solution.py:67
  440.6 12.2 %fusion.8 = (bf16[1024,1024]{1,0:T(8,128)(2,1)S(1)}, bf16[1024,1024]{1,0:T(8,128)(2,1)S(1)}, bf16[1024,1024]{1,0:T(8,128)(2,1)}) fusion(f32[1024,2048]{1,0:T(8,128)} %fusion.87, bf16[1,1024,2048]{2,1,0:T(8,128)(2,1)} %all-gather.23.cloned.1.call-done, bf16[256,2048]{1,0:T(8,128)(2,1)} %get-tuple-element.73, bf16[256,2048]{1,0:T(8,128)(2,1)} %get-tuple-element.74, ...), kind=kOutput, calls=%fused_computation.18 | convolution fusion | flops 4327473152 | bytes 23068672 | tf_op jit(solution)/shard_map/dot_general | solution.py:67
  465.4 60.0 %reduce-scatter.10.cloned.1.call-done = bf16[128,2048]{1,0:T(8,128)(2,1)} async-done(((bf16[1024,2048]{1,0:T(8,128)(2,1)}), bf16[128,2048]{1,0:T(8,128)(2,1)}) %reduce-scatter.10.cloned.1.call-update) | async-done | bytes 524304 | tf_op jit(solution)/shard_map/reduce_scatter | solution.py:81
  532.4 12.3 %collective-permute-done.21 = bf16[128,2048]{1,0:T(8,128)(2,1)S(1)} collective-permute-done((bf16[128,2048]{1,0:T(8,128)(2,1)S(1)}, bf16[128,2048]{1,0:T(8,128)(2,1)S(1)}, u32[]{:S(2)}, u32[]{:S(2)}) %collective-permute-start.21) | collective-permute-done | bytes 524320 | tf_op jit(solution)/shard_map/ppermute | solution.py:16
  590.9 22.5 %collective-permute-done.35 = bf16[256,2048]{1,0:T(8,128)(2,1)S(1)} collective-permute-done((bf16[256,2048]{1,0:T(8,128)(2,1)S(1)}, bf16[256,2048]{1,0:T(8,128)(2,1)S(1)}, u32[]{:S(2)}, u32[]{:S(2)}) %collective-permute-start.35) | collective-permute-done | bytes 1048608 | tf_op jit(solution)/shard_map/ppermute | solution.py:16
  613.4 22.6 %collective-permute-done.37 = bf16[256,2048]{1,0:T(8,128)(2,1)S(1)} collective-permute-done((bf16[256,2048]{1,0:T(8,128)(2,1)S(1)}, bf16[256,2048]{1,0:T(8,128)(2,1)S(1)}, u32[]{:S(2)}, u32[]{:S(2)}) %collective-permute-start.37) | collective-permute-done | bytes 1048608 | tf_op jit(solution)/shard_map/ppermute | solution.py:16
  649.4 15.1 %fusion.19 = f32[2048,2048]{0,1:T(8,128)} fusion(bf16[1024,2048]{1,0:T(8,128)(2,1)} %all-gather.15.cloned.1.call-done, bf16[1024,1024]{1,0:T(8,128)(2,1)} %copy-done.52, bf16[1024,1024]{1,0:T(8,128)(2,1)S(1)} %copy-done.51), kind=kOutput, calls=%fused_computation.35 | convolution fusion | flops 8598323200 | bytes 25165824 | tf_op jit(solution)/shard_map/dot_general | solution.py:67
  664.5 16.9 %copy.228 = f32[2048,2,4,256]{3,0,1,2:T(8,128)} copy(f32[2048,2,4,256]{0,3,2,1:T(8,128)} %bitcast.181) | data formatting | bytes 33554432 | tf_op jit(solution)/shard_map/reshape | solution.py:217
  698.7 62.1 %collective-permute-done.25 = bf16[2048,2,256]{2,0,1:T(8,128)(2,1)S(1)} collective-permute-done((bf16[2048,2,256]{2,0,1:T(8,128)(2,1)}, bf16[2048,2,256]{2,0,1:T(8,128)(2,1)S(1)}, u32[]{:S(2)}, u32[]{:S(2)}) %collective-permute-start.25) | collective-permute-done | bytes 2097184 | tf_op jit(solution)/shard_map/ppermute | solution.py:16
  761.3 44.4 %collective-permute-done.27 = bf16[2048,2,256]{2,0,1:T(8,128)(2,1)S(1)} collective-permute-done((bf16[2048,2,256]{2,0,1:T(8,128)(2,1)S(1)}, bf16[2048,2,256]{2,0,1:T(8,128)(2,1)S(1)}, u32[]{:S(2)}, u32[]{:S(2)}) %collective-permute-start.27) | collective-permute-done | bytes 2097184 | tf_op jit(solution)/shard_map/ppermute | solution.py:16
  843.1 24.8 %collective-permute-done.30 = bf16[1,256,2,256]{3,1,0,2:T(8,128)(2,1)S(1)} collective-permute-done((bf16[1,256,2,256]{3,1,0,2:T(8,128)(2,1)}, bf16[1,256,2,256]{3,1,0,2:T(8,128)(2,1)S(1)}, u32[]{:S(2)}, u32[]{:S(2)}) %collective-permute-start.30) | collective-permute-done | bytes 262176 | tf_op jit(solution)/shard_map/ppermute | solution.py:16
  868.6 20.5 %collective-permute-done.31 = bf16[1,256,2,256]{3,1,0,2:T(8,128)(2,1)S(1)} collective-permute-done((bf16[1,256,2,256]{3,1,0,2:T(8,128)(2,1)}, bf16[1,256,2,256]{3,1,0,2:T(8,128)(2,1)S(1)}, u32[]{:S(2)}, u32[]{:S(2)}) %collective-permute-start.31) | collective-permute-done | bytes 262176 | tf_op jit(solution)/shard_map/ppermute | solution.py:16
  917.4 82.2 %all-gather.19.cloned.1.call-done = bf16[4,8,256,2,256]{4,2,3,1,0:T(8,128)(2,1)} async-done(((bf16[1,8,256,2,256]{4,2,3,1,0:T(8,128)(2,1)}), bf16[4,8,256,2,256]{4,2,3,1,0:T(8,128)(2,1)}) %all-gather.19.cloned.1.call-update) | async-done | bytes 8388624 | tf_op jit(solution)/shard_map/all_gather | solution.py:220
  999.6 11.8 %copy.231 = bf16[4,8,256,2,256]{2,4,0,1,3:T(8,128)(2,1)} copy(bf16[4,8,256,2,256]{4,2,3,1,0:T(8,128)(2,1)} %all-gather.19.cloned.1.call-done) | data formatting | bytes 16777216 | tf_op jit(solution)/shard_map/all_gather | solution.py:220
  1011.4 11.5 %convert_element_type.226 = f32[4,8,256,2,256]{2,4,0,1,3:T(8,128)} convert(bf16[4,8,256,2,256]{2,4,0,1,3:T(8,128)(2,1)} %copy.231) | non-fusion elementwise | flops 4194304 | bytes 25165824 | tf_op jit(solution)/shard_map/convert_element_type | solution.py:246
  1022.9 25.4 %copy.233 = f32[256,2,8192]{2,1,0:T(2,128)} copy(f32[256,2,8192]{0,2,1:T(8,128)} %bitcast.174) | data formatting | bytes 33554432
  (301 shorter events, 307.1 us)
Async XLA Ops:
  7.2 75.0 %all-gather.11.cloned.1.call-start = ((), (), s32[]{:S(2)}) async-start(), calls=%async_computation.5 | async-start | bytes 7077888 | tf_op jit(solution)/shard_map/all_gather | solution.py:77
  14.1 97.5 %all-gather.13.cloned.1.call-start = ((), (), s32[]{:S(2)}) async-start(), calls=%async_computation.6 | async-start | bytes 2359296 | tf_op jit(solution)/shard_map/all_gather | solution.py:77
  35.6 390.3 %all-gather.15.cloned.1.call-start = ((), (), s32[]{:S(2)}) async-start(), calls=%async_computation.7 | async-start | bytes 4718592 | tf_op jit(solution)/shard_map/all_gather | solution.py:77
  144.5 296.1 %all-gather.23.cloned.1.call-start = ((), (), s32[]{:S(2)}) async-start(), calls=%async_computation.15 | async-start | bytes 4718592 | tf_op jit(solution)/shard_map/all_gather | solution.py:77
  145.1 380.4 %reduce-scatter.10.cloned.1.call-start = ((), (), s32[]{:S(2)}) async-start(), calls=%async_computation.9 | async-start | bytes 4718592 | tf_op jit(solution)/shard_map/reduce_scatter | solution.py:81
  169.6 51.7 %collective-permute-start.10 = (bf16[1,256,2,256]{3,0,2,1:T(2,128)(2,1)S(1)}, bf16[1,256,2,256]{3,0,2,1:T(2,128)(2,1)}, u32[]{:S(2)}, u32[]{:S(2)}) collective-permute-start(bf16[1,256,2,256]{3,0,2,1:T(2,128)(2,1)S(1)} %copy.206), channel_id=1, source_target_pairs={{0,2},{1,3},{2,0},{3,1},{4,6},{5,7},{6,4},{7,5},{8,10},{9,11},{10,... | collective-permute-start | bytes 786440 | tf_op jit(solution)/shard_map/ppermute | solution.py:16
  172.3 79.5 %collective-permute-start.11 = (bf16[1,256,2,256]{3,0,2,1:T(2,128)(2,1)}, bf16[1,256,2,256]{3,0,2,1:T(2,128)(2,1)}, u32[]{:S(2)}, u32[]{:S(2)}) collective-permute-start(bf16[1,256,2,256]{3,0,2,1:T(2,128)(2,1)} %copy.208), channel_id=1, source_target_pairs={{0,3},{1,2},{2,1},{3,0},{4,7},{5,6},{6,5},{7,4},{8,11},{9,10},{10,... | collective-permute-start | bytes 786440 | tf_op jit(solution)/shard_map/ppermute | solution.py:16
  173.7 90.0 %collective-permute-start.12 = (bf16[1,256,2,256]{3,0,2,1:T(2,128)(2,1)}, bf16[1,256,2,256]{3,0,2,1:T(2,128)(2,1)}, u32[]{:S(2)}, u32[]{:S(2)}) collective-permute-start(bf16[1,256,2,256]{3,0,2,1:T(2,128)(2,1)} %copy.210), channel_id=1, source_target_pairs={{0,4},{1,5},{2,6},{3,7},{4,0},{5,1},{6,2},{7,3},{8,12},{9,13},{10,... | collective-permute-start | bytes 786440 | tf_op jit(solution)/shard_map/ppermute | solution.py:16
  176.8 98.8 %collective-permute-start.13 = (bf16[1,256,2,256]{3,0,2,1:T(2,128)(2,1)}, bf16[1,256,2,256]{3,0,2,1:T(2,128)(2,1)}, u32[]{:S(2)}, u32[]{:S(2)}) collective-permute-start(bf16[1,256,2,256]{3,0,2,1:T(2,128)(2,1)} %copy.212), channel_id=1, source_target_pairs={{0,5},{1,4},{2,7},{3,6},{4,1},{5,0},{6,3},{7,2},{8,13},{9,12},{10,... | collective-permute-start | bytes 786440 | tf_op jit(solution)/shard_map/ppermute | solution.py:16
  179.6 107.9 %collective-permute-start.14 = (bf16[1,256,2,256]{3,0,2,1:T(2,128)(2,1)}, bf16[1,256,2,256]{3,0,2,1:T(2,128)(2,1)}, u32[]{:S(2)}, u32[]{:S(2)}) collective-permute-start(bf16[1,256,2,256]{3,0,2,1:T(2,128)(2,1)} %copy.214), channel_id=1, source_target_pairs={{0,6},{1,7},{2,4},{3,5},{4,2},{5,3},{6,0},{7,1},{8,14},{9,15},{10,... | collective-permute-start | bytes 786440 | tf_op jit(solution)/shard_map/ppermute | solution.py:16
  221.3 78.2 %collective-permute-start.15 = (bf16[1,256,2,256]{3,0,2,1:T(2,128)(2,1)}, bf16[1,256,2,256]{3,0,2,1:T(2,128)(2,1)}, u32[]{:S(2)}, u32[]{:S(2)}) collective-permute-start(bf16[1,256,2,256]{3,0,2,1:T(2,128)(2,1)} %copy.216), channel_id=1, source_target_pairs={{0,7},{1,6},{2,5},{3,4},{4,3},{5,2},{6,1},{7,0},{8,15},{9,14},{10,... | collective-permute-start | bytes 786440 | tf_op jit(solution)/shard_map/ppermute | solution.py:16
  313.7 49.6 %collective-permute-start.18 = (bf16[2048,2,256]{2,0,1:T(8,128)(2,1)S(1)}, bf16[2048,2,256]{2,0,1:T(8,128)(2,1)}, u32[]{:S(2)}, u32[]{:S(2)}) collective-permute-start(bf16[2048,2,256]{2,0,1:T(8,128)(2,1)S(1)} %bitcast.189), channel_id=1, source_target_pairs={{0,24},{8,16},{16,8},{24,0},{1,25},{9,17},{17,9},{25,1},{2,26},{10... | collective-permute-start | bytes 6291464 | tf_op jit(solution)/shard_map/ppermute | solution.py:16
  315.9 91.7 %collective-permute-start.17 = (bf16[2048,2,256]{2,0,1:T(8,128)(2,1)S(1)}, bf16[2048,2,256]{2,0,1:T(8,128)(2,1)}, u32[]{:S(2)}, u32[]{:S(2)}) collective-permute-start(bf16[2048,2,256]{2,0,1:T(8,128)(2,1)S(1)} %bitcast.190), channel_id=1, source_target_pairs={{0,16},{8,24},{16,0},{24,8},{1,17},{9,25},{17,1},{25,9},{2,18},{10... | collective-permute-start | bytes 6291464 | tf_op jit(solution)/shard_map/ppermute | solution.py:16
  316.7 91.1 %collective-permute-start.16 = (bf16[2048,2,256]{2,0,1:T(8,128)(2,1)S(1)}, bf16[2048,2,256]{2,0,1:T(8,128)(2,1)}, u32[]{:S(2)}, u32[]{:S(2)}) collective-permute-start(bf16[2048,2,256]{2,0,1:T(8,128)(2,1)S(1)} %bitcast.191), channel_id=1, source_target_pairs={{0,8},{8,0},{16,24},{24,16},{1,9},{9,1},{17,25},{25,17},{2,10},{10... | collective-permute-start | bytes 6291464 | tf_op jit(solution)/shard_map/ppermute | solution.py:16
  465.4 370.1 %reduce-scatter.14.cloned.1.call-start = ((), (), s32[]{:S(2)}) async-start(), calls=%async_computation.11 | async-start | bytes 2359296 | tf_op jit(solution)/shard_map/reduce_scatter | solution.py:81
  557.9 336.0 %reduce-scatter.12.cloned.1.call-start = ((), (), s32[]{:S(2)}) async-start(), calls=%async_computation.10 | async-start | bytes 7077888 | tf_op jit(solution)/shard_map/reduce_scatter | solution.py:81
  579.0 315.7 %all-gather.21.cloned.1.call-start = ((), (), s32[]{:S(2)}) async-start(), calls=%async_computation.14 | async-start | bytes 5242880 | tf_op jit(solution)/shard_map/all_gather | solution.py:77
  639.1 262.4 %reduce-scatter.8.cloned.1.call-start = ((), (), s32[]{:S(2)}) async-start(), calls=%async_computation.8 | async-start | bytes 4718592 | tf_op jit(solution)/shard_map/reduce_scatter | solution.py:81
  647.8 256.5 %reduce-scatter.16.cloned.1.call-start = ((), (), s32[]{:S(2)}) async-start(), calls=%async_computation.17 | async-start | bytes 1179648
  689.6 71.2 %collective-permute-start.25 = (bf16[2048,2,256]{2,0,1:T(8,128)(2,1)}, bf16[2048,2,256]{2,0,1:T(8,128)(2,1)S(1)}, u32[]{:S(2)}, u32[]{:S(2)}) collective-permute-start(bf16[2048,2,256]{2,0,1:T(8,128)(2,1)} %get-tuple-element.57), channel_id=1, source_target_pairs={{0,8},{8,0},{16,24},{24,16},{1,9},{9,1},{17,25},{25,17},{2,10},{10... | collective-permute-start | bytes 6291464 | tf_op jit(solution)/shard_map/ppermute | solution.py:16
  689.8 115.9 %collective-permute-start.27 = (bf16[2048,2,256]{2,0,1:T(8,128)(2,1)S(1)}, bf16[2048,2,256]{2,0,1:T(8,128)(2,1)S(1)}, u32[]{:S(2)}, u32[]{:S(2)}) collective-permute-start(bf16[2048,2,256]{2,0,1:T(8,128)(2,1)S(1)} %get-tuple-element.58), channel_id=1, source_target_pairs={{0,24},{8,16},{16,8},{24,0},{1,25},{9,17},{17,9},{25,1},{2,26},{10... | collective-permute-start | bytes 6291464 | tf_op jit(solution)/shard_map/ppermute | solution.py:16
  691.5 115.4 %collective-permute-start.26 = (bf16[2048,2,256]{2,0,1:T(8,128)(2,1)S(1)}, bf16[2048,2,256]{2,0,1:T(8,128)(2,1)}, u32[]{:S(2)}, u32[]{:S(2)}) collective-permute-start(bf16[2048,2,256]{2,0,1:T(8,128)(2,1)S(1)} %get-tuple-element.59), channel_id=1, source_target_pairs={{0,16},{8,24},{16,0},{24,8},{1,17},{9,25},{17,1},{25,9},{2,18},{10... | collective-permute-start | bytes 6291464 | tf_op jit(solution)/shard_map/ppermute | solution.py:16
  696.8 120.3 %collective-permute-start.22 = (bf16[128,2048]{1,0:T(8,128)(2,1)S(1)}, bf16[128,2048]{1,0:T(8,128)(2,1)S(1)}, u32[]{:S(2)}, u32[]{:S(2)}) collective-permute-start(bf16[128,2048]{1,0:T(8,128)(2,1)S(1)} %get-tuple-element.84), channel_id=1, source_target_pairs={{0,8},{8,0},{16,24},{24,16},{1,9},{9,1},{17,25},{25,17},{2,10},{10... | collective-permute-start | bytes 1572872 | tf_op jit(solution)/shard_map/ppermute | solution.py:16
  697.0 128.2 %collective-permute-start.24 = (bf16[128,2048]{1,0:T(8,128)(2,1)S(1)}, bf16[128,2048]{1,0:T(8,128)(2,1)S(1)}, u32[]{:S(2)}, u32[]{:S(2)}) collective-permute-start(bf16[128,2048]{1,0:T(8,128)(2,1)S(1)} %get-tuple-element.85), channel_id=1, source_target_pairs={{0,24},{8,16},{16,8},{24,0},{1,25},{9,17},{17,9},{25,1},{2,26},{10... | collective-permute-start | bytes 1572872 | tf_op jit(solution)/shard_map/ppermute | solution.py:16
  760.9 65.5 %collective-permute-start.23 = (bf16[128,2048]{1,0:T(8,128)(2,1)S(1)}, bf16[128,2048]{1,0:T(8,128)(2,1)S(1)}, u32[]{:S(2)}, u32[]{:S(2)}) collective-permute-start(bf16[128,2048]{1,0:T(8,128)(2,1)S(1)} %get-tuple-element.86), channel_id=1, source_target_pairs={{0,16},{8,24},{16,0},{24,8},{1,17},{9,25},{17,1},{25,9},{2,18},{10... | collective-permute-start | bytes 1572872 | tf_op jit(solution)/shard_map/ppermute | solution.py:16
  829.2 85.4 %all-gather.17.cloned.1.call-start = ((), (), s32[]{:S(2)}) async-start(), calls=%async_computation.12 | async-start | bytes 1310720 | tf_op jit(solution)/shard_map/all_gather | solution.py:77
  831.6 61.4 %collective-permute-start.34 = (bf16[1,256,2,256]{3,1,0,2:T(8,128)(2,1)}, bf16[1,256,2,256]{3,1,0,2:T(8,128)(2,1)S(1)}, u32[]{:S(2)}, u32[]{:S(2)}) collective-permute-start(bf16[1,256,2,256]{3,1,0,2:T(8,128)(2,1)} %get-tuple-element.77), channel_id=1, source_target_pairs={{0,7},{1,6},{2,5},{3,4},{4,3},{5,2},{6,1},{7,0},{8,15},{9,14},{10,... | collective-permute-start | bytes 786440 | tf_op jit(solution)/shard_map/ppermute | solution.py:16
  831.6 59.8 %collective-permute-start.33 = (bf16[1,256,2,256]{3,1,0,2:T(8,128)(2,1)}, bf16[1,256,2,256]{3,1,0,2:T(8,128)(2,1)}, u32[]{:S(2)}, u32[]{:S(2)}) collective-permute-start(bf16[1,256,2,256]{3,1,0,2:T(8,128)(2,1)} %get-tuple-element.78), channel_id=1, source_target_pairs={{0,6},{1,7},{2,4},{3,5},{4,2},{5,3},{6,0},{7,1},{8,14},{9,15},{10,... | collective-permute-start | bytes 786440 | tf_op jit(solution)/shard_map/ppermute | solution.py:16
  833.6 56.1 %collective-permute-start.32 = (bf16[1,256,2,256]{3,1,0,2:T(8,128)(2,1)}, bf16[1,256,2,256]{3,1,0,2:T(8,128)(2,1)}, u32[]{:S(2)}, u32[]{:S(2)}) collective-permute-start(bf16[1,256,2,256]{3,1,0,2:T(8,128)(2,1)} %get-tuple-element.79), channel_id=1, source_target_pairs={{0,5},{1,4},{2,7},{3,6},{4,1},{5,0},{6,3},{7,2},{8,13},{9,12},{10,... | collective-permute-start | bytes 786440 | tf_op jit(solution)/shard_map/ppermute | solution.py:16
  835.5 164.1 %all-gather.19.cloned.1.call-start = ((), (), s32[]{:S(2)}) async-start(), calls=%async_computation.13 | async-start | bytes 10485760 | tf_op jit(solution)/shard_map/all_gather | solution.py:220
  839.3 49.7 %collective-permute-start.31 = (bf16[1,256,2,256]{3,1,0,2:T(8,128)(2,1)}, bf16[1,256,2,256]{3,1,0,2:T(8,128)(2,1)S(1)}, u32[]{:S(2)}, u32[]{:S(2)}) collective-permute-start(bf16[1,256,2,256]{3,1,0,2:T(8,128)(2,1)} %get-tuple-element.80), channel_id=1, source_target_pairs={{0,4},{1,5},{2,6},{3,7},{4,0},{5,1},{6,2},{7,3},{8,12},{9,13},{10,... | collective-permute-start | bytes 786440 | tf_op jit(solution)/shard_map/ppermute | solution.py:16
  893.8 154.5 %all-gather.25.cloned.1.call-start = ((), (), s32[]{:S(2)}) async-start(), calls=%async_computation.16 | async-start | bytes 3932160 | tf_op jit(solution)/shard_map/all_gather | solution.py:230
  (74 other events, 1316.3 us)
Sparse Core Ops, SparseCore 0:
  14.3 67.8 all-gather.10
  84.4 27.2 all-gather.12
  144.6 73.5 all-gather.14
  219.7 89.2 all-gather.22
  465.5 59.9 reduce-scatter.9
  558.0 35.6 reduce-scatter.13
  596.5 68.5 reduce-scatter.11
  667.0 73.6 all-gather.20
  743.0 50.0 reduce-scatter.7
  829.3 44.3 reduce-scatter.15
  875.6 33.9 all-gather.16
  911.8 87.7 all-gather.18
  1001.5 43.9 all-gather.24

commit v2 on v1

--- a/solution.py
+++ b/solution.py
@@ -1,6 +1,10 @@
+import functools
+
 import jax
 import jax.numpy as jnp
 from jax import lax
+from jax.experimental import pallas as pl
+from jax.experimental.pallas import tpu as pltpu
 from jax.sharding import PartitionSpec as P
 
 HD = 64
@@ -27,15 +31,120 @@
     return total
 
 
-def exchanged(blocks, axis):
-    size = lax.axis_size(axis)
-    own = lax.axis_index(axis)
-    result = blocks
-    for k in range(1, size):
-        other = own ^ k
-        block = lax.dynamic_index_in_dim(blocks, other, 0, keepdims=True)
-        result = lax.dynamic_update_slice_in_dim(result, swapped(block, axis, k), other, 0)
+def paired(blocks):
+    core = lax.axis_index("fsdp") % 2
+    grid = blocks.reshape((blocks.shape[0] // 2, 2) + blocks.shape[1:])
+    keep = lax.dynamic_index_in_dim(grid, core, 1, keepdims=False)
+    got = swapped(lax.dynamic_index_in_dim(grid, 1 - core, 1, keepdims=False), "fsdp", 1)
+    return jnp.stack([jnp.where(core == 0, keep, got), jnp.where(core == 0, got, keep)], 1)
+
+
+def crossing(pairs):
+    chip = lax.axis_index("fsdp") // 2
+    return [
+        lax.dynamic_index_in_dim(pairs, chip ^ k, 0, keepdims=False)
+        for k in range(1, pairs.shape[0])
+    ]
+
+
+def crossed(sends):
+    return [swapped(send, "fsdp", 2 * k) for k, send in enumerate(sends, 1)]
+
+
+def in_order(pairs, received):
+    chip = lax.axis_index("fsdp") // 2
+    for k, pair in enumerate(received, 1):
+        pairs = lax.dynamic_update_index_in_dim(pairs, pair, chip ^ k, 0)
+    return pairs.reshape((-1,) + pairs.shape[2:])
+
+
+def first_hop(array):
+    size = lax.axis_size("ctx")
+    return [array] + [swapped(array, "ctx", k) for k in range(1, 3 if size == 4 else size)]
+
+
+def second_hop(pieces):
+    if lax.axis_size("ctx") != 4:
+        return []
+    half = pieces[0].shape[0] // 2
+    return [swapped(pieces[1][:half], "ctx", 2), swapped(pieces[2][half:], "ctx", 1)]
+
+
+def first_fold(parts):
+    size = lax.axis_size("ctx")
+    if size != 4:
+        return [swapped(parts[k], "ctx", k) for k in range(1, size)]
+    half = parts[0].shape[0] // 2
+    return [swapped(parts[3][:half], "ctx", 1), swapped(parts[3][half:], "ctx", 2)]
+
+
+def folded(parts, halves):
+    if lax.axis_size("ctx") != 4:
+        return []
+    half = parts[0].shape[0] // 2
+    over_x = jnp.concatenate([parts[1][:half], plus(parts[1][half:], halves[1])], 0)
+    over_y = jnp.concatenate([plus(parts[2][:half], halves[0]), parts[2][half:]], 0)
+    return [over_x, over_y]
+
+
+def second_fold(sends, halves):
+    if not sends:
+        return halves
+    return [swapped(sends[0], "ctx", 1), swapped(sends[1], "ctx", 2)]
+
+
+def butterfly(array, axis):
+    step = 1
+    while step < lax.axis_size(axis):
+        array = array + swapped(array, axis, step)
+        step *= 2
+    return array
+
+
+def plus(*terms):
+    return low(sum(term.astype(jnp.float32) for term in terms))
+
+
+def placed(pieces, shape, block, body, result=None):
+    own = lax.axis_index("ctx").astype(jnp.int32)[None]
+    for piece, k, index in pieces:
+
+        def out_map(step, own_ref, k=k, index=index):
+            return index(own_ref[0] ^ k, step)
+
+        in_specs = [pl.BlockSpec((1,) + piece.shape[1:], lambda step, own_ref: (step, 0, 0))]
+        operands = [own, piece]
+        aliases = {}
+        if result is not None:
+            in_specs.append(pl.BlockSpec(memory_space=pl.ANY))
+            operands.append(result)
+            aliases = {2: 0}
+        result = pl.pallas_call(
+            body,
+            grid_spec=pltpu.PrefetchScalarGridSpec(
+                num_scalar_prefetch=1,
+                grid=(piece.shape[0],),
+                in_specs=in_specs,
+                out_specs=pl.BlockSpec(block, out_map),
+            ),
+            out_shape=jax.ShapeDtypeStruct(shape, jnp.float32),
+            input_output_aliases=aliases,
+            cost_estimate=pl.CostEstimate(
+                flops=piece.size, bytes_accessed=6 * piece.size, transcendentals=0
+            ),
+        )(*operands)
     return result
+
+
+def write_pair(own_ref, piece_ref, *refs):
+    out_ref = refs[-1]
+    half = piece_ref.shape[2] // 2
+    out_ref[:, 0, :] = piece_ref[0, :, :half].astype(jnp.float32)
+    out_ref[:, 1, :] = piece_ref[0, :, half:].astype(jnp.float32)
+
+
+def write_rows(own_ref, piece_ref, *refs):
+    refs[-1][...] = piece_ref[0].astype(jnp.float32)
 
 
 def angles(positions, width):
@@ -73,12 +182,33 @@
     return values.astype(jnp.bfloat16)
 
 
+def together(*arrays):
+    return lax.optimization_barrier(arrays)
+
+
 def gather_rows(array, axis):
     return lax.all_gather(array, axis, axis=0, tiled=True)
 
 
 def scatter_rows(array, axis):
     return lax.psum_scatter(low(array), axis, scatter_dimension=0, tiled=True)
+
+
+def write_heads(groups, piece_ref, out_ref):
+    count = piece_ref.shape[0]
+    each = piece_ref.shape[2] // groups
+    for group in range(groups):
+        row = [
+            piece_ref[index, :, group * each : (group + 1) * each].astype(jnp.float32)
+            for index in range(count)
+        ]
+        out_ref[0, :, group * count * each : (group + 1) * count * each] = jnp.concatenate(row, 1)
+
+
+def own_columns(own_ref, in_ref, out_ref):
+    half = in_ref.shape[2]
+    out_ref[0, :, :half] = in_ref[:, 0, :]
+    out_ref[0, :, half:] = in_ref[:, 1, :]
 
 
 def per_device(
@@ -129,20 +259,51 @@
     gain_one, gain_two = gains[0], gains[1]
 
     hidden_own = w_down.shape[0]
-    block = hidden_own // ctx_count
-    gate_up_own = lax.dynamic_index_in_dim(
-        w_gate_up.reshape(shard, 2, fsdp_count, ctx_count, block), ctx, 3, keepdims=False
-    )
-    gate_up_mine = exchanged(jnp.transpose(gate_up_own, (2, 0, 1, 3)), "fsdp")
-    gate_up_mine = gate_up_mine.reshape(width, 2, block)
-    gate_up_weight = jnp.stack(gathered(gate_up_mine, "ctx"), 2).reshape(width, 2 * hidden_own)
-    down_weight = jnp.concatenate(
-        [
-            lax.dynamic_slice_in_dim(w_down, (ctx ^ k) * block, block, 0)
-            for k in range(ctx_count)
-        ],
-        0,
-    )
+    part = shard // ctx_count
+    gate_up_own = pl.pallas_call(
+        own_columns,
+        grid_spec=pltpu.PrefetchScalarGridSpec(
+            num_scalar_prefetch=1,
+            grid=(fsdp_count,),
+            in_specs=[pl.BlockSpec((part, 2, hidden_own), lambda step, own: (own[0], 0, step))],
+            out_specs=pl.BlockSpec((1, part, 2 * hidden_own), lambda step, own: (step, 0, 0)),
+        ),
+        out_shape=jax.ShapeDtypeStruct((fsdp_count, part, 2 * hidden_own), jnp.bfloat16),
+        cost_estimate=pl.CostEstimate(
+            flops=0, bytes_accessed=8 * width * part * fsdp_count, transcendentals=0
+        ),
+    )(ctx.astype(jnp.int32)[None], w_gate_up)
+    inputs, gate_up_own = together(inputs, gate_up_own)
+    gate_up_own = paired(gate_up_own)
+    gate_up_mine = in_order(gate_up_own, crossed(crossing(gate_up_own)))
+    gate_up_mine = gate_up_mine.reshape(fsdp_count * part, 2 * hidden_own)
+    gate_up_mine, qkv_weight = together(gate_up_mine, qkv_weight)
+    gate_up_pieces = first_hop(gate_up_mine)
+
+    def to_parts(array):
+        lead = array.shape[:-1]
+        array = array.reshape(lead + (fsdp_count, ctx_count, part))
+        array = jnp.swapaxes(array, -3, -2).reshape(lead + (ctx_count, fsdp_count * part))
+        return jnp.concatenate(
+            [
+                lax.dynamic_index_in_dim(array, ctx ^ k, array.ndim - 2, keepdims=False)
+                for k in range(ctx_count)
+            ],
+            -1,
+        )
+
+    def from_parts(array):
+        lead = array.shape[:-1]
+        array = array.reshape(lead + (ctx_count, fsdp_count * part))
+        array = jnp.stack(
+            [
+                lax.dynamic_index_in_dim(array, ctx ^ k, array.ndim - 2, keepdims=False)
+                for k in range(ctx_count)
+            ],
+            -2,
+        )
+        array = array.reshape(lead + (ctx_count, fsdp_count, part))
+        return jnp.swapaxes(array, -3, -2).reshape(lead + (width,))
 
     inverse_one = inverse_rms(inputs)
     normed_one = inputs * inverse_one
@@ -168,27 +329,66 @@
 
     inverse_two = inverse_rms(resid)
     normed_two = resid * inverse_two
-    act_two = gather_rows(low(normed_two * gain_two), "fsdp")
     cot = gather_rows(cotangent[0], "fsdp")
+    act_two, cot, gate_up_pieces = together(
+        to_parts(low(normed_two * gain_two)), cot, gate_up_pieces
+    )
+    act_two = gather_rows(act_two, "fsdp")
+    gate_up_weight = jnp.concatenate(gate_up_pieces + second_hop(gate_up_pieces), 0)
     gate_up = product(act_two, gate_up_weight, 1, 0)
     gate = gate_up[:, :hidden_own]
     upward = gate_up[:, hidden_own:]
     sigma = jax.nn.sigmoid(gate)
     swish = gate * sigma
     hidden = low(swish * upward)
-    layer_out = resid + scatter_rows(product(hidden, down_weight, 1, 0), "fsdp").astype(jnp.float32)
-    grad_hidden = product(cot, down_weight, 1, 1)
+    block = hidden_own // ctx_count
+    grad_hidden = product(cot, w_down, 1, 1)
     grad_gate = grad_hidden * upward * sigma * (1.0 + gate * (1.0 - sigma))
     grad_up = grad_hidden * swish
     grad_gu = low(jnp.concatenate([grad_gate, grad_up], 1))
-    grad_act_two = scatter_rows(product(grad_gu, gate_up_weight, 1, 1), "fsdp").astype(jnp.float32)
+    span = fsdp_count * part
+
+    def gu_term(k):
+        return low(product(act_two[:, k * span : (k + 1) * span], grad_gu, 0, 0))
+
+    grad_act_two = low(product(grad_gu, gate_up_weight, 1, 1))
+    gu_final = gu_term(ctx_count - 1)
+    grad_act_two, grad_gu, gu_final = together(grad_act_two, grad_gu, gu_final)
+    grad_act_two = scatter_rows(grad_act_two, "fsdp")
+    part_gu = [gu_term(k) for k in range(ctx_count - 1)] + [gu_final]
+    gu_halves = first_fold(part_gu)
+    out_part = low(product(hidden, w_down, 1, 0))
+    part_down = low(product(hidden, cot, 0, 0)).reshape(ctx_count, block, width)
+    part_down = [
+        lax.dynamic_index_in_dim(part_down, ctx ^ k, 0, keepdims=False) for k in range(ctx_count)
+    ]
+    part_gu, gu_halves, out_part, part_down = together(part_gu, gu_halves, out_part, part_down)
+    gu_sends = folded(part_gu, gu_halves)
+    down_halves = first_fold(part_down)
+    down_sends = folded(part_down, down_halves)
+    grad_act_two, gu_sends, out_part, down_sends = together(
+        grad_act_two, gu_sends, out_part, down_sends
+    )
+    gu_last = second_fold(gu_sends, gu_halves)
+    layer_part = scatter_rows(out_part, "fsdp")
+    grad_act_two = from_parts(grad_act_two).astype(jnp.float32)
     grad_gain_two = jnp.sum(grad_act_two * normed_two, 0)
     grad_resid = cotangent[0].astype(jnp.float32) + norm_back(
         grad_act_two, normed_two, gain_two, inverse_two
     )
 
     grad_branch = jnp.concatenate(gathered(low(grad_resid), "ctx"), 0)
+    grad_branch, gu_last = together(grad_branch, gu_last)
+    gu_pairs = paired(plus(part_gu[0], *gu_last).reshape(fsdp_count, part, 2 * hidden_own))
     grad_att = low(product(grad_branch, out_weight, 1, 1)).reshape(length, heads, HD)
+    gu_sends = crossing(gu_pairs)
+    part_out = low(product(attn_b, grad_branch, 0, 0))
+    grad_att, gu_pairs, gu_sends, down_sends, part_out = together(
+        grad_att, gu_pairs, gu_sends, down_sends, part_out
+    )
+    part_out = scatter_rows(part_out, "fsdp") if strided else part_out
+    gu_received = crossed(gu_sends)
+    down_last = second_fold(down_sends, down_halves)
     delta = jnp.sum(grad_att.astype(jnp.float32) * attended, -1)
     grad_values = jnp.einsum("hqk,qhe->khe", probs_b, grad_att, preferred_element_type=jnp.float32)
     grad_probs = jnp.einsum("qhe,khe->hqk", grad_att, values, preferred_element_type=jnp.float32)
@@ -206,44 +406,114 @@
             [rotate(grad_query, cosine, -sine), rotate(grad_keys, cosine, -sine), grad_values], 1
         )
     ).reshape(length, 3 * own_width)
-    back = product(grad_qkv, qkv_weight, 1, 1).reshape(ctx_count, rows, width)
-    grad_act_one = scattered([back[k] for k in range(ctx_count)], "ctx")
+    grad_qkv, down_last, layer_part, gu_received[::2] = together(
+        grad_qkv, down_last, layer_part, gu_received[::2]
+    )
+    down_pieces = first_hop(plus(part_down[0], *down_last))
+    part_qkv = low(product(act_seq, grad_qkv, 0, 0))
+    back = low(product(grad_qkv, qkv_weight, 1, 1)).reshape(ctx_count, rows, width)
+    back = [back[k] for k in range(ctx_count)]
+    part_qkv, part_out, back, gu_received, down_pieces = together(
+        part_qkv, part_out, back, gu_received, down_pieces
+    )
+    part_qkv = scatter_rows(part_qkv, "fsdp")
+
+    grad_act_one = scattered(back, "ctx")
+    gu_sum = in_order(gu_pairs, gu_received)
+    gu_pieces = first_hop(gu_sum)
+    grad_act_one, down_pieces = together(grad_act_one, down_pieces)
+    down_last = second_hop(down_pieces)
+    layer_out = low(resid + layer_part.astype(jnp.float32))
     grad_gain_one = jnp.sum(grad_act_one * normed_one, 0)
+    grad_gains = jnp.stack([grad_gain_one, grad_gain_two])
+    grad_gains = butterfly(grad_gains, "fsdp")
     input_grad = low(grad_resid + norm_back(grad_act_one, normed_one, gain_one, inverse_one))
-
-    part_down = product(hidden, cot, 0, 0).reshape(ctx_count, block, width)
-    part_down = low(scattered([part_down[k] for k in range(ctx_count)], "ctx"))
-    grad_down = gather_rows(part_down, "ctx").astype(jnp.float32)
-    part_gu = product(act_two, grad_gu, 0, 0).reshape(width, 2, ctx_count, block)
-    part_gu = low(scattered([part_gu[:, :, k] for k in range(ctx_count)], "ctx"))
-    part_gu = exchanged(part_gu.reshape(fsdp_count, shard, 2, block), "fsdp")
-    part_gu = lax.all_gather(part_gu, "ctx", axis=0)
-    grad_gate_up = jnp.transpose(part_gu, (2, 3, 1, 0, 4)).reshape(w_gate_up.shape)
-    part_out = product(attn_b, grad_branch, 0, 0)
-    if strided:
-        part_out = scatter_rows(part_out, "fsdp")
-        grad_out = gather_rows(part_out, "ctx").astype(jnp.float32)
-    else:
-        part_out = gather_rows(low(part_out), "ctx")
-        grad_out = scatter_rows(part_out, "fsdp").astype(jnp.float32)
-    part_qkv = scatter_rows(product(act_seq, grad_qkv, 0, 0), "fsdp")
+    rows_each = block // 2
+
+    def down_rows(offset):
+        return lambda other, step: (other * 2 + offset + step, 0)
+
+    grad_down = placed(
+        [
+            (piece.reshape(2, rows_each, width), k, down_rows(0))
+            for k, piece in enumerate(down_pieces)
+        ],
+        w_down.shape,
+        (rows_each, width),
+        write_rows,
+    )
+    gu_pieces, down_last, layer_out, input_grad, grad_down, part_out, grad_gains, part_qkv = (
+        together(
+            gu_pieces, down_last, layer_out, input_grad, grad_down, part_out, grad_gains, part_qkv
+        )
+    )
+    gu_last = second_hop(gu_pieces)
     part_qkv = lax.all_gather(part_qkv, "ctx", axis=0)
     if strided:
-        part_qkv = part_qkv.reshape(ctx_count, shard, 3, fsdp_count, own_width // fsdp_count)
-        part_qkv = jnp.transpose(part_qkv, (1, 2, 3, 0, 4))
+        out_pieces = gathered(part_out, "ctx")
+    else:
+        out_pieces = [scatter_rows(gather_rows(part_out, "ctx"), "fsdp")]
+
+    def gate_up_columns(offset):
+        return lambda other, step: (other, 0, offset + step)
+
+    grad_gate_up = placed(
+        [(piece, k, gate_up_columns(0)) for k, piece in enumerate(gu_pieces)],
+        w_gate_up.shape,
+        (part, 2, hidden_own),
+        write_pair,
+    )
+    grad_gate_up, gu_last, out_pieces, grad_gains = together(
+        grad_gate_up, gu_last, out_pieces, grad_gains
+    )
+    grad_gains = butterfly(grad_gains, "ctx")
+    grad_gains = lax.dynamic_slice_in_dim(grad_gains, lax.axis_index("fsdp") * shard, shard, 1)
+    grad_gate_up = placed(
+        [(piece, 3, gate_up_columns(k * fsdp_count // 2)) for k, piece in enumerate(gu_last)],
+        w_gate_up.shape,
+        (part, 2, hidden_own),
+        write_pair,
+        grad_gate_up,
+    )
+    grad_down = placed(
+        [(piece[None], 3, down_rows(k)) for k, piece in enumerate(down_last)],
+        w_down.shape,
+        (rows_each, width),
+        write_rows,
+        grad_down,
+    )
+    if strided:
+        grad_out = placed(
+            [(piece[None], k, lambda other, step: (other, 0)) for k, piece in enumerate(out_pieces)],
+            w_out.shape,
+            out_pieces[0].shape,
+            write_rows,
+        )
+    else:
+        grad_out = out_pieces[0].astype(jnp.float32)
+    if strided:
+        grad_w_qkv = pl.pallas_call(
+            functools.partial(write_heads, fsdp_count),
+            grid=(3,),
+            in_specs=[pl.BlockSpec((ctx_count, shard, own_width), lambda step: (0, 0, step))],
+            out_specs=pl.BlockSpec((1, shard, width), lambda step: (step, 0, 0)),
+            out_shape=jax.ShapeDtypeStruct((3, shard, width), jnp.float32),
+            cost_estimate=pl.CostEstimate(
+                flops=part_qkv.size, bytes_accessed=6 * part_qkv.size, transcendentals=0
+            ),
+        )(part_qkv)
+        grad_w_qkv = jnp.transpose(grad_w_qkv, (1, 0, 2))
     else:
         part_qkv = jnp.transpose(part_qkv.reshape(ctx_count, shard, 3, own_width), (1, 2, 0, 3))
-    grad_w_qkv = part_qkv.reshape(w_qkv.shape)
-    grad_gains = lax.psum(jnp.stack([grad_gain_one, grad_gain_two]), "ctx")
-    grad_gains = lax.psum_scatter(grad_gains, "fsdp", scatter_dimension=1, tiled=True)
+        grad_w_qkv = part_qkv.reshape(w_qkv.shape).astype(jnp.float32)
     return (
-        low(layer_out)[None],
+        layer_out[None],
         input_grad[None],
         grad_gains[0],
-        grad_w_qkv.astype(jnp.float32),
+        grad_w_qkv,
         grad_out,
         grad_gains[1],
-        grad_gate_up.astype(jnp.float32),
+        grad_gate_up,
         grad_down,
     )
 

time: 1090 us -> 705 us (0.65)
  waiting for transfers between devices: 580 us -> 326 us
  local copies, waits for them, and re-layouts: 255 us -> 64.8 us
  Pallas kernels: 0 us -> 58.2 us
  starting transfers between devices: 46.3 us -> 63.9 us
  other arithmetic: 54.9 us -> 43.9 us
    ppermute x38 -> x51, waiting for transfers between devices: 405 us -> 297 us  [swapped(): return lax.ppermute(array, axis, [(i, i ^ by) for i in range(size)])]
    dynamic_update_slice x15 -> x7, local copies, waits for them, and re-layouts: 94.6 us -> 11.5 us  [in_order(): pairs = lax.dynamic_update_index_in_dim(pairs, pair, chip ^ k, 0)]
    all_gather x1 -> x0, waiting for transfers between devices: 82.2 us -> none  [per_device(): part_gu = lax.all_gather(part_gu, 'ctx', axis=0)]
    reduce_scatter x4, waiting for transfers between devices: 60.1 us -> 0.13 us  [scatter_rows(): return lax.psum_scatter(low(array), axis, scatter_dimension=0, tiled=True)]
    pallas_call x0 -> x16, Pallas kernels: none -> 58.2 us  [the longest x14 44.7 us: placed(): pl.pallas_call(body, grid_spec=pltpu.PrefetchScalarGridSpec(num_scalar_pr...]
    unnamed x116 -> x123, local copies, waits for them, and re-layouts: 73.3 us -> 25.3 us
    convert_element_type x3 -> x2, other arithmetic: 21.1 us -> 0.2 us  [the longest x1 0.11 us: per_device(): grad_act_two = from_parts(grad_act_two).astype(jnp.float32)]
    convert_element_type x4 -> x3, local copies, waits for them, and re-layouts: 21.8 us -> 2.98 us  [the longest x2 2.71 us: per_device(): grad_act_two = from_parts(grad_act_two).astype(jnp.float32)]
  transfers between devices with their start and end apart: 51 -> 60, of which waited for: 26 -> 27; matrix products, arithmetic and copies ran while one was open for 31% -> 23% of each run, Pallas kernels for 0% -> 8%
where the time goes in v2:
time: 705 us; the launch traced here: 700 us
  waiting for transfers between devices  326 us (46%)
  matrix products  116 us (16%)
  local copies, waits for them, and re-layouts  64.8 us (9%)
  starting transfers between devices  63.9 us (9%)
  Pallas kernels  58.2 us (8%)
  other arithmetic  43.9 us (6%)
  between operations  15.1 us (2%)
  blocking collectives  12.4 us (2%)
    ppermute x51, waiting for transfers between devices, swapped(): return lax.ppermute(array, axis, [(i, i ^ by) for i in range(size)])  297 us
    dot_general x15, matrix products, product(): lax.dot_general(left, right, (((left_dim,), (right_dim,)), ((), ())), pre...  97.3 us
    ppermute x51, starting transfers between devices, swapped(): return lax.ppermute(array, axis, [(i, i ^ by) for i in range(size)])  62.3 us
    pallas_call x14, Pallas kernels, placed(): pl.pallas_call(body, grid_spec=pltpu.PrefetchScalarGridSpec(num_scalar_pr...  44.7 us
    all_gather x4, waiting for transfers between devices, gather_rows(): return lax.all_gather(array, axis, axis=0, tiled=True)  27.9 us
    unnamed x123, local copies, waits for them, and re-layouts  25.3 us
    convert_element_type x11, other arithmetic, low(): return values.astype(jnp.bfloat16)  19.1 us
  transfers between devices with their start and end apart: 60, of which 27 were waited for; matrix products, arithmetic and copies ran while one was open for 23% of the time, Pallas kernels for 8%

profile of v2, /device:TPU:0, one launch (start us, length us, event | category | flops | bytes accessed | tf_op | source)
XLA Modules:
  0.0 700.4 jit_solution(16967882558246445374)
XLA Ops:
  19.6 8.0 %shard_map.161 = bf16[8,64,2048]{2,1,0:T(8,128)(2,1)} custom-call(s32[1]{0:T(128)} %bitcast.2.own_ref, bf16[256,2,8192]{2,1,0:T(2,128)(2,1)} %in_ref.1), custom_call_target="tpu_custom_call" | custom-call | bytes 8388608 | tf_op jit(solution)/shard_map/pallas_call | solution.py:263
  27.7 12.4 %all_gather.21 = bf16[2,2048]{1,0:T(2,128)(2,1)S(1)} all-gather(bf16[2,256]{1,0:T(2,128)(2,1)S(1)} %pad_maximum_fusion.29), channel_id=1, replica_groups=mesh['ctx'=4,'fsdp'=8] {'fsdp'}, dimensions={1}, use_global_device_ids=true | all-gather | bytes 9216 | tf_op jit(solution)/shard_map/all_gather | solution.py:256
  50.8 7.9 %collective-permute-start.5 = (bf16[2,64,2048]{2,1,0:T(8,128)(2,1)S(1)}, bf16[2,64,2048]{2,1,0:T(8,128)(2,1)S(1)}, u32[]{:S(2)}, u32[]{:S(2)}) collective-permute-start(bf16[2,64,2048]{2,1,0:T(8,128)(2,1)S(1)} %get-tuple-element.201), channel_id=1, source_target_pairs={{0,4},{1,5},{2,6},{3,7},{4,0},{5,1},{6,2},{7,3},{8,12},{9,13},{10,... | collective-permute-start | bytes 1572872 | tf_op jit(solution)/shard_map/ppermute | solution.py:20
  60.2 39.7 %collective-permute-done.4 = bf16[2,64,2048]{2,1,0:T(8,128)(2,1)S(1)} collective-permute-done((bf16[2,64,2048]{2,1,0:T(8,128)(2,1)S(1)}, bf16[2,64,2048]{2,1,0:T(8,128)(2,1)S(1)}, u32[]{:S(2)}, u32[]{:S(2)}) %collective-permute-start.4) | collective-permute-done | bytes 524320 | tf_op jit(solution)/shard_map/ppermute | solution.py:20
  104.5 11.1 %collective-permute-done.6 = bf16[2,64,2048]{2,1,0:T(8,128)(2,1)S(1)} collective-permute-done((bf16[2,64,2048]{2,1,0:T(8,128)(2,1)S(1)}, bf16[2,64,2048]{2,1,0:T(8,128)(2,1)S(1)}, u32[]{:S(2)}, u32[]{:S(2)}) %collective-permute-start.6) | collective-permute-done | bytes 524320 | tf_op jit(solution)/shard_map/ppermute | solution.py:20
  119.1 6.2 fusion.36
  126.9 5.7 fusion.62
  155.2 23.2 %collective-permute-done.10 = bf16[128,2048]{1,0:T(8,128)(2,1)S(1)} collective-permute-done((bf16[128,2048]{1,0:T(8,128)(2,1)}, bf16[128,2048]{1,0:T(8,128)(2,1)S(1)}, u32[]{:S(2)}, u32[]{:S(2)}) %collective-permute-start.10) | collective-permute-done | bytes 524320 | tf_op jit(solution)/shard_map/ppermute | solution.py:20
  178.5 11.7 %collective-permute-done.12 = bf16[128,2048]{1,0:T(8,128)(2,1)S(1)} collective-permute-done((bf16[128,2048]{1,0:T(8,128)(2,1)}, bf16[128,2048]{1,0:T(8,128)(2,1)S(1)}, u32[]{:S(2)}, u32[]{:S(2)}) %collective-permute-start.12) | collective-permute-done | bytes 524320 | tf_op jit(solution)/shard_map/ppermute | solution.py:20
  209.4 11.4 %collective-permute-done.15 = bf16[256,2048]{1,0:T(8,128)(2,1)S(1)} collective-permute-done((bf16[256,2048]{1,0:T(8,128)(2,1)S(1)}, bf16[256,2048]{1,0:T(8,128)(2,1)S(1)}, u32[]{:S(2)}, u32[]{:S(2)}) %collective-permute-start.15) | collective-permute-done | bytes 1048608 | tf_op jit(solution)/shard_map/ppermute | solution.py:20
  224.4 22.5 %all-gather.12.cloned.1.call-done = bf16[1024,2048]{1,0:T(8,128)(2,1)} async-done(((bf16[128,2048]{1,0:T(8,128)(2,1)}), bf16[1024,2048]{1,0:T(8,128)(2,1)}) %all-gather.12.cloned.1.call-update) | async-done | bytes 4194320 | tf_op jit(solution)/shard_map/all_gather | solution.py:190
  246.9 15.4 %fusion.65 = f32[1024,2048]{0,1:T(8,128)} fusion(bf16[1024,2048]{1,0:T(8,128)(2,1)} %all-gather.12.cloned.1.call-done, bf16[2048,2048]{1,0:T(8,128)(2,1)} %constant_dynamic-update-slice_fusion), kind=kOutput, calls=%fused_computation.197 | convolution fusion | flops 8589934592 | bytes 20971520 | tf_op jit(solution)/shard_map/dot_general | solution.py:176
  262.3 9.4 %multiply_convert_fusion.3 = (bf16[1024,1024]{0,1:T(8,128)(2,1)S(1)}, bf16[1024,1024]{0,1:T(8,128)(2,1)S(1)}, bf16[1024,1024]{0,1:T(8,128)(2,1)}) fusion(f32[1024,2048]{0,1:T(8,128)} %fusion.65, bf16[1024,2048]{1,0:T(8,128)(2,1)S(1)} %bitcast.232, bf16[1024,2048]{1,0:T(8,128)(2,1)S(1)} %copy-done.49), kind=kOutput, calls=%fused_computation.10 | convolution fusion | flops 4310695936 | bytes 23068672 | tf_op jit(solution)/shard_map/dot_general | solution.py:176
  272.9 12.9 %convolution_convert_fusion.1 = bf16[1024,2048]{1,0:T(8,128)(2,1)} fusion(bf16[2048,2048]{1,0:T(8,128)(2,1)} %constant_dynamic-update-slice_fusion, bf16[1024,1024]{0,1:T(8,128)(2,1)S(1)} %get-tuple-element.175, bf16[1024,1024]{0,1:T(8,128)(2,1)S(1)} %get-tuple-element.174), kind=kOutput, calls=%fused_computation.17 | convolution fusion | flops 8600420352 | bytes 16777216 | tf_op jit(solution)/shard_map/dot_general | solution.py:176
  298.8 5.1 convolution_convert_fusion.4
  319.4 6.2 convolution_convert_fusion.3
  335.1 5.5 collective-permute-done.20
  354.8 50.8 %collective-permute-done.23 = bf16[128,2048]{1,0:T(8,128)(2,1)S(1)} collective-permute-done((bf16[128,2048]{1,0:T(8,128)(2,1)S(1)}, bf16[128,2048]{1,0:T(8,128)(2,1)S(1)}, u32[]{:S(2)}, u32[]{:S(2)}) %collective-permute-start.23) | collective-permute-done | bytes 524320 | tf_op jit(solution)/shard_map/ppermute | solution.py:20
  405.6 8.7 %collective-permute-done.22 = bf16[128,2048]{1,0:T(8,128)(2,1)S(1)} collective-permute-done((bf16[128,2048]{1,0:T(8,128)(2,1)S(1)}, bf16[128,2048]{1,0:T(8,128)(2,1)S(1)}, u32[]{:S(2)}, u32[]{:S(2)}) %collective-permute-start.22) | collective-permute-done | bytes 524320 | tf_op jit(solution)/shard_map/ppermute | solution.py:20
  450.8 18.8 %collective-permute-done.29 = bf16[2,64,2048]{2,1,0:T(8,128)(2,1)} collective-permute-done((bf16[2,64,2048]{2,1,0:T(8,128)(2,1)S(1)}, bf16[2,64,2048]{2,1,0:T(8,128)(2,1)}, u32[]{:S(2)}, u32[]{:S(2)}) %collective-permute-start.29) | collective-permute-done | bytes 524320 | tf_op jit(solution)/shard_map/ppermute | solution.py:20
  469.6 19.3 %collective-permute-done.30 = bf16[2,64,2048]{2,1,0:T(8,128)(2,1)} collective-permute-done((bf16[2,64,2048]{2,1,0:T(8,128)(2,1)S(1)}, bf16[2,64,2048]{2,1,0:T(8,128)(2,1)}, u32[]{:S(2)}, u32[]{:S(2)}) %collective-permute-start.30) | collective-permute-done | bytes 524320 | tf_op jit(solution)/shard_map/ppermute | solution.py:20
  494.8 7.4 %convolution_convert_fusion.8 = bf16[512,2048]{1,0:T(8,128)(2,1)} fusion(bf16[512,1536]{0,1:T(8,128)(2,1)S(1)} %bitcast.201, bf16[2048,1536]{0,1:T(8,128)(2,1)} %all-gather.8.cloned.1.call-done), kind=kOutput, calls=%fused_computation.25 | convolution fusion | flops 3222274048 | bytes 9961472 | tf_op jit(solution)/shard_map/dot_general | solution.py:176
  502.2 6.9 convolution_convert_fusion
  511.9 5.2 collective-permute-done.33
  533.8 11.3 %collective-permute-done.37 = bf16[128,2048]{1,0:T(8,128)(2,1)S(1)} collective-permute-done((bf16[128,2048]{1,0:T(8,128)(2,1)}, bf16[128,2048]{1,0:T(8,128)(2,1)S(1)}, u32[]{:S(2)}, u32[]{:S(2)}) %collective-permute-start.37) | collective-permute-done | bytes 524320 | tf_op jit(solution)/shard_map/ppermute | solution.py:20
  564.2 34.5 %collective-permute-done.40 = bf16[128,2048]{1,0:T(8,128)(2,1)S(1)} collective-permute-done((bf16[128,2048]{1,0:T(8,128)(2,1)}, bf16[128,2048]{1,0:T(8,128)(2,1)S(1)}, u32[]{:S(2)}, u32[]{:S(2)}) %collective-permute-start.40) | collective-permute-done | bytes 524320 | tf_op jit(solution)/shard_map/ppermute | solution.py:20
  608.2 6.2 shard_map.165.refs_0_
  614.5 6.2 shard_map.166.refs_0_
  620.7 6.2 shard_map.167.refs_0_
  627.0 28.9 %collective-permute-done.48 = bf16[64,2048]{1,0:T(8,128)(2,1)} collective-permute-done((bf16[64,2048]{1,0:T(8,128)(2,1)S(1)}, bf16[64,2048]{1,0:T(8,128)(2,1)}, u32[]{:S(2)}, u32[]{:S(2)}) %collective-permute-start.48) | collective-permute-done | bytes 262176 | tf_op jit(solution)/shard_map/ppermute | solution.py:20
  657.4 6.6 collective-permute-done.46
  688.2 5.4 shard_map.168
  (362 shorter events, 248.4 us)
Async XLA Ops:
  7.2 111.3 %all-gather.8.cloned.1.call-start = ((), (), s32[]{:S(2)}) async-start(), calls=%async_computation.4 | async-start | bytes 7077888 | tf_op jit(solution)/shard_map/all_gather | solution.py:190
  14.1 131.7 %all-gather.10.cloned.1.call-start = ((), (), s32[]{:S(2)}) async-start(), calls=%async_computation.5 | async-start | bytes 2359296 | tf_op jit(solution)/shard_map/all_gather | solution.py:190
  14.9 179.7 %all-gather.14.cloned.1.call-start = ((), (), s32[]{:S(2)}) async-start(), calls=%async_computation.11 | async-start | bytes 4718592 | tf_op jit(solution)/shard_map/all_gather | solution.py:190
  41.3 77.8 %collective-permute-start.2 = (bf16[128,2048]{1,0:T(8,128)(2,1)}, bf16[128,2048]{1,0:T(8,128)(2,1)}, u32[]{:S(2)}, u32[]{:S(2)}) collective-permute-start(bf16[128,2048]{1,0:T(8,128)(2,1)} %multiply_convert_fusion.5), channel_id=1, source_target_pairs={{0,24},{8,16},{16,8},{24,0},{1,25},{9,17},{17,9},{25,1},{2,26},{10... | collective-permute-start | bytes 1572872 | tf_op jit(solution)/shard_map/ppermute | solution.py:20
  45.2 201.7 %all-gather.12.cloned.1.call-start = ((), (), s32[]{:S(2)}) async-start(), calls=%async_computation.6 | async-start | bytes 4718592 | tf_op jit(solution)/shard_map/all_gather | solution.py:190
  47.8 71.2 %collective-permute-start.1 = (bf16[128,2048]{1,0:T(8,128)(2,1)}, bf16[128,2048]{1,0:T(8,128)(2,1)}, u32[]{:S(2)}, u32[]{:S(2)}) collective-permute-start(bf16[128,2048]{1,0:T(8,128)(2,1)} %multiply_convert_fusion.5), channel_id=1, source_target_pairs={{0,16},{8,24},{16,0},{24,8},{1,17},{9,25},{17,1},{25,9},{2,18},{10... | collective-permute-start | bytes 1572872 | tf_op jit(solution)/shard_map/ppermute | solution.py:20
  49.9 69.2 %collective-permute-start = (bf16[128,2048]{1,0:T(8,128)(2,1)}, bf16[128,2048]{1,0:T(8,128)(2,1)}, u32[]{:S(2)}, u32[]{:S(2)}) collective-permute-start(bf16[128,2048]{1,0:T(8,128)(2,1)} %multiply_convert_fusion.5), channel_id=1, source_target_pairs={{0,8},{8,0},{16,24},{24,16},{1,9},{9,1},{17,25},{25,17},{2,10},{10... | collective-permute-start | bytes 1572872 | tf_op jit(solution)/shard_map/ppermute | solution.py:20
  50.5 49.5 %collective-permute-start.4 = (bf16[2,64,2048]{2,1,0:T(8,128)(2,1)S(1)}, bf16[2,64,2048]{2,1,0:T(8,128)(2,1)S(1)}, u32[]{:S(2)}, u32[]{:S(2)}) collective-permute-start(bf16[2,64,2048]{2,1,0:T(8,128)(2,1)S(1)} %get-tuple-element.200), channel_id=1, source_target_pairs={{0,2},{1,3},{2,0},{3,1},{4,6},{5,7},{6,4},{7,5},{8,10},{9,11},{10,... | collective-permute-start | bytes 1572872 | tf_op jit(solution)/shard_map/ppermute | solution.py:20
  50.8 52.9 %collective-permute-start.5 = (bf16[2,64,2048]{2,1,0:T(8,128)(2,1)S(1)}, bf16[2,64,2048]{2,1,0:T(8,128)(2,1)S(1)}, u32[]{:S(2)}, u32[]{:S(2)}) collective-permute-start(bf16[2,64,2048]{2,1,0:T(8,128)(2,1)S(1)} %get-tuple-element.201), channel_id=1, source_target_pairs={{0,4},{1,5},{2,6},{3,7},{4,0},{5,1},{6,2},{7,3},{8,12},{9,13},{10,... | collective-permute-start | bytes 1572872 | tf_op jit(solution)/shard_map/ppermute | solution.py:20
  118.5 76.1 %collective-permute-start.14 = (bf16[512,2048]{1,0:T(8,128)(2,1)}, bf16[512,2048]{1,0:T(8,128)(2,1)}, u32[]{:S(2)}, u32[]{:S(2)}) collective-permute-start(bf16[512,2048]{1,0:T(8,128)(2,1)} %bitcast.16), channel_id=1, source_target_pairs={{0,16},{8,24},{16,0},{24,8},{1,17},{9,25},{17,1},{25,9},{2,18},{10... | collective-permute-start | bytes 6291464 | tf_op jit(solution)/shard_map/ppermute | solution.py:20
  118.5 76.1 %collective-permute-start.13 = (bf16[512,2048]{1,0:T(8,128)(2,1)}, bf16[512,2048]{1,0:T(8,128)(2,1)}, u32[]{:S(2)}, u32[]{:S(2)}) collective-permute-start(bf16[512,2048]{1,0:T(8,128)(2,1)} %bitcast.16), channel_id=1, source_target_pairs={{0,8},{8,0},{16,24},{24,16},{1,9},{9,1},{17,25},{25,17},{2,10},{10... | collective-permute-start | bytes 6291464 | tf_op jit(solution)/shard_map/ppermute | solution.py:20
  194.6 148.6 %reduce-scatter.5.cloned.1.call-start = ((), (), s32[]{:S(2)}) async-start(), calls=%async_computation.7 | async-start | bytes 4718592 | tf_op jit(solution)/shard_map/reduce_scatter | solution.py:194
  294.4 194.6 %reduce-scatter.7.cloned.1.call-start = ((), (), s32[]{:S(2)}) async-start(), calls=%async_computation.8 | async-start | bytes 4718592 | tf_op jit(solution)/shard_map/reduce_scatter | solution.py:194
  343.3 168.6 %reduce-scatter.9.cloned.1.call-start = ((), (), s32[]{:S(2)}) async-start(), calls=%async_computation.9 | async-start | bytes 2359296 | tf_op jit(solution)/shard_map/reduce_scatter | solution.py:194
  344.6 70.0 %collective-permute-start.24 = (bf16[512,2048]{1,0:T(8,128)(2,1)}, bf16[512,2048]{1,0:T(8,128)(2,1)}, u32[]{:S(2)}, u32[]{:S(2)}) collective-permute-start(bf16[512,2048]{1,0:T(8,128)(2,1)} %pad_maximum_fusion.4), channel_id=1, source_target_pairs={{0,8},{8,0},{16,24},{24,16},{1,9},{9,1},{17,25},{25,17},{2,10},{10... | collective-permute-start | bytes 6291464 | tf_op jit(solution)/shard_map/ppermute | solution.py:20
  346.1 68.5 %collective-permute-start.25 = (bf16[512,2048]{1,0:T(8,128)(2,1)}, bf16[512,2048]{1,0:T(8,128)(2,1)}, u32[]{:S(2)}, u32[]{:S(2)}) collective-permute-start(bf16[512,2048]{1,0:T(8,128)(2,1)} %pad_maximum_fusion.5), channel_id=1, source_target_pairs={{0,16},{8,24},{16,0},{24,8},{1,17},{9,25},{17,1},{25,9},{2,18},{10... | collective-permute-start | bytes 6291464 | tf_op jit(solution)/shard_map/ppermute | solution.py:20
  351.2 54.4 %collective-permute-start.23 = (bf16[128,2048]{1,0:T(8,128)(2,1)S(1)}, bf16[128,2048]{1,0:T(8,128)(2,1)S(1)}, u32[]{:S(2)}, u32[]{:S(2)}) collective-permute-start(bf16[128,2048]{1,0:T(8,128)(2,1)S(1)} %fusion.54), channel_id=1, source_target_pairs={{0,24},{8,16},{16,8},{24,0},{1,25},{9,17},{17,9},{25,1},{2,26},{10... | collective-permute-start | bytes 1572872 | tf_op jit(solution)/shard_map/ppermute | solution.py:20
  351.8 62.5 %collective-permute-start.22 = (bf16[128,2048]{1,0:T(8,128)(2,1)S(1)}, bf16[128,2048]{1,0:T(8,128)(2,1)S(1)}, u32[]{:S(2)}, u32[]{:S(2)}) collective-permute-start(bf16[128,2048]{1,0:T(8,128)(2,1)S(1)} %fusion.54), channel_id=1, source_target_pairs={{0,16},{8,24},{16,0},{24,8},{1,17},{9,25},{17,1},{25,9},{2,18},{10... | collective-permute-start | bytes 1572872 | tf_op jit(solution)/shard_map/ppermute | solution.py:20
  353.3 61.0 %collective-permute-start.21 = (bf16[128,2048]{1,0:T(8,128)(2,1)S(1)}, bf16[128,2048]{1,0:T(8,128)(2,1)S(1)}, u32[]{:S(2)}, u32[]{:S(2)}) collective-permute-start(bf16[128,2048]{1,0:T(8,128)(2,1)S(1)} %fusion.54), channel_id=1, source_target_pairs={{0,8},{8,0},{16,24},{24,16},{1,9},{9,1},{17,25},{25,17},{2,10},{10... | collective-permute-start | bytes 1572872 | tf_op jit(solution)/shard_map/ppermute | solution.py:20
  431.7 57.2 %collective-permute-start.27 = (bf16[256,2048]{1,0:T(8,128)(2,1)}, bf16[256,2048]{1,0:T(8,128)(2,1)}, u32[]{:S(2)}, u32[]{:S(2)}) collective-permute-start(bf16[256,2048]{1,0:T(8,128)(2,1)} %pad_maximum_fusion.8), channel_id=1, source_target_pairs={{0,8},{8,0},{16,24},{24,16},{1,9},{9,1},{17,25},{25,17},{2,10},{10... | collective-permute-start | bytes 3145736 | tf_op jit(solution)/shard_map/ppermute | solution.py:20
  433.0 55.9 %collective-permute-start.28 = (bf16[256,2048]{1,0:T(8,128)(2,1)}, bf16[256,2048]{1,0:T(8,128)(2,1)}, u32[]{:S(2)}, u32[]{:S(2)}) collective-permute-start(bf16[256,2048]{1,0:T(8,128)(2,1)} %pad_maximum_fusion.9), channel_id=1, source_target_pairs={{0,16},{8,24},{16,0},{24,8},{1,17},{9,25},{17,1},{25,9},{2,18},{10... | collective-permute-start | bytes 3145736 | tf_op jit(solution)/shard_map/ppermute | solution.py:20
  438.4 161.2 %reduce-scatter.11.cloned.1.call-start = ((), (), s32[]{:S(2)}) async-start(), calls=%async_computation.10 | async-start | bytes 7077888 | tf_op jit(solution)/shard_map/reduce_scatter | solution.py:194
  447.6 64.2 %collective-permute-start.31 = (bf16[2,64,2048]{2,1,0:T(8,128)(2,1)}, bf16[2,64,2048]{2,1,0:T(8,128)(2,1)}, u32[]{:S(2)}, u32[]{:S(2)}) collective-permute-start(bf16[2,64,2048]{2,1,0:T(8,128)(2,1)} %get-tuple-element.127), channel_id=1, source_target_pairs={{0,4},{1,5},{2,6},{3,7},{4,0},{5,1},{6,2},{7,3},{8,12},{9,13},{10,... | collective-permute-start | bytes 1572872 | tf_op jit(solution)/shard_map/ppermute | solution.py:20
  518.4 169.8 %all-gather.16.cloned.1.call-start = ((), (), s32[]{:S(2)}) async-start(), calls=%async_computation.12 | async-start | bytes 3932160 | tf_op jit(solution)/shard_map/all_gather | solution.py:451
  531.2 68.3 %collective-permute-start.35 = (bf16[8,64,2048]{2,1,0:T(8,128)(2,1)}, bf16[8,64,2048]{2,1,0:T(8,128)(2,1)}, u32[]{:S(2)}, u32[]{:S(2)}) collective-permute-start(bf16[8,64,2048]{2,1,0:T(8,128)(2,1)} %bitcast.66.piece_ref), channel_id=1, source_target_pairs={{0,16},{8,24},{16,0},{24,8},{1,17},{9,25},{17,1},{25,9},{2,18},{10... | collective-permute-start | bytes 6291464 | tf_op jit(solution)/shard_map/ppermute | solution.py:20
  531.6 67.9 %collective-permute-start.34 = (bf16[8,64,2048]{2,1,0:T(8,128)(2,1)}, bf16[8,64,2048]{2,1,0:T(8,128)(2,1)}, u32[]{:S(2)}, u32[]{:S(2)}) collective-permute-start(bf16[8,64,2048]{2,1,0:T(8,128)(2,1)} %bitcast.66.piece_ref), channel_id=1, source_target_pairs={{0,8},{8,0},{16,24},{24,16},{1,9},{9,1},{17,25},{25,17},{2,10},{10... | collective-permute-start | bytes 6291464 | tf_op jit(solution)/shard_map/ppermute | solution.py:20
  551.0 47.6 %collective-permute-start.40 = (bf16[128,2048]{1,0:T(8,128)(2,1)}, bf16[128,2048]{1,0:T(8,128)(2,1)S(1)}, u32[]{:S(2)}, u32[]{:S(2)}) collective-permute-start(bf16[128,2048]{1,0:T(8,128)(2,1)} %slice.195), channel_id=1, source_target_pairs={{0,8},{8,0},{16,24},{24,16},{1,9},{9,1},{17,25},{25,17},{2,10},{10... | collective-permute-start | bytes 1572872 | tf_op jit(solution)/shard_map/ppermute | solution.py:20
  603.2 60.8 %collective-permute-start.44 = (bf16[4,64,2048]{2,1,0:T(8,128)(2,1)}, bf16[4,64,2048]{2,1,0:T(8,128)(2,1)S(1)}, u32[]{:S(2)}, u32[]{:S(2)}) collective-permute-start(bf16[4,64,2048]{2,1,0:T(8,128)(2,1)} %slice.196), channel_id=1, source_target_pairs={{0,16},{8,24},{16,0},{24,8},{1,17},{9,25},{17,1},{25,9},{2,18},{10... | collective-permute-start | bytes 3145736 | tf_op jit(solution)/shard_map/ppermute | solution.py:20
  603.8 60.2 %collective-permute-start.45 = (bf16[4,64,2048]{2,1,0:T(8,128)(2,1)S(1)}, bf16[4,64,2048]{2,1,0:T(8,128)(2,1)S(1)}, u32[]{:S(2)}, u32[]{:S(2)}) collective-permute-start(bf16[4,64,2048]{2,1,0:T(8,128)(2,1)S(1)} %slice.197), channel_id=1, source_target_pairs={{0,8},{8,0},{16,24},{24,16},{1,9},{9,1},{17,25},{25,17},{2,10},{10... | collective-permute-start | bytes 3145736 | tf_op jit(solution)/shard_map/ppermute | solution.py:20
  604.8 51.1 %collective-permute-start.48 = (bf16[64,2048]{1,0:T(8,128)(2,1)S(1)}, bf16[64,2048]{1,0:T(8,128)(2,1)}, u32[]{:S(2)}, u32[]{:S(2)}) collective-permute-start(bf16[64,2048]{1,0:T(8,128)(2,1)S(1)} %copy-done.41), channel_id=1, source_target_pairs={{0,24},{8,16},{16,8},{24,0},{1,25},{9,17},{17,9},{25,1},{2,26},{10... | collective-permute-start | bytes 786440 | tf_op jit(solution)/shard_map/ppermute | solution.py:20
  606.7 50.7 %collective-permute-start.47 = (bf16[64,2048]{1,0:T(8,128)(2,1)S(1)}, bf16[64,2048]{1,0:T(8,128)(2,1)}, u32[]{:S(2)}, u32[]{:S(2)}) collective-permute-start(bf16[64,2048]{1,0:T(8,128)(2,1)S(1)} %copy-done.41), channel_id=1, source_target_pairs={{0,16},{8,24},{16,0},{24,8},{1,17},{9,25},{17,1},{25,9},{2,18},{10... | collective-permute-start | bytes 786440 | tf_op jit(solution)/shard_map/ppermute | solution.py:20
  607.3 56.7 %collective-permute-start.46 = (bf16[64,2048]{1,0:T(8,128)(2,1)S(1)}, bf16[64,2048]{1,0:T(8,128)(2,1)}, u32[]{:S(2)}, u32[]{:S(2)}) collective-permute-start(bf16[64,2048]{1,0:T(8,128)(2,1)S(1)} %copy-done.41), channel_id=1, source_target_pairs={{0,8},{8,0},{16,24},{24,16},{1,9},{9,1},{17,25},{25,17},{2,10},{10... | collective-permute-start | bytes 786440 | tf_op jit(solution)/shard_map/ppermute | solution.py:20
  (89 other events, 1356.5 us)
Sparse Core Ops, SparseCore 0:
  14.2 104.1 all-gather.7
  120.6 25.1 all-gather.9
  147.4 46.6 all-gather.13
  196.2 50.6 all-gather.11
  294.5 48.7 reduce-scatter.4
  346.0 48.1 reduce-scatter.6
  438.5 51.8 reduce-scatter.8
  518.5 68.3 reduce-scatter.10
  599.7 64.5 all-gather.15

commit v3 on v2

--- a/solution.py
+++ b/solution.py
@@ -13,6 +13,7 @@
 norm_eps = 1e-05
 score_scale = 0.125
 masked_score = -1e30
+free = pl.CostEstimate(flops=1, bytes_accessed=1, transcendentals=0)
 
 
 def swapped(array, axis, by):
@@ -47,8 +48,8 @@
     ]
 
 
-def crossed(sends):
-    return [swapped(send, "fsdp", 2 * k) for k, send in enumerate(sends, 1)]
+def crossed(sends, first=1):
+    return [swapped(send, "fsdp", 2 * k) for k, send in enumerate(sends, first)]
 
 
 def in_order(pairs, received):
@@ -101,16 +102,47 @@
     return array
 
 
+def wide_fold(parts):
+    size = lax.axis_size("ctx")
+    if size != 4:
+        return first_fold(parts)
+    half = parts[0].shape[0] // 2
+    return first_fold(parts) + [
+        swapped(parts[1][:half], "ctx", 1),
+        swapped(parts[2][half:], "ctx", 2),
+    ]
+
+
+def late_terms(parts, arrived):
+    if lax.axis_size("ctx") != 4:
+        return []
+    half = parts[0].shape[0] // 2
+    return [plus(parts[1][half:], arrived[1]), plus(parts[2][:half], arrived[0])]
+
+
+def late_fold(terms):
+    return [swapped(term, "ctx", k) for k, term in enumerate(terms, 1)]
+
+
+def wide_sum(own, arrived, late):
+    if not late:
+        return plus(own, *arrived)
+    half = own.shape[0] // 2
+    return jnp.concatenate(
+        [plus(own[:half], arrived[2], late[1]), plus(own[half:], arrived[3], late[0])], 0
+    )
+
+
 def plus(*terms):
     return low(sum(term.astype(jnp.float32) for term in terms))
 
 
 def placed(pieces, shape, block, body, result=None):
-    own = lax.axis_index("ctx").astype(jnp.int32)[None]
+    own = jnp.stack([lax.axis_index("ctx"), lax.axis_index("fsdp") // 2]).astype(jnp.int32)
     for piece, k, index in pieces:
 
         def out_map(step, own_ref, k=k, index=index):
-            return index(own_ref[0] ^ k, step)
+            return index(own_ref[0] ^ k, own_ref[1], step)
 
         in_specs = [pl.BlockSpec((1,) + piece.shape[1:], lambda step, own_ref: (step, 0, 0))]
         operands = [own, piece]
@@ -129,9 +161,7 @@
             ),
             out_shape=jax.ShapeDtypeStruct(shape, jnp.float32),
             input_output_aliases=aliases,
-            cost_estimate=pl.CostEstimate(
-                flops=piece.size, bytes_accessed=6 * piece.size, transcendentals=0
-            ),
+            cost_estimate=free,
         )(*operands)
     return result
 
@@ -223,7 +253,6 @@
     length = rows * ctx_count
     heads = width // HD // ctx_count
     own_width = heads * HD
-    inputs = tokens[0].astype(jnp.float32)
     strided = (shard // HD) % ctx_count == 0
 
     chunks = jnp.bitwise_xor(ctx, jnp.arange(ctx_count, dtype=jnp.int32))
@@ -236,9 +265,6 @@
     picked = jnp.sum(jnp.where(matches, order_row[None, :], 0), axis=1)
     positions = picked * half + jnp.tile(local % half, ctx_count)
     cosine, sine = angles(positions, HD)
-    blocks = jnp.concatenate(gathered(block_ids[0], "ctx"), 0)
-    allowed = (blocks[None, :] <= blocks[:, None])[None]
-
     if strided:
         per = heads // fsdp_count
         qkv_own = lax.dynamic_index_in_dim(
@@ -253,11 +279,6 @@
         out_weight = lax.dynamic_slice_in_dim(
             gather_rows(w_out, "fsdp"), ctx * own_width, own_width, 0
         )
-    gains = lax.all_gather(
-        jnp.stack([attn_gain, ffn_gain]), "fsdp", axis=1, tiled=True
-    ).astype(jnp.float32)
-    gain_one, gain_two = gains[0], gains[1]
-
     hidden_own = w_down.shape[0]
     part = shard // ctx_count
     gate_up_own = pl.pallas_call(
@@ -269,14 +290,21 @@
             out_specs=pl.BlockSpec((1, part, 2 * hidden_own), lambda step, own: (step, 0, 0)),
         ),
         out_shape=jax.ShapeDtypeStruct((fsdp_count, part, 2 * hidden_own), jnp.bfloat16),
-        cost_estimate=pl.CostEstimate(
-            flops=0, bytes_accessed=8 * width * part * fsdp_count, transcendentals=0
-        ),
+        cost_estimate=free,
     )(ctx.astype(jnp.int32)[None], w_gate_up)
-    inputs, gate_up_own = together(inputs, gate_up_own)
     gate_up_own = paired(gate_up_own)
-    gate_up_mine = in_order(gate_up_own, crossed(crossing(gate_up_own)))
+    gate_up_sends = crossing(gate_up_own)
+    gate_up_sends, gains, own_tokens = together(
+        gate_up_sends, jnp.stack([attn_gain, ffn_gain]), tokens[0]
+    )
+    gate_up_mine = in_order(gate_up_own, crossed(gate_up_sends))
     gate_up_mine = gate_up_mine.reshape(fsdp_count * part, 2 * hidden_own)
+    seq_inputs = jnp.concatenate(gathered(own_tokens, "ctx"), 0)
+    gains = lax.all_gather(gains, "fsdp", axis=1, tiled=True).astype(jnp.float32)
+    gain_one, gain_two = gains[0], gains[1]
+    own_blocks, seq_inputs = together(block_ids[0], seq_inputs)
+    blocks = jnp.concatenate(gathered(own_blocks, "ctx"), 0)
+    allowed = (blocks[None, :] <= blocks[:, None])[None]
     gate_up_mine, qkv_weight = together(gate_up_mine, qkv_weight)
     gate_up_pieces = first_hop(gate_up_mine)
 
@@ -305,10 +333,11 @@
         array = array.reshape(lead + (ctx_count, fsdp_count, part))
         return jnp.swapaxes(array, -3, -2).reshape(lead + (width,))
 
-    inverse_one = inverse_rms(inputs)
-    normed_one = inputs * inverse_one
-    act_one = low(normed_one * gain_one)
-    act_seq = jnp.concatenate(gathered(act_one, "ctx"), 0)
+    seq_inputs = seq_inputs.astype(jnp.float32)
+    seq_inverse = inverse_rms(seq_inputs)
+    seq_normed = seq_inputs * seq_inverse
+    act_seq = low(seq_normed * gain_one)
+    inputs, inverse_one, normed_one = seq_inputs[:rows], seq_inverse[:rows], seq_normed[:rows]
     qkv = product(act_seq, qkv_weight, 1, 0).reshape(length, 3, heads, HD)
     query = low(rotate(qkv[:, 0], cosine, sine))
     keys = low(rotate(qkv[:, 1], cosine, sine))
@@ -329,10 +358,9 @@
 
     inverse_two = inverse_rms(resid)
     normed_two = resid * inverse_two
+    act_two = to_parts(low(normed_two * gain_two))
     cot = gather_rows(cotangent[0], "fsdp")
-    act_two, cot, gate_up_pieces = together(
-        to_parts(low(normed_two * gain_two)), cot, gate_up_pieces
-    )
+    act_two, cot, gate_up_pieces = together(act_two, cot, gate_up_pieces)
     act_two = gather_rows(act_two, "fsdp")
     gate_up_weight = jnp.concatenate(gate_up_pieces + second_hop(gate_up_pieces), 0)
     gate_up = product(act_two, gate_up_weight, 1, 0)
@@ -356,20 +384,16 @@
     grad_act_two, grad_gu, gu_final = together(grad_act_two, grad_gu, gu_final)
     grad_act_two = scatter_rows(grad_act_two, "fsdp")
     part_gu = [gu_term(k) for k in range(ctx_count - 1)] + [gu_final]
-    gu_halves = first_fold(part_gu)
+    gu_arrived = wide_fold(part_gu)
     out_part = low(product(hidden, w_down, 1, 0))
     part_down = low(product(hidden, cot, 0, 0)).reshape(ctx_count, block, width)
     part_down = [
         lax.dynamic_index_in_dim(part_down, ctx ^ k, 0, keepdims=False) for k in range(ctx_count)
     ]
-    part_gu, gu_halves, out_part, part_down = together(part_gu, gu_halves, out_part, part_down)
-    gu_sends = folded(part_gu, gu_halves)
-    down_halves = first_fold(part_down)
-    down_sends = folded(part_down, down_halves)
-    grad_act_two, gu_sends, out_part, down_sends = together(
-        grad_act_two, gu_sends, out_part, down_sends
-    )
-    gu_last = second_fold(gu_sends, gu_halves)
+    part_gu, gu_arrived, out_part, part_down = together(part_gu, gu_arrived, out_part, part_down)
+    gu_terms = late_terms(part_gu, gu_arrived)
+    grad_act_two, out_part = together(grad_act_two, out_part)
+    gu_late = late_fold(gu_terms)
     layer_part = scatter_rows(out_part, "fsdp")
     grad_act_two = from_parts(grad_act_two).astype(jnp.float32)
     grad_gain_two = jnp.sum(grad_act_two * normed_two, 0)
@@ -378,21 +402,24 @@
     )
 
     grad_branch = jnp.concatenate(gathered(low(grad_resid), "ctx"), 0)
-    grad_branch, gu_last = together(grad_branch, gu_last)
-    gu_pairs = paired(plus(part_gu[0], *gu_last).reshape(fsdp_count, part, 2 * hidden_own))
+    grad_branch, gu_late, part_down = together(grad_branch, gu_late, part_down)
+    down_halves = first_fold(part_down)
+    gu_sum = wide_sum(part_gu[0], gu_arrived, gu_late)
+    gu_pairs = paired(gu_sum.reshape(fsdp_count, part, 2 * hidden_own))
+    part_out = low(product(attn_b, grad_branch, 0, 0))
     grad_att = low(product(grad_branch, out_weight, 1, 1)).reshape(length, heads, HD)
     gu_sends = crossing(gu_pairs)
-    part_out = low(product(attn_b, grad_branch, 0, 0))
-    grad_att, gu_pairs, gu_sends, down_sends, part_out = together(
-        grad_att, gu_pairs, gu_sends, down_sends, part_out
-    )
+    grad_att, part_out, gu_pairs, gu_sends, down_halves = together(
+        grad_att, part_out, gu_pairs, gu_sends, down_halves
+    )
+    gu_received = crossed(gu_sends)
+    down_last = second_fold(folded(part_down, down_halves), down_halves)
     part_out = scatter_rows(part_out, "fsdp") if strided else part_out
-    gu_received = crossed(gu_sends)
-    down_last = second_fold(down_sends, down_halves)
     delta = jnp.sum(grad_att.astype(jnp.float32) * attended, -1)
-    grad_values = jnp.einsum("hqk,qhe->khe", probs_b, grad_att, preferred_element_type=jnp.float32)
     grad_probs = jnp.einsum("qhe,khe->hqk", grad_att, values, preferred_element_type=jnp.float32)
     grad_scores = low(probs * (grad_probs - delta.T[..., None]))
+    grad_scores, gu_received[:1] = together(grad_scores, gu_received[:1])
+    grad_values = jnp.einsum("hqk,qhe->khe", probs_b, grad_att, preferred_element_type=jnp.float32)
     grad_query = (
         jnp.einsum("hqk,khe->qhe", grad_scores, keys, preferred_element_type=jnp.float32)
         * score_scale
@@ -409,82 +436,94 @@
     grad_qkv, down_last, layer_part, gu_received[::2] = together(
         grad_qkv, down_last, layer_part, gu_received[::2]
     )
-    down_pieces = first_hop(plus(part_down[0], *down_last))
+
+    gu_own = lax.dynamic_index_in_dim(gu_pairs, lax.axis_index("fsdp") // 2, 0, keepdims=False)
+    chips = len(gu_received) + 1
+    gu_near = first_hop(jnp.concatenate([gu_own] + gu_received[: chips // 2 - 1], 0))
     part_qkv = low(product(act_seq, grad_qkv, 0, 0))
-    back = low(product(grad_qkv, qkv_weight, 1, 1)).reshape(ctx_count, rows, width)
+    back = low(product(grad_qkv, qkv_weight, 1, 1))
+    grad_gain_one = jnp.sum(back.astype(jnp.float32) * seq_normed, 0)
+    grad_gains = jnp.stack([grad_gain_one, grad_gain_two])
+    back = back.reshape(ctx_count, rows, width)
     back = [back[k] for k in range(ctx_count)]
-    part_qkv, part_out, back, gu_received, down_pieces = together(
-        part_qkv, part_out, back, gu_received, down_pieces
+    part_down = plus(part_down[0], *down_last)
+    part_qkv, part_out, back, gu_near, gu_received, grad_gains, part_down = together(
+        part_qkv, part_out, back, gu_near, gu_received, grad_gains, part_down
     )
     part_qkv = scatter_rows(part_qkv, "fsdp")
-
-    grad_act_one = scattered(back, "ctx")
-    gu_sum = in_order(gu_pairs, gu_received)
-    gu_pieces = first_hop(gu_sum)
-    grad_act_one, down_pieces = together(grad_act_one, down_pieces)
+    back_halves = first_fold(back)
+    grad_gains, back_halves = together(grad_gains, back_halves)
+    gu_far = first_hop(jnp.concatenate(gu_received[chips // 2 - 1 :], 0))
+    back_last = second_fold(folded(back, back_halves), back_halves)
+    grad_act_one = sum(term.astype(jnp.float32) for term in [back[0]] + back_last)
+    if ctx_count == 4:
+        gu_near.append(swapped(gu_near[1], "ctx", 2))
+    layer_out = low(resid + layer_part.astype(jnp.float32))
+    input_grad = low(grad_resid + norm_back(grad_act_one, normed_one, gain_one, inverse_one))
+
+    def gate_up_columns(offset):
+        return lambda other, chip, step: (other, 0, 2 * (chip ^ (offset + step // 2)) + step % 2)
+
+    grad_gate_up = placed(
+        [(piece, k, gate_up_columns(0)) for k, piece in enumerate(gu_near[:3])],
+        w_gate_up.shape,
+        (part, 2, hidden_own),
+        write_pair,
+    )
+    gu_far, gu_near, layer_out, input_grad, part_down, grad_gains, grad_gate_up = together(
+        gu_far, gu_near, layer_out, input_grad, part_down, grad_gains, grad_gate_up
+    )
+    if ctx_count == 4:
+        gu_far.append(swapped(gu_far[2], "ctx", 1))
+    down_pieces = first_hop(part_down)
+    grad_gains = butterfly(grad_gains, "fsdp")
+    grad_gate_up = placed(
+        [(piece, k, gate_up_columns(0)) for k, piece in enumerate(gu_near) if k > 2]
+        + [(piece, k, gate_up_columns(chips // 2)) for k, piece in enumerate(gu_far[:3])],
+        w_gate_up.shape,
+        (part, 2, hidden_own),
+        write_pair,
+        grad_gate_up,
+    )
+    gu_far, down_pieces, grad_gate_up, part_qkv = together(
+        gu_far, down_pieces, grad_gate_up, part_qkv
+    )
+    part_qkv = lax.all_gather(part_qkv, "ctx", axis=0)
     down_last = second_hop(down_pieces)
-    layer_out = low(resid + layer_part.astype(jnp.float32))
-    grad_gain_one = jnp.sum(grad_act_one * normed_one, 0)
-    grad_gains = jnp.stack([grad_gain_one, grad_gain_two])
-    grad_gains = butterfly(grad_gains, "fsdp")
-    input_grad = low(grad_resid + norm_back(grad_act_one, normed_one, gain_one, inverse_one))
+    if strided:
+        out_pieces = gathered(part_out, "ctx")
+    else:
+        out_pieces = [scatter_rows(gather_rows(part_out, "ctx"), "fsdp")]
+    grad_gains = butterfly(grad_gains, "ctx")
+    grad_gains = lax.dynamic_slice_in_dim(grad_gains, lax.axis_index("fsdp") * shard, shard, 1)
+    grad_gate_up = placed(
+        [(piece, k, gate_up_columns(chips // 2)) for k, piece in enumerate(gu_far) if k > 2],
+        w_gate_up.shape,
+        (part, 2, hidden_own),
+        write_pair,
+        grad_gate_up,
+    )
     rows_each = block // 2
 
     def down_rows(offset):
-        return lambda other, step: (other * 2 + offset + step, 0)
+        return lambda other, chip, step: (other * 2 + offset + step, 0)
 
     grad_down = placed(
         [
             (piece.reshape(2, rows_each, width), k, down_rows(0))
             for k, piece in enumerate(down_pieces)
-        ],
+        ]
+        + [(piece[None], 3, down_rows(k)) for k, piece in enumerate(down_last)],
         w_down.shape,
         (rows_each, width),
         write_rows,
     )
-    gu_pieces, down_last, layer_out, input_grad, grad_down, part_out, grad_gains, part_qkv = (
-        together(
-            gu_pieces, down_last, layer_out, input_grad, grad_down, part_out, grad_gains, part_qkv
-        )
-    )
-    gu_last = second_hop(gu_pieces)
-    part_qkv = lax.all_gather(part_qkv, "ctx", axis=0)
-    if strided:
-        out_pieces = gathered(part_out, "ctx")
-    else:
-        out_pieces = [scatter_rows(gather_rows(part_out, "ctx"), "fsdp")]
-
-    def gate_up_columns(offset):
-        return lambda other, step: (other, 0, offset + step)
-
-    grad_gate_up = placed(
-        [(piece, k, gate_up_columns(0)) for k, piece in enumerate(gu_pieces)],
-        w_gate_up.shape,
-        (part, 2, hidden_own),
-        write_pair,
-    )
-    grad_gate_up, gu_last, out_pieces, grad_gains = together(
-        grad_gate_up, gu_last, out_pieces, grad_gains
-    )
-    grad_gains = butterfly(grad_gains, "ctx")
-    grad_gains = lax.dynamic_slice_in_dim(grad_gains, lax.axis_index("fsdp") * shard, shard, 1)
-    grad_gate_up = placed(
-        [(piece, 3, gate_up_columns(k * fsdp_count // 2)) for k, piece in enumerate(gu_last)],
-        w_gate_up.shape,
-        (part, 2, hidden_own),
-        write_pair,
-        grad_gate_up,
-    )
-    grad_down = placed(
-        [(piece[None], 3, down_rows(k)) for k, piece in enumerate(down_last)],
-        w_down.shape,
-        (rows_each, width),
-        write_rows,
-        grad_down,
-    )
     if strided:
         grad_out = placed(
-            [(piece[None], k, lambda other, step: (other, 0)) for k, piece in enumerate(out_pieces)],
+            [
+                (piece[None], k, lambda other, chip, step: (other, 0))
+                for k, piece in enumerate(out_pieces)
+            ],
             w_out.shape,
             out_pieces[0].shape,
             write_rows,
@@ -498,9 +537,7 @@
             in_specs=[pl.BlockSpec((ctx_count, shard, own_width), lambda step: (0, 0, step))],
             out_specs=pl.BlockSpec((1, shard, width), lambda step: (step, 0, 0)),
             out_shape=jax.ShapeDtypeStruct((3, shard, width), jnp.float32),
-            cost_estimate=pl.CostEstimate(
-                flops=part_qkv.size, bytes_accessed=6 * part_qkv.size, transcendentals=0
-            ),
+            cost_estimate=free,
         )(part_qkv)
         grad_w_qkv = jnp.transpose(grad_w_qkv, (1, 0, 2))
     else:

time: 705 us -> 684 us (0.970)
  waiting for transfers between devices: 326 us -> 238 us
  blocking collectives: 12.4 us -> 53.6 us
  Pallas kernels: 58.2 us -> 73.3 us
  other arithmetic: 43.9 us -> 55.1 us
  local copies, waits for them, and re-layouts: 64.8 us -> 55.7 us
    ppermute x51 -> x56, waiting for transfers between devices: 297 us -> 211 us  [swapped(): return lax.ppermute(array, axis, [(i, i ^ by) for i in range(size)])]
    all_gather x1, blocking collectives: 12.4 us -> 53.6 us  [per_device(): lax.all_gather(gains, 'fsdp', axis=1, tiled=True).astype(jnp.float32)]
    pallas_call x14 -> x17, Pallas kernels: 44.7 us -> 60.1 us  [placed(): pl.pallas_call(body, grid_spec=pltpu.PrefetchScalarGridSpec(num_scalar_pr...]
    dynamic_update_slice x7 -> x3, local copies, waits for them, and re-layouts: 11.5 us -> 2.58 us  [in_order(): pairs = lax.dynamic_update_index_in_dim(pairs, pair, chip ^ k, 0)]
    convert_element_type x11 -> x12, other arithmetic: 19.1 us -> 24.2 us  [low(): return values.astype(jnp.bfloat16)]
    ppermute x51 -> x56, starting transfers between devices: 62.3 us -> 65.8 us  [swapped(): return lax.ppermute(array, axis, [(i, i ^ by) for i in range(size)])]
    unnamed x123 -> x135, local copies, waits for them, and re-layouts: 25.3 us -> 23.8 us
  transfers between devices with their start and end apart: 60 -> 65, of which waited for: 27 -> 30; matrix products, arithmetic and copies ran while one was open for 23% -> 25% of each run, Pallas kernels for 8% -> 10%
where the time goes in v3:
time: 684 us; the launch traced here: 676 us
  waiting for transfers between devices  238 us (35%)
  matrix products  119 us (17%)
  Pallas kernels  73.3 us (11%)
  starting transfers between devices  66.7 us (10%)
  local copies, waits for them, and re-layouts  55.7 us (8%)
  other arithmetic  55.1 us (8%)
  blocking collectives  53.6 us (8%)
  between operations  15.3 us (2%)
    ppermute x56, waiting for transfers between devices, swapped(): return lax.ppermute(array, axis, [(i, i ^ by) for i in range(size)])  211 us
    dot_general x15, matrix products, product(): lax.dot_general(left, right, (((left_dim,), (right_dim,)), ((), ())), pre...  96.4 us
    ppermute x56, starting transfers between devices, swapped(): return lax.ppermute(array, axis, [(i, i ^ by) for i in range(size)])  65.8 us
    pallas_call x17, Pallas kernels, placed(): pl.pallas_call(body, grid_spec=pltpu.PrefetchScalarGridSpec(num_scalar_pr...  60.1 us
    all_gather x1, blocking collectives, per_device(): lax.all_gather(gains, 'fsdp', axis=1, tiled=True).astype(jnp.float32)  53.6 us
    all_gather x4, waiting for transfers between devices, gather_rows(): return lax.all_gather(array, axis, axis=0, tiled=True)  27 us
    convert_element_type x12, other arithmetic, low(): return values.astype(jnp.bfloat16)  24.2 us
    unnamed x135, local copies, waits for them, and re-layouts  23.8 us
  transfers between devices with their start and end apart: 65, of which 30 were waited for; matrix products, arithmetic and copies ran while one was open for 25% of the time, Pallas kernels for 10%

profile of v3, /device:TPU:0, one launch (start us, length us, event | category | flops | bytes accessed | tf_op | source)
XLA Modules:
  0.0 676.5 jit_solution(1190125187631758000)
XLA Ops:
  7.2 4.7 copy.67
  15.0 7.8 %shard_map.161 = bf16[8,64,2048]{2,1,0:T(8,128)(2,1)} custom-call(s32[1]{0:T(128)} %bitcast.1.own_ref, bf16[256,2,8192]{2,1,0:T(2,128)(2,1)} %in_ref.1), custom_call_target="tpu_custom_call" | custom-call | flops 1 | bytes 1 | tf_op jit(solution)/shard_map/pallas_call | solution.py:284
  37.8 53.6 %all_gather.21 = bf16[2,2048]{1,0:T(2,128)(2,1)S(1)} all-gather(bf16[2,256]{1,0:T(2,128)(2,1)S(1)} %pad_maximum_fusion.29), channel_id=1, replica_groups=mesh['ctx'=4,'fsdp'=8] {'fsdp'}, dimensions={1}, use_global_device_ids=true | all-gather | bytes 9216 | tf_op jit(solution)/shard_map/all_gather | solution.py:303
  98.4 15.5 %collective-permute-done.6 = bf16[2,64,2048]{2,1,0:T(8,128)(2,1)S(1)} collective-permute-done((bf16[2,64,2048]{2,1,0:T(8,128)(2,1)S(1)}, bf16[2,64,2048]{2,1,0:T(8,128)(2,1)S(1)}, u32[]{:S(2)}, u32[]{:S(2)}) %collective-permute-start.6) | collective-permute-done | bytes 524320 | tf_op jit(solution)/shard_map/ppermute | solution.py:21
  116.3 7.7 %all-gather.8.cloned.1.call-done = bf16[2048,1536]{0,1:T(8,128)(2,1)} async-done(((bf16[256,1536]{0,1:T(8,128)(2,1)}), bf16[2048,1536]{0,1:T(8,128)(2,1)}) %all-gather.8.cloned.1.call-update) | async-done | bytes 6291472 | tf_op jit(solution)/shard_map/all_gather | solution.py:220
  126.7 6.0 fusion.23
  134.6 8.3 %fusion.60 = (f32[8,512]{1,0:T(8,128)S(1)}, f32[8,512,512]{1,2,0:T(8,128)}) fusion(pred[512,512]{0,1:T(8,128)(4,1)} %broadcast_compare_fusion, bf16[512,8,32]{0,2,1:T(8,128)(2,1)S(1)} %get-tuple-element.238, bf16[512,8,32]{0,2,1:T(8,128)(2,1)} %get-tuple-element.239, bf16[512,8,32]{0,2,1:T(8,128)(2,1)} %get-tuple-element.219, ...), kind=kOutput, calls=%fused_computation.201 | convolution fusion | flops 281018880 | bytes 9715712 | tf_op jit(solution)/shard_map/sub | solution.py:350
  142.9 4.7 fusion.6
  153.2 4.9 fusion.62
  163.3 21.3 %collective-permute-done.12 = bf16[128,2048]{1,0:T(8,128)(2,1)S(1)} collective-permute-done((bf16[128,2048]{1,0:T(8,128)(2,1)}, bf16[128,2048]{1,0:T(8,128)(2,1)S(1)}, u32[]{:S(2)}, u32[]{:S(2)}) %collective-permute-start.12) | collective-permute-done | bytes 524320 | tf_op jit(solution)/shard_map/ppermute | solution.py:21
  184.6 10.7 %collective-permute-done.11 = bf16[128,2048]{1,0:T(8,128)(2,1)S(1)} collective-permute-done((bf16[128,2048]{1,0:T(8,128)(2,1)}, bf16[128,2048]{1,0:T(8,128)(2,1)S(1)}, u32[]{:S(2)}, u32[]{:S(2)}) %collective-permute-start.11) | collective-permute-done | bytes 524320 | tf_op jit(solution)/shard_map/ppermute | solution.py:21
  216.8 11.4 %collective-permute-done.15 = bf16[256,2048]{1,0:T(8,128)(2,1)S(1)} collective-permute-done((bf16[256,2048]{1,0:T(8,128)(2,1)S(1)}, bf16[256,2048]{1,0:T(8,128)(2,1)S(1)}, u32[]{:S(2)}, u32[]{:S(2)}) %collective-permute-start.15) | collective-permute-done | bytes 1048608 | tf_op jit(solution)/shard_map/ppermute | solution.py:21
  231.8 17.6 %all-gather.12.cloned.1.call-done = bf16[1024,2048]{1,0:T(8,128)(2,1)} async-done(((bf16[128,2048]{1,0:T(8,128)(2,1)}), bf16[1024,2048]{1,0:T(8,128)(2,1)}) %all-gather.12.cloned.1.call-update) | async-done | bytes 4194320 | tf_op jit(solution)/shard_map/all_gather | solution.py:220
  249.4 15.4 %fusion.63 = f32[1024,2048]{0,1:T(8,128)} fusion(bf16[1024,2048]{1,0:T(8,128)(2,1)} %all-gather.12.cloned.1.call-done, bf16[2048,2048]{1,0:T(8,128)(2,1)} %constant_dynamic-update-slice_fusion.1), kind=kOutput, calls=%fused_computation.204 | convolution fusion | flops 8589934592 | bytes 20971520 | tf_op jit(solution)/shard_map/dot_general | solution.py:206
  264.8 9.3 %multiply_convert_fusion.3 = (bf16[1024,1024]{0,1:T(8,128)(2,1)S(1)}, bf16[1024,1024]{0,1:T(8,128)(2,1)S(1)}, bf16[1024,1024]{0,1:T(8,128)(2,1)}) fusion(f32[1024,2048]{0,1:T(8,128)} %fusion.63, bf16[1024,2048]{1,0:T(8,128)(2,1)S(1)} %bitcast.225, bf16[1024,2048]{1,0:T(8,128)(2,1)S(1)} %copy-done.52), kind=kOutput, calls=%fused_computation.10 | convolution fusion | flops 4310695936 | bytes 23068672 | tf_op jit(solution)/shard_map/dot_general | solution.py:206
  275.4 12.9 %convolution_convert_fusion.1 = bf16[1024,2048]{1,0:T(8,128)(2,1)} fusion(bf16[2048,2048]{1,0:T(8,128)(2,1)} %constant_dynamic-update-slice_fusion.1, bf16[1024,1024]{0,1:T(8,128)(2,1)S(1)} %get-tuple-element.183, bf16[1024,1024]{0,1:T(8,128)(2,1)S(1)} %get-tuple-element.182), kind=kOutput, calls=%fused_computation.19 | convolution fusion | flops 8600420352 | bytes 16777216 | tf_op jit(solution)/shard_map/dot_general | solution.py:206
  315.2 4.9 convolution_convert_fusion.2
  323.9 6.2 convolution_convert_fusion.3
  330.1 16.4 %collective-permute-done.19 = bf16[256,2048]{1,0:T(8,128)(2,1)} collective-permute-done((bf16[256,2048]{1,0:T(8,128)(2,1)}, bf16[256,2048]{1,0:T(8,128)(2,1)}, u32[]{:S(2)}, u32[]{:S(2)}) %collective-permute-start.19) | collective-permute-done | bytes 1048608 | tf_op jit(solution)/shard_map/ppermute | solution.py:21
  363.9 25.3 %collective-permute-done.23 = bf16[128,2048]{1,0:T(8,128)(2,1)S(1)} collective-permute-done((bf16[128,2048]{1,0:T(8,128)(2,1)S(1)}, bf16[128,2048]{1,0:T(8,128)(2,1)S(1)}, u32[]{:S(2)}, u32[]{:S(2)}) %collective-permute-start.23) | collective-permute-done | bytes 524320 | tf_op jit(solution)/shard_map/ppermute | solution.py:21
  389.2 11.4 %collective-permute-done.22 = bf16[128,2048]{1,0:T(8,128)(2,1)} collective-permute-done((bf16[128,2048]{1,0:T(8,128)(2,1)S(1)}, bf16[128,2048]{1,0:T(8,128)(2,1)}, u32[]{:S(2)}, u32[]{:S(2)}) %collective-permute-start.22) | collective-permute-done | bytes 524320 | tf_op jit(solution)/shard_map/ppermute | solution.py:21
  449.1 6.0 collective-permute-done.32
  459.7 7.2 %convolution_convert_fusion = bf16[2048,1536]{1,0:T(8,128)(2,1)} fusion(bf16[512,1536]{0,1:T(8,128)(2,1)} %bitcast.177, f32[2048]{0:T(1024)S(1)} %bitcast.216, f32[512]{0:T(512)S(1)} %copy-done.50, bf16[512,2048]{1,0:T(8,128)(2,1)S(1)} %copy-done.4), kind=kOutput, calls=%fused_computation.4 | convolution fusion | flops 3228565504 | bytes 9971712 | tf_op jit(solution)/shard_map/dot_general | solution.py:206
  466.9 9.2 %broadcast_multiply_fusion = (f32[512,2048]{1,0:T(8,128)}, f32[2048]{0:T(1024)S(1)}, bf16[512,2048]{1,0:T(8,128)(2,1)S(1)}) fusion(f32[512]{0:T(512)S(1)} %copy-done.50, bf16[512,2048]{1,0:T(8,128)(2,1)S(1)} %copy-done.4, bf16[512,1536]{0,1:T(8,128)(2,1)} %bitcast.178, bf16[2048,1536]{0,1:T(8,128)(2,1)} %all-gather.8.cloned.1.call-done), kind=kOutput, calls=%fused_computation.51 | convolution fusion | flops 3227514880 | bytes 16263168 | tf_op jit(solution)/shard_map/dot_general | solution.py:206
  479.4 19.4 %collective-permute-done.35 = bf16[2,64,2048]{2,1,0:T(8,128)(2,1)} collective-permute-done((bf16[2,64,2048]{2,1,0:T(8,128)(2,1)}, bf16[2,64,2048]{2,1,0:T(8,128)(2,1)}, u32[]{:S(2)}, u32[]{:S(2)}) %collective-permute-start.35) | collective-permute-done | bytes 524320 | tf_op jit(solution)/shard_map/ppermute | solution.py:21
  501.1 4.7 collective-permute-done.39
  536.6 7.7 %collective-permute-done.36.piece_ref = bf16[4,64,2048]{2,1,0:T(8,128)(2,1)} collective-permute-done((bf16[4,64,2048]{2,1,0:T(8,128)(2,1)}, bf16[4,64,2048]{2,1,0:T(8,128)(2,1)}, u32[]{:S(2)}, u32[]{:S(2)}) %collective-permute-start.36) | collective-permute-done | bytes 1048608 | tf_op jit(solution)/shard_map/ppermute | solution.py:21
  544.7 19.7 %collective-permute-done.38.piece_ref = bf16[4,64,2048]{2,1,0:T(8,128)(2,1)} collective-permute-done((bf16[4,64,2048]{2,1,0:T(8,128)(2,1)}, bf16[4,64,2048]{2,1,0:T(8,128)(2,1)}, u32[]{:S(2)}, u32[]{:S(2)}) %collective-permute-start.38) | collective-permute-done | bytes 1048608 | tf_op jit(solution)/shard_map/ppermute | solution.py:21
  585.9 4.8 collective-permute-done.48.piece_ref
  590.7 19.6 %collective-permute-done.49 = bf16[256,2048]{1,0:T(8,128)(2,1)S(1)} collective-permute-done((bf16[256,2048]{1,0:T(8,128)(2,1)}, bf16[256,2048]{1,0:T(8,128)(2,1)S(1)}, u32[]{:S(2)}, u32[]{:S(2)}) %collective-permute-start.49) | collective-permute-done | bytes 1048608 | tf_op jit(solution)/shard_map/ppermute | solution.py:21
  615.1 5.5 collective-permute-start.44
  664.3 5.4 shard_map.169
  (391 shorter events, 276.2 us)
Async XLA Ops:
  7.2 116.8 %all-gather.8.cloned.1.call-start = ((), (), s32[]{:S(2)}) async-start(), calls=%async_computation.4 | async-start | bytes 7077888 | tf_op jit(solution)/shard_map/all_gather | solution.py:220
  14.1 139.1 %all-gather.10.cloned.1.call-start = ((), (), s32[]{:S(2)}) async-start(), calls=%async_computation.5 | async-start | bytes 2359296 | tf_op jit(solution)/shard_map/all_gather | solution.py:220
  14.9 186.6 %all-gather.14.cloned.1.call-start = ((), (), s32[]{:S(2)}) async-start(), calls=%async_computation.11 | async-start | bytes 4718592 | tf_op jit(solution)/shard_map/all_gather | solution.py:220
  24.8 224.6 %all-gather.12.cloned.1.call-start = ((), (), s32[]{:S(2)}) async-start(), calls=%async_computation.6 | async-start | bytes 4718592 | tf_op jit(solution)/shard_map/all_gather | solution.py:220
  28.6 64.4 %collective-permute-start.3 = (bf16[128,2048]{1,0:T(8,128)(2,1)S(1)}, bf16[128,2048]{1,0:T(8,128)(2,1)S(1)}, u32[]{:S(2)}, u32[]{:S(2)}) collective-permute-start(bf16[128,2048]{1,0:T(8,128)(2,1)S(1)} %bitcast.205), channel_id=1, source_target_pairs={{0,24},{8,16},{16,8},{24,0},{1,25},{9,17},{17,9},{25,1},{2,26},{10... | collective-permute-start | bytes 1572872 | tf_op jit(solution)/shard_map/ppermute | solution.py:21
  32.8 60.2 %collective-permute-start.2 = (bf16[128,2048]{1,0:T(8,128)(2,1)S(1)}, bf16[128,2048]{1,0:T(8,128)(2,1)S(1)}, u32[]{:S(2)}, u32[]{:S(2)}) collective-permute-start(bf16[128,2048]{1,0:T(8,128)(2,1)S(1)} %bitcast.206), channel_id=1, source_target_pairs={{0,16},{8,24},{16,0},{24,8},{1,17},{9,25},{17,1},{25,9},{2,18},{10... | collective-permute-start | bytes 1572872 | tf_op jit(solution)/shard_map/ppermute | solution.py:21
  33.3 59.6 %collective-permute-start.1 = (bf16[128,2048]{1,0:T(8,128)(2,1)S(1)}, bf16[128,2048]{1,0:T(8,128)(2,1)S(1)}, u32[]{:S(2)}, u32[]{:S(2)}) collective-permute-start(bf16[128,2048]{1,0:T(8,128)(2,1)S(1)} %bitcast.207), channel_id=1, source_target_pairs={{0,8},{8,0},{16,24},{24,16},{1,9},{9,1},{17,25},{25,17},{2,10},{10... | collective-permute-start | bytes 1572872 | tf_op jit(solution)/shard_map/ppermute | solution.py:21
  33.4 63.0 %collective-permute-start.4 = (bf16[2,64,2048]{2,1,0:T(8,128)(2,1)S(1)}, bf16[2,64,2048]{2,1,0:T(8,128)(2,1)S(1)}, u32[]{:S(2)}, u32[]{:S(2)}) collective-permute-start(bf16[2,64,2048]{2,1,0:T(8,128)(2,1)S(1)} %get-tuple-element.96), channel_id=1, source_target_pairs={{0,2},{1,3},{2,0},{3,1},{4,6},{5,7},{6,4},{7,5},{8,10},{9,11},{10,... | collective-permute-start | bytes 1572872 | tf_op jit(solution)/shard_map/ppermute | solution.py:21
  35.4 62.2 %collective-permute-start.5 = (bf16[2,64,2048]{2,1,0:T(8,128)(2,1)S(1)}, bf16[2,64,2048]{2,1,0:T(8,128)(2,1)S(1)}, u32[]{:S(2)}, u32[]{:S(2)}) collective-permute-start(bf16[2,64,2048]{2,1,0:T(8,128)(2,1)S(1)} %get-tuple-element.97), channel_id=1, source_target_pairs={{0,4},{1,5},{2,6},{3,7},{4,0},{5,1},{6,2},{7,3},{8,12},{9,13},{10,... | collective-permute-start | bytes 1572872 | tf_op jit(solution)/shard_map/ppermute | solution.py:21
  124.0 77.5 %collective-permute-start.13 = (bf16[512,2048]{1,0:T(8,128)(2,1)}, bf16[512,2048]{1,0:T(8,128)(2,1)}, u32[]{:S(2)}, u32[]{:S(2)}) collective-permute-start(bf16[512,2048]{1,0:T(8,128)(2,1)} %bitcast.16), channel_id=1, source_target_pairs={{0,8},{8,0},{16,24},{24,16},{1,9},{9,1},{17,25},{25,17},{2,10},{10... | collective-permute-start | bytes 6291464 | tf_op jit(solution)/shard_map/ppermute | solution.py:21
  125.1 76.3 %collective-permute-start.14 = (bf16[512,2048]{1,0:T(8,128)(2,1)}, bf16[512,2048]{1,0:T(8,128)(2,1)}, u32[]{:S(2)}, u32[]{:S(2)}) collective-permute-start(bf16[512,2048]{1,0:T(8,128)(2,1)} %bitcast.16), channel_id=1, source_target_pairs={{0,16},{8,24},{16,0},{24,8},{1,17},{9,25},{17,1},{25,9},{2,18},{10... | collective-permute-start | bytes 6291464 | tf_op jit(solution)/shard_map/ppermute | solution.py:21
  161.6 33.7 %collective-permute-start.11 = (bf16[128,2048]{1,0:T(8,128)(2,1)}, bf16[128,2048]{1,0:T(8,128)(2,1)S(1)}, u32[]{:S(2)}, u32[]{:S(2)}) collective-permute-start(bf16[128,2048]{1,0:T(8,128)(2,1)} %get-tuple-element.210), channel_id=1, source_target_pairs={{0,16},{8,24},{16,0},{24,8},{1,17},{9,25},{17,1},{25,9},{2,18},{10... | collective-permute-start | bytes 1572872 | tf_op jit(solution)/shard_map/ppermute | solution.py:21
  162.2 33.2 %collective-permute-start.10 = (bf16[128,2048]{1,0:T(8,128)(2,1)}, bf16[128,2048]{1,0:T(8,128)(2,1)}, u32[]{:S(2)}, u32[]{:S(2)}) collective-permute-start(bf16[128,2048]{1,0:T(8,128)(2,1)} %get-tuple-element.208), channel_id=1, source_target_pairs={{0,8},{8,0},{16,24},{24,16},{1,9},{9,1},{17,25},{25,17},{2,10},{10... | collective-permute-start | bytes 1572872 | tf_op jit(solution)/shard_map/ppermute | solution.py:21
  201.5 153.8 %reduce-scatter.5.cloned.1.call-start = ((), (), s32[]{:S(2)}) async-start(), calls=%async_computation.7 | async-start | bytes 4718592 | tf_op jit(solution)/shard_map/reduce_scatter | solution.py:224
  296.8 158.3 %reduce-scatter.7.cloned.1.call-start = ((), (), s32[]{:S(2)}) async-start(), calls=%async_computation.8 | async-start | bytes 4718592 | tf_op jit(solution)/shard_map/reduce_scatter | solution.py:224
  298.4 31.7 %collective-permute-start.17 = (bf16[256,2048]{1,0:T(8,128)(2,1)}, bf16[256,2048]{1,0:T(8,128)(2,1)}, u32[]{:S(2)}, u32[]{:S(2)}) collective-permute-start(bf16[256,2048]{1,0:T(8,128)(2,1)} %get-tuple-element.207), channel_id=1, source_target_pairs={{0,8},{8,0},{16,24},{24,16},{1,9},{9,1},{17,25},{25,17},{2,10},{10... | collective-permute-start | bytes 3145736 | tf_op jit(solution)/shard_map/ppermute | solution.py:21
  306.4 40.1 %collective-permute-start.19 = (bf16[256,2048]{1,0:T(8,128)(2,1)}, bf16[256,2048]{1,0:T(8,128)(2,1)}, u32[]{:S(2)}, u32[]{:S(2)}) collective-permute-start(bf16[256,2048]{1,0:T(8,128)(2,1)} %slice.257), channel_id=1, source_target_pairs={{0,8},{8,0},{16,24},{24,16},{1,9},{9,1},{17,25},{25,17},{2,10},{10... | collective-permute-start | bytes 3145736 | tf_op jit(solution)/shard_map/ppermute | solution.py:21
  310.3 37.4 %collective-permute-start.20 = (bf16[256,2048]{1,0:T(8,128)(2,1)}, bf16[256,2048]{1,0:T(8,128)(2,1)}, u32[]{:S(2)}, u32[]{:S(2)}) collective-permute-start(bf16[256,2048]{1,0:T(8,128)(2,1)} %slice.258), channel_id=1, source_target_pairs={{0,16},{8,24},{16,0},{24,8},{1,17},{9,25},{17,1},{25,9},{2,18},{10... | collective-permute-start | bytes 3145736 | tf_op jit(solution)/shard_map/ppermute | solution.py:21
  350.7 51.3 %collective-permute-start.24 = (bf16[256,2048]{1,0:T(8,128)(2,1)}, bf16[256,2048]{1,0:T(8,128)(2,1)}, u32[]{:S(2)}, u32[]{:S(2)}) collective-permute-start(bf16[256,2048]{1,0:T(8,128)(2,1)} %add_convert_fusion.4), channel_id=1, source_target_pairs={{0,8},{8,0},{16,24},{24,16},{1,9},{9,1},{17,25},{25,17},{2,10},{10... | collective-permute-start | bytes 3145736 | tf_op jit(solution)/shard_map/ppermute | solution.py:21
  353.9 48.2 %collective-permute-start.25 = (bf16[256,2048]{1,0:T(8,128)(2,1)}, bf16[256,2048]{1,0:T(8,128)(2,1)}, u32[]{:S(2)}, u32[]{:S(2)}) collective-permute-start(bf16[256,2048]{1,0:T(8,128)(2,1)} %add_convert_fusion.3), channel_id=1, source_target_pairs={{0,16},{8,24},{16,0},{24,8},{1,17},{9,25},{17,1},{25,9},{2,18},{10... | collective-permute-start | bytes 3145736 | tf_op jit(solution)/shard_map/ppermute | solution.py:21
  356.7 142.1 %reduce-scatter.9.cloned.1.call-start = ((), (), s32[]{:S(2)}) async-start(), calls=%async_computation.9 | async-start | bytes 2359296 | tf_op jit(solution)/shard_map/reduce_scatter | solution.py:224
  361.9 38.7 %collective-permute-start.22 = (bf16[128,2048]{1,0:T(8,128)(2,1)S(1)}, bf16[128,2048]{1,0:T(8,128)(2,1)}, u32[]{:S(2)}, u32[]{:S(2)}) collective-permute-start(bf16[128,2048]{1,0:T(8,128)(2,1)S(1)} %fusion.51), channel_id=1, source_target_pairs={{0,16},{8,24},{16,0},{24,8},{1,17},{9,25},{17,1},{25,9},{2,18},{10... | collective-permute-start | bytes 1572872 | tf_op jit(solution)/shard_map/ppermute | solution.py:21
  363.3 37.2 %collective-permute-start.21 = (bf16[128,2048]{1,0:T(8,128)(2,1)S(1)}, bf16[128,2048]{1,0:T(8,128)(2,1)}, u32[]{:S(2)}, u32[]{:S(2)}) collective-permute-start(bf16[128,2048]{1,0:T(8,128)(2,1)S(1)} %fusion.51), channel_id=1, source_target_pairs={{0,8},{8,0},{16,24},{24,16},{1,9},{9,1},{17,25},{25,17},{2,10},{10... | collective-permute-start | bytes 1572872 | tf_op jit(solution)/shard_map/ppermute | solution.py:21
  433.8 65.0 %collective-permute-start.35 = (bf16[2,64,2048]{2,1,0:T(8,128)(2,1)}, bf16[2,64,2048]{2,1,0:T(8,128)(2,1)}, u32[]{:S(2)}, u32[]{:S(2)}) collective-permute-start(bf16[2,64,2048]{2,1,0:T(8,128)(2,1)} %get-tuple-element.141), channel_id=1, source_target_pairs={{0,4},{1,5},{2,6},{3,7},{4,0},{5,1},{6,2},{7,3},{8,12},{9,13},{10,... | collective-permute-start | bytes 1572872 | tf_op jit(solution)/shard_map/ppermute | solution.py:21
  439.3 171.0 %reduce-scatter.11.cloned.1.call-start = ((), (), s32[]{:S(2)}) async-start(), calls=%async_computation.10 | async-start | bytes 7077888 | tf_op jit(solution)/shard_map/reduce_scatter | solution.py:224
  457.5 41.3 %collective-permute-start.33 = (bf16[4,64,2048]{2,1,0:T(8,128)(2,1)}, bf16[4,64,2048]{2,1,0:T(8,128)(2,1)}, u32[]{:S(2)}, u32[]{:S(2)}) collective-permute-start(bf16[4,64,2048]{2,1,0:T(8,128)(2,1)} %pad_maximum_fusion.9.piece_ref), channel_id=1, source_target_pairs={{0,8},{8,0},{16,24},{24,16},{1,9},{9,1},{17,25},{25,17},{2,10},{10... | collective-permute-start | bytes 3145736 | tf_op jit(solution)/shard_map/ppermute | solution.py:21
  458.2 40.6 %collective-permute-start.34 = (bf16[4,64,2048]{2,1,0:T(8,128)(2,1)}, bf16[4,64,2048]{2,1,0:T(8,128)(2,1)}, u32[]{:S(2)}, u32[]{:S(2)}) collective-permute-start(bf16[4,64,2048]{2,1,0:T(8,128)(2,1)} %pad_maximum_fusion.9.piece_ref), channel_id=1, source_target_pairs={{0,16},{8,24},{16,0},{24,8},{1,17},{9,25},{17,1},{25,9},{2,18},{10... | collective-permute-start | bytes 3145736 | tf_op jit(solution)/shard_map/ppermute | solution.py:21
  498.8 165.5 %all-gather.16.cloned.1.call-start = ((), (), s32[]{:S(2)}) async-start(), calls=%async_computation.12 | async-start | bytes 3932160 | tf_op jit(solution)/shard_map/all_gather | solution.py:491
  521.7 42.7 %collective-permute-start.38 = (bf16[4,64,2048]{2,1,0:T(8,128)(2,1)}, bf16[4,64,2048]{2,1,0:T(8,128)(2,1)}, u32[]{:S(2)}, u32[]{:S(2)}) collective-permute-start(bf16[4,64,2048]{2,1,0:T(8,128)(2,1)} %collective-permute-done.33.piece_ref), channel_id=1, source_target_pairs={{0,16},{8,24},{16,0},{24,8},{1,17},{9,25},{17,1},{25,9},{2,18},{10... | collective-permute-start | bytes 3145736 | tf_op jit(solution)/shard_map/ppermute | solution.py:21
  565.8 44.5 %collective-permute-start.49 = (bf16[256,2048]{1,0:T(8,128)(2,1)}, bf16[256,2048]{1,0:T(8,128)(2,1)S(1)}, u32[]{:S(2)}, u32[]{:S(2)}) collective-permute-start(bf16[256,2048]{1,0:T(8,128)(2,1)} %add_convert_fusion), channel_id=1, source_target_pairs={{0,8},{8,0},{16,24},{24,16},{1,9},{9,1},{17,25},{25,17},{2,10},{10... | collective-permute-start | bytes 3145736 | tf_op jit(solution)/shard_map/ppermute | solution.py:21
  566.4 43.9 %collective-permute-start.50 = (bf16[256,2048]{1,0:T(8,128)(2,1)}, bf16[256,2048]{1,0:T(8,128)(2,1)S(1)}, u32[]{:S(2)}, u32[]{:S(2)}) collective-permute-start(bf16[256,2048]{1,0:T(8,128)(2,1)} %add_convert_fusion), channel_id=1, source_target_pairs={{0,16},{8,24},{16,0},{24,8},{1,17},{9,25},{17,1},{25,9},{2,18},{10... | collective-permute-start | bytes 3145736 | tf_op jit(solution)/shard_map/ppermute | solution.py:21
  630.9 30.7 %collective-permute-start.54 = (bf16[128,2048]{1,0:T(8,128)(2,1)}, bf16[128,2048]{1,0:T(8,128)(2,1)}, u32[]{:S(2)}, u32[]{:S(2)}) collective-permute-start(bf16[128,2048]{1,0:T(8,128)(2,1)} %slice.235), channel_id=1, source_target_pairs={{0,8},{8,0},{16,24},{24,16},{1,9},{9,1},{17,25},{25,17},{2,10},{10... | collective-permute-start | bytes 1572872 | tf_op jit(solution)/shard_map/ppermute | solution.py:21
  (97 other events, 1501.0 us)
Sparse Core Ops, SparseCore 0:
  14.2 109.7 all-gather.7
  126.1 26.9 all-gather.9
  154.8 46.6 all-gather.13
  203.5 45.8 all-gather.11
  297.0 48.7 reduce-scatter.4
  356.9 47.7 reduce-scatter.6
  439.5 53.8 reduce-scatter.8
  499.0 75.4 reduce-scatter.10
  610.4 49.6 all-gather.15

commit v4 on v3

--- a/solution.py
+++ b/solution.py
@@ -175,6 +175,30 @@
 
 def write_rows(own_ref, piece_ref, *refs):
     refs[-1][...] = piece_ref[0].astype(jnp.float32)
+
+
+def stacked(pieces, shape):
+    own = lax.axis_index("ctx").astype(jnp.int32)[None]
+    each = shape[0] // lax.axis_size("ctx")
+
+    def body(own_ref, *refs):
+        for ref, (piece, k, row) in zip(refs, pieces):
+            start = pl.multiple_of((own_ref[0] ^ k) * each + row, 16)
+            refs[-1][pl.ds(start, piece.shape[0]), :] = ref[...].astype(jnp.float32)
+
+    return pl.pallas_call(
+        body,
+        grid_spec=pltpu.PrefetchScalarGridSpec(
+            num_scalar_prefetch=1,
+            grid=(1,),
+            in_specs=[
+                pl.BlockSpec(piece.shape, lambda step, own_ref: (0, 0)) for piece, _, _ in pieces
+            ],
+            out_specs=pl.BlockSpec(shape, lambda step, own_ref: (0, 0)),
+        ),
+        out_shape=jax.ShapeDtypeStruct(shape, jnp.float32),
+        cost_estimate=free,
+    )(own, *[piece for piece, _, _ in pieces])
 
 
 def angles(positions, width):
@@ -419,6 +443,9 @@
     grad_probs = jnp.einsum("qhe,khe->hqk", grad_att, values, preferred_element_type=jnp.float32)
     grad_scores = low(probs * (grad_probs - delta.T[..., None]))
     grad_scores, gu_received[:1] = together(grad_scores, gu_received[:1])
+    gu_own = lax.dynamic_index_in_dim(gu_pairs, lax.axis_index("fsdp") // 2, 0, keepdims=False)
+    chips = len(gu_received) + 1
+    gu_near = first_hop(jnp.concatenate([gu_own] + gu_received[: chips // 2 - 1], 0))
     grad_values = jnp.einsum("hqk,qhe->khe", probs_b, grad_att, preferred_element_type=jnp.float32)
     grad_query = (
         jnp.einsum("hqk,khe->qhe", grad_scores, keys, preferred_element_type=jnp.float32)
@@ -433,31 +460,28 @@
             [rotate(grad_query, cosine, -sine), rotate(grad_keys, cosine, -sine), grad_values], 1
         )
     ).reshape(length, 3 * own_width)
-    grad_qkv, down_last, layer_part, gu_received[::2] = together(
-        grad_qkv, down_last, layer_part, gu_received[::2]
-    )
-
-    gu_own = lax.dynamic_index_in_dim(gu_pairs, lax.axis_index("fsdp") // 2, 0, keepdims=False)
-    chips = len(gu_received) + 1
-    gu_near = first_hop(jnp.concatenate([gu_own] + gu_received[: chips // 2 - 1], 0))
     part_qkv = low(product(act_seq, grad_qkv, 0, 0))
     back = low(product(grad_qkv, qkv_weight, 1, 1))
     grad_gain_one = jnp.sum(back.astype(jnp.float32) * seq_normed, 0)
     grad_gains = jnp.stack([grad_gain_one, grad_gain_two])
     back = back.reshape(ctx_count, rows, width)
     back = [back[k] for k in range(ctx_count)]
-    part_down = plus(part_down[0], *down_last)
-    part_qkv, part_out, back, gu_near, gu_received, grad_gains, part_down = together(
-        part_qkv, part_out, back, gu_near, gu_received, grad_gains, part_down
+    part_qkv, back, grad_gains, down_last, layer_part, gu_received[::2], gu_near = together(
+        part_qkv, back, grad_gains, down_last, layer_part, gu_received[::2], gu_near
+    )
+
+    back_halves = first_fold(back)
+    down_pieces = first_hop(plus(part_down[0], *down_last))
+    part_qkv, part_out, back_halves, gu_received, down_pieces = together(
+        part_qkv, part_out, back_halves, gu_received, down_pieces
     )
     part_qkv = scatter_rows(part_qkv, "fsdp")
-    back_halves = first_fold(back)
-    grad_gains, back_halves = together(grad_gains, back_halves)
     gu_far = first_hop(jnp.concatenate(gu_received[chips // 2 - 1 :], 0))
     back_last = second_fold(folded(back, back_halves), back_halves)
     grad_act_one = sum(term.astype(jnp.float32) for term in [back[0]] + back_last)
     if ctx_count == 4:
         gu_near.append(swapped(gu_near[1], "ctx", 2))
+    grad_act_one, gu_near[:3] = together(grad_act_one, gu_near[:3])
     layer_out = low(resid + layer_part.astype(jnp.float32))
     input_grad = low(grad_resid + norm_back(grad_act_one, normed_one, gain_one, inverse_one))
 
@@ -470,13 +494,13 @@
         (part, 2, hidden_own),
         write_pair,
     )
-    gu_far, gu_near, layer_out, input_grad, part_down, grad_gains, grad_gate_up = together(
-        gu_far, gu_near, layer_out, input_grad, part_down, grad_gains, grad_gate_up
-    )
+    gu_far, gu_near, layer_out, input_grad, down_pieces, grad_gate_up, part_qkv = together(
+        gu_far, gu_near, layer_out, input_grad, down_pieces, grad_gate_up, part_qkv
+    )
+    part_qkv = lax.all_gather(part_qkv, "ctx", axis=0)
     if ctx_count == 4:
         gu_far.append(swapped(gu_far[2], "ctx", 1))
-    down_pieces = first_hop(part_down)
-    grad_gains = butterfly(grad_gains, "fsdp")
+    down_last = second_hop(down_pieces)
     grad_gate_up = placed(
         [(piece, k, gate_up_columns(0)) for k, piece in enumerate(gu_near) if k > 2]
         + [(piece, k, gate_up_columns(chips // 2)) for k, piece in enumerate(gu_far[:3])],
@@ -485,17 +509,29 @@
         write_pair,
         grad_gate_up,
     )
-    gu_far, down_pieces, grad_gate_up, part_qkv = together(
-        gu_far, down_pieces, grad_gate_up, part_qkv
-    )
-    part_qkv = lax.all_gather(part_qkv, "ctx", axis=0)
-    down_last = second_hop(down_pieces)
+    rows_each = block // 2
+
+    def down_rows(offset):
+        return lambda other, chip, step: (other * 2 + offset + step, 0)
+
+    grad_down = placed(
+        [
+            (piece.reshape(2, rows_each, width), k, down_rows(0))
+            for k, piece in enumerate(down_pieces)
+        ],
+        w_down.shape,
+        (rows_each, width),
+        write_rows,
+    )
+    grad_gate_up, grad_down, grad_gains = together(grad_gate_up, grad_down, grad_gains)
+    grad_gains = butterfly(grad_gains, "fsdp")
+    gu_far, down_last, grad_gate_up, grad_down, grad_gains = together(
+        gu_far, down_last, grad_gate_up, grad_down, grad_gains
+    )
     if strided:
         out_pieces = gathered(part_out, "ctx")
     else:
         out_pieces = [scatter_rows(gather_rows(part_out, "ctx"), "fsdp")]
-    grad_gains = butterfly(grad_gains, "ctx")
-    grad_gains = lax.dynamic_slice_in_dim(grad_gains, lax.axis_index("fsdp") * shard, shard, 1)
     grad_gate_up = placed(
         [(piece, k, gate_up_columns(chips // 2)) for k, piece in enumerate(gu_far) if k > 2],
         w_gate_up.shape,
@@ -503,33 +539,22 @@
         write_pair,
         grad_gate_up,
     )
-    rows_each = block // 2
-
-    def down_rows(offset):
-        return lambda other, chip, step: (other * 2 + offset + step, 0)
-
     grad_down = placed(
-        [
-            (piece.reshape(2, rows_each, width), k, down_rows(0))
-            for k, piece in enumerate(down_pieces)
-        ]
-        + [(piece[None], 3, down_rows(k)) for k, piece in enumerate(down_last)],
+        [(piece[None], 3, down_rows(k)) for k, piece in enumerate(down_last)],
         w_down.shape,
         (rows_each, width),
         write_rows,
+        grad_down,
+    )
+    grad_gains, grad_gate_up, grad_down, out_pieces, part_qkv = together(
+        grad_gains, grad_gate_up, grad_down, out_pieces, part_qkv
     )
     if strided:
-        grad_out = placed(
-            [
-                (piece[None], k, lambda other, chip, step: (other, 0))
-                for k, piece in enumerate(out_pieces)
-            ],
-            w_out.shape,
-            out_pieces[0].shape,
-            write_rows,
-        )
+        grad_out = stacked([(piece, k, 0) for k, piece in enumerate(out_pieces)], w_out.shape)
     else:
         grad_out = out_pieces[0].astype(jnp.float32)
+    grad_gains = butterfly(grad_gains, "ctx")
+    grad_gains = lax.dynamic_slice_in_dim(grad_gains, lax.axis_index("fsdp") * shard, shard, 1)
     if strided:
         grad_w_qkv = pl.pallas_call(
             functools.partial(write_heads, fsdp_count),

time: 684 us -> 677 us (0.990)
  local copies, waits for them, and re-layouts: 55.7 us -> 64.4 us
  Pallas kernels: 73.3 us -> 66.2 us
    pallas_call x17 -> x13, Pallas kernels: 60.1 us -> 50.3 us  [placed(): pl.pallas_call(body, grid_spec=pltpu.PrefetchScalarGridSpec(num_scalar_pr...]
    reduce_scatter x4, waiting for transfers between devices: 0.03 us -> 8.18 us  [scatter_rows(): return lax.psum_scatter(low(array), axis, scatter_dimension=0, tiled=True)]
    unnamed x135 -> x141, local copies, waits for them, and re-layouts: 23.8 us -> 26.3 us
  transfers between devices with their start and end apart: 65 -> 65, of which waited for: 30 -> 31; matrix products, arithmetic and copies ran while one was open for 25% -> 25% of each run, Pallas kernels for 10% -> 10%
where the time goes in v4:
time: 677 us; the launch traced here: 671 us
  waiting for transfers between devices  241 us (36%)
  matrix products  113 us (17%)
  Pallas kernels  66.2 us (10%)
  local copies, waits for them, and re-layouts  64.4 us (10%)
  starting transfers between devices  63.9 us (9%)
  blocking collectives  53.6 us (8%)
  other arithmetic  52.8 us (8%)
  between operations  15.3 us (2%)
    ppermute x56, waiting for transfers between devices, swapped(): return lax.ppermute(array, axis, [(i, i ^ by) for i in range(size)])  206 us
    dot_general x15, matrix products, product(): lax.dot_general(left, right, (((left_dim,), (right_dim,)), ((), ())), pre...  91.6 us
    ppermute x56, starting transfers between devices, swapped(): return lax.ppermute(array, axis, [(i, i ^ by) for i in range(size)])  63 us
    all_gather x1, blocking collectives, per_device(): lax.all_gather(gains, 'fsdp', axis=1, tiled=True).astype(jnp.float32)  53.6 us
    pallas_call x13, Pallas kernels, placed(): pl.pallas_call(body, grid_spec=pltpu.PrefetchScalarGridSpec(num_scalar_pr...  50.3 us
    all_gather x4, waiting for transfers between devices, gather_rows(): return lax.all_gather(array, axis, axis=0, tiled=True)  27.1 us
    unnamed x141, local copies, waits for them, and re-layouts  26.3 us
    convert_element_type x12, other arithmetic, low(): return values.astype(jnp.bfloat16)  24.8 us
  transfers between devices with their start and end apart: 65, of which 31 were waited for; matrix products, arithmetic and copies ran while one was open for 25% of the time, Pallas kernels for 10%

profile of v4, /device:TPU:0, one launch (start us, length us, event | category | flops | bytes accessed | tf_op | source)
XLA Modules:
  0.0 670.7 jit_solution(6222565594557938235)
XLA Ops:
  7.2 4.7 copy.64
  15.0 7.8 %shard_map.161 = bf16[8,64,2048]{2,1,0:T(8,128)(2,1)} custom-call(s32[1]{0:T(128)} %bitcast.1.own_ref, bf16[256,2,8192]{2,1,0:T(2,128)(2,1)} %in_ref.1), custom_call_target="tpu_custom_call" | custom-call | flops 1 | bytes 1 | tf_op jit(solution)/shard_map/pallas_call | solution.py:308
  37.8 53.6 %all_gather.21 = bf16[2,2048]{1,0:T(2,128)(2,1)S(1)} all-gather(bf16[2,256]{1,0:T(2,128)(2,1)S(1)} %pad_maximum_fusion.29), channel_id=1, replica_groups=mesh['ctx'=4,'fsdp'=8] {'fsdp'}, dimensions={1}, use_global_device_ids=true | all-gather | bytes 9216 | tf_op jit(solution)/shard_map/all_gather | solution.py:327
  98.4 15.5 %collective-permute-done.6 = bf16[2,64,2048]{2,1,0:T(8,128)(2,1)S(1)} collective-permute-done((bf16[2,64,2048]{2,1,0:T(8,128)(2,1)S(1)}, bf16[2,64,2048]{2,1,0:T(8,128)(2,1)S(1)}, u32[]{:S(2)}, u32[]{:S(2)}) %collective-permute-start.6) | collective-permute-done | bytes 524320 | tf_op jit(solution)/shard_map/ppermute | solution.py:21
  116.3 7.7 %all-gather.8.cloned.1.call-done = bf16[2048,1536]{0,1:T(8,128)(2,1)} async-done(((bf16[256,1536]{0,1:T(8,128)(2,1)}), bf16[2048,1536]{0,1:T(8,128)(2,1)}) %all-gather.8.cloned.1.call-update) | async-done | bytes 6291472 | tf_op jit(solution)/shard_map/all_gather | solution.py:244
  126.7 6.0 fusion.23
  134.6 8.3 %fusion.60 = (f32[8,512]{1,0:T(8,128)S(1)}, f32[8,512,512]{1,2,0:T(8,128)}) fusion(pred[512,512]{0,1:T(8,128)(4,1)} %broadcast_compare_fusion, bf16[512,8,32]{0,2,1:T(8,128)(2,1)S(1)} %get-tuple-element.272, bf16[512,8,32]{0,2,1:T(8,128)(2,1)} %get-tuple-element.273, bf16[512,8,32]{0,2,1:T(8,128)(2,1)} %get-tuple-element.253, ...), kind=kOutput, calls=%fused_computation.201 | convolution fusion | flops 281018880 | bytes 9715712 | tf_op jit(solution)/shard_map/sub | solution.py:374
  142.9 4.7 fusion.6
  153.2 4.9 fusion.62
  163.3 21.3 %collective-permute-done.12 = bf16[128,2048]{1,0:T(8,128)(2,1)S(1)} collective-permute-done((bf16[128,2048]{1,0:T(8,128)(2,1)}, bf16[128,2048]{1,0:T(8,128)(2,1)S(1)}, u32[]{:S(2)}, u32[]{:S(2)}) %collective-permute-start.12) | collective-permute-done | bytes 524320 | tf_op jit(solution)/shard_map/ppermute | solution.py:21
  184.6 10.7 %collective-permute-done.11 = bf16[128,2048]{1,0:T(8,128)(2,1)S(1)} collective-permute-done((bf16[128,2048]{1,0:T(8,128)(2,1)}, bf16[128,2048]{1,0:T(8,128)(2,1)S(1)}, u32[]{:S(2)}, u32[]{:S(2)}) %collective-permute-start.11) | collective-permute-done | bytes 524320 | tf_op jit(solution)/shard_map/ppermute | solution.py:21
  216.8 11.4 %collective-permute-done.15 = bf16[256,2048]{1,0:T(8,128)(2,1)S(1)} collective-permute-done((bf16[256,2048]{1,0:T(8,128)(2,1)S(1)}, bf16[256,2048]{1,0:T(8,128)(2,1)S(1)}, u32[]{:S(2)}, u32[]{:S(2)}) %collective-permute-start.15) | collective-permute-done | bytes 1048608 | tf_op jit(solution)/shard_map/ppermute | solution.py:21
  231.8 17.6 %all-gather.12.cloned.1.call-done = bf16[1024,2048]{1,0:T(8,128)(2,1)} async-done(((bf16[128,2048]{1,0:T(8,128)(2,1)}), bf16[1024,2048]{1,0:T(8,128)(2,1)}) %all-gather.12.cloned.1.call-update) | async-done | bytes 4194320 | tf_op jit(solution)/shard_map/all_gather | solution.py:244
  249.4 15.4 %fusion.63 = f32[1024,2048]{0,1:T(8,128)} fusion(bf16[1024,2048]{1,0:T(8,128)(2,1)} %all-gather.12.cloned.1.call-done, bf16[2048,2048]{1,0:T(8,128)(2,1)} %constant_dynamic-update-slice_fusion.1), kind=kOutput, calls=%fused_computation.204 | convolution fusion | flops 8589934592 | bytes 20971520 | tf_op jit(solution)/shard_map/dot_general | solution.py:230
  264.8 9.3 %multiply_convert_fusion.3 = (bf16[1024,1024]{0,1:T(8,128)(2,1)S(1)}, bf16[1024,1024]{0,1:T(8,128)(2,1)S(1)}, bf16[1024,1024]{0,1:T(8,128)(2,1)}) fusion(f32[1024,2048]{0,1:T(8,128)} %fusion.63, bf16[1024,2048]{1,0:T(8,128)(2,1)S(1)} %bitcast.222, bf16[1024,2048]{1,0:T(8,128)(2,1)S(1)} %copy-done.53), kind=kOutput, calls=%fused_computation.10 | convolution fusion | flops 4310695936 | bytes 23068672 | tf_op jit(solution)/shard_map/dot_general | solution.py:230
  275.4 12.9 %convolution_convert_fusion.1 = bf16[1024,2048]{1,0:T(8,128)(2,1)} fusion(bf16[2048,2048]{1,0:T(8,128)(2,1)} %constant_dynamic-update-slice_fusion.1, bf16[1024,1024]{0,1:T(8,128)(2,1)S(1)} %get-tuple-element.217, bf16[1024,1024]{0,1:T(8,128)(2,1)S(1)} %get-tuple-element.216), kind=kOutput, calls=%fused_computation.19 | convolution fusion | flops 8600420352 | bytes 16777216 | tf_op jit(solution)/shard_map/dot_general | solution.py:230
  315.2 4.9 convolution_convert_fusion.2
  323.9 6.3 convolution_convert_fusion.3
  330.2 16.3 %collective-permute-done.19 = bf16[256,2048]{1,0:T(8,128)(2,1)} collective-permute-done((bf16[256,2048]{1,0:T(8,128)(2,1)}, bf16[256,2048]{1,0:T(8,128)(2,1)}, u32[]{:S(2)}, u32[]{:S(2)}) %collective-permute-start.19) | collective-permute-done | bytes 1048608 | tf_op jit(solution)/shard_map/ppermute | solution.py:21
  363.8 25.3 %collective-permute-done.23 = bf16[128,2048]{1,0:T(8,128)(2,1)S(1)} collective-permute-done((bf16[128,2048]{1,0:T(8,128)(2,1)S(1)}, bf16[128,2048]{1,0:T(8,128)(2,1)S(1)}, u32[]{:S(2)}, u32[]{:S(2)}) %collective-permute-start.23) | collective-permute-done | bytes 524320 | tf_op jit(solution)/shard_map/ppermute | solution.py:21
  389.1 11.4 %collective-permute-done.22 = bf16[128,2048]{1,0:T(8,128)(2,1)} collective-permute-done((bf16[128,2048]{1,0:T(8,128)(2,1)S(1)}, bf16[128,2048]{1,0:T(8,128)(2,1)}, u32[]{:S(2)}, u32[]{:S(2)}) %collective-permute-start.22) | collective-permute-done | bytes 524320 | tf_op jit(solution)/shard_map/ppermute | solution.py:21
  452.0 5.5 broadcast_multiply_fusion
  457.5 5.9 convolution_convert_fusion
  466.3 9.4 %collective-permute-done.33.piece_ref = bf16[4,64,2048]{2,1,0:T(8,128)(2,1)} collective-permute-done((bf16[4,64,2048]{2,1,0:T(8,128)(2,1)S(1)}, bf16[4,64,2048]{2,1,0:T(8,128)(2,1)}, u32[]{:S(2)}, u32[]{:S(2)}) %collective-permute-start.33) | collective-permute-done | bytes 1048608 | tf_op jit(solution)/shard_map/ppermute | solution.py:21
  487.3 20.0 %collective-permute-done.37 = bf16[2,64,2048]{2,1,0:T(8,128)(2,1)} collective-permute-done((bf16[2,64,2048]{2,1,0:T(8,128)(2,1)}, bf16[2,64,2048]{2,1,0:T(8,128)(2,1)}, u32[]{:S(2)}, u32[]{:S(2)}) %collective-permute-start.37) | collective-permute-done | bytes 524320 | tf_op jit(solution)/shard_map/ppermute | solution.py:21
  525.0 4.5 collective-permute-done.43
  540.5 4.5 shard_map.164.refs_0_
  552.1 18.9 %collective-permute-done.41.piece_ref = bf16[4,64,2048]{2,1,0:T(8,128)(2,1)} collective-permute-done((bf16[4,64,2048]{2,1,0:T(8,128)(2,1)}, bf16[4,64,2048]{2,1,0:T(8,128)(2,1)}, u32[]{:S(2)}, u32[]{:S(2)}) %collective-permute-start.41) | collective-permute-done | bytes 1048608 | tf_op jit(solution)/shard_map/ppermute | solution.py:21
  571.0 8.2 %reduce-scatter.11.cloned.1.call-done = bf16[256,1536]{1,0:T(8,128)(2,1)} async-done(((bf16[2048,1536]{1,0:T(8,128)(2,1)}), bf16[256,1536]{1,0:T(8,128)(2,1)}) %reduce-scatter.11.cloned.1.call-update) | async-done | bytes 786448 | tf_op jit(solution)/shard_map/reduce_scatter | solution.py:248
  585.1 4.5 shard_map.165.refs_0_
  624.8 11.4 %collective-permute-done.47 = bf16[128,2048]{1,0:T(8,128)(2,1)S(1)} collective-permute-done((bf16[128,2048]{1,0:T(8,128)(2,1)S(1)}, bf16[128,2048]{1,0:T(8,128)(2,1)S(1)}, u32[]{:S(2)}, u32[]{:S(2)}) %collective-permute-start.47) | collective-permute-done | bytes 524320 | tf_op jit(solution)/shard_map/ppermute | solution.py:21
  655.3 5.4 shard_map.175
  (396 shorter events, 281.2 us)
Async XLA Ops:
  7.2 116.8 %all-gather.8.cloned.1.call-start = ((), (), s32[]{:S(2)}) async-start(), calls=%async_computation.4 | async-start | bytes 7077888 | tf_op jit(solution)/shard_map/all_gather | solution.py:244
  14.1 139.1 %all-gather.10.cloned.1.call-start = ((), (), s32[]{:S(2)}) async-start(), calls=%async_computation.5 | async-start | bytes 2359296 | tf_op jit(solution)/shard_map/all_gather | solution.py:244
  14.9 186.6 %all-gather.14.cloned.1.call-start = ((), (), s32[]{:S(2)}) async-start(), calls=%async_computation.11 | async-start | bytes 4718592 | tf_op jit(solution)/shard_map/all_gather | solution.py:244
  24.8 224.6 %all-gather.12.cloned.1.call-start = ((), (), s32[]{:S(2)}) async-start(), calls=%async_computation.6 | async-start | bytes 4718592 | tf_op jit(solution)/shard_map/all_gather | solution.py:244
  28.6 64.4 %collective-permute-start.3 = (bf16[128,2048]{1,0:T(8,128)(2,1)S(1)}, bf16[128,2048]{1,0:T(8,128)(2,1)S(1)}, u32[]{:S(2)}, u32[]{:S(2)}) collective-permute-start(bf16[128,2048]{1,0:T(8,128)(2,1)S(1)} %bitcast.204), channel_id=1, source_target_pairs={{0,24},{8,16},{16,8},{24,0},{1,25},{9,17},{17,9},{25,1},{2,26},{10... | collective-permute-start | bytes 1572872 | tf_op jit(solution)/shard_map/ppermute | solution.py:21
  32.8 60.2 %collective-permute-start.2 = (bf16[128,2048]{1,0:T(8,128)(2,1)S(1)}, bf16[128,2048]{1,0:T(8,128)(2,1)S(1)}, u32[]{:S(2)}, u32[]{:S(2)}) collective-permute-start(bf16[128,2048]{1,0:T(8,128)(2,1)S(1)} %bitcast.205), channel_id=1, source_target_pairs={{0,16},{8,24},{16,0},{24,8},{1,17},{9,25},{17,1},{25,9},{2,18},{10... | collective-permute-start | bytes 1572872 | tf_op jit(solution)/shard_map/ppermute | solution.py:21
  33.3 59.6 %collective-permute-start.1 = (bf16[128,2048]{1,0:T(8,128)(2,1)S(1)}, bf16[128,2048]{1,0:T(8,128)(2,1)S(1)}, u32[]{:S(2)}, u32[]{:S(2)}) collective-permute-start(bf16[128,2048]{1,0:T(8,128)(2,1)S(1)} %bitcast.206), channel_id=1, source_target_pairs={{0,8},{8,0},{16,24},{24,16},{1,9},{9,1},{17,25},{25,17},{2,10},{10... | collective-permute-start | bytes 1572872 | tf_op jit(solution)/shard_map/ppermute | solution.py:21
  33.4 63.0 %collective-permute-start.4 = (bf16[2,64,2048]{2,1,0:T(8,128)(2,1)S(1)}, bf16[2,64,2048]{2,1,0:T(8,128)(2,1)S(1)}, u32[]{:S(2)}, u32[]{:S(2)}) collective-permute-start(bf16[2,64,2048]{2,1,0:T(8,128)(2,1)S(1)} %get-tuple-element.113), channel_id=1, source_target_pairs={{0,2},{1,3},{2,0},{3,1},{4,6},{5,7},{6,4},{7,5},{8,10},{9,11},{10,... | collective-permute-start | bytes 1572872 | tf_op jit(solution)/shard_map/ppermute | solution.py:21
  35.4 62.2 %collective-permute-start.5 = (bf16[2,64,2048]{2,1,0:T(8,128)(2,1)S(1)}, bf16[2,64,2048]{2,1,0:T(8,128)(2,1)S(1)}, u32[]{:S(2)}, u32[]{:S(2)}) collective-permute-start(bf16[2,64,2048]{2,1,0:T(8,128)(2,1)S(1)} %get-tuple-element.114), channel_id=1, source_target_pairs={{0,4},{1,5},{2,6},{3,7},{4,0},{5,1},{6,2},{7,3},{8,12},{9,13},{10,... | collective-permute-start | bytes 1572872 | tf_op jit(solution)/shard_map/ppermute | solution.py:21
  124.0 77.5 %collective-permute-start.13 = (bf16[512,2048]{1,0:T(8,128)(2,1)}, bf16[512,2048]{1,0:T(8,128)(2,1)}, u32[]{:S(2)}, u32[]{:S(2)}) collective-permute-start(bf16[512,2048]{1,0:T(8,128)(2,1)} %bitcast.16), channel_id=1, source_target_pairs={{0,8},{8,0},{16,24},{24,16},{1,9},{9,1},{17,25},{25,17},{2,10},{10... | collective-permute-start | bytes 6291464 | tf_op jit(solution)/shard_map/ppermute | solution.py:21
  125.2 76.3 %collective-permute-start.14 = (bf16[512,2048]{1,0:T(8,128)(2,1)}, bf16[512,2048]{1,0:T(8,128)(2,1)}, u32[]{:S(2)}, u32[]{:S(2)}) collective-permute-start(bf16[512,2048]{1,0:T(8,128)(2,1)} %bitcast.16), channel_id=1, source_target_pairs={{0,16},{8,24},{16,0},{24,8},{1,17},{9,25},{17,1},{25,9},{2,18},{10... | collective-permute-start | bytes 6291464 | tf_op jit(solution)/shard_map/ppermute | solution.py:21
  161.6 33.7 %collective-permute-start.11 = (bf16[128,2048]{1,0:T(8,128)(2,1)}, bf16[128,2048]{1,0:T(8,128)(2,1)S(1)}, u32[]{:S(2)}, u32[]{:S(2)}) collective-permute-start(bf16[128,2048]{1,0:T(8,128)(2,1)} %get-tuple-element.244), channel_id=1, source_target_pairs={{0,16},{8,24},{16,0},{24,8},{1,17},{9,25},{17,1},{25,9},{2,18},{10... | collective-permute-start | bytes 1572872 | tf_op jit(solution)/shard_map/ppermute | solution.py:21
  162.2 33.2 %collective-permute-start.10 = (bf16[128,2048]{1,0:T(8,128)(2,1)}, bf16[128,2048]{1,0:T(8,128)(2,1)}, u32[]{:S(2)}, u32[]{:S(2)}) collective-permute-start(bf16[128,2048]{1,0:T(8,128)(2,1)} %get-tuple-element.242), channel_id=1, source_target_pairs={{0,8},{8,0},{16,24},{24,16},{1,9},{9,1},{17,25},{25,17},{2,10},{10... | collective-permute-start | bytes 1572872 | tf_op jit(solution)/shard_map/ppermute | solution.py:21
  201.5 153.7 %reduce-scatter.5.cloned.1.call-start = ((), (), s32[]{:S(2)}) async-start(), calls=%async_computation.7 | async-start | bytes 4718592 | tf_op jit(solution)/shard_map/reduce_scatter | solution.py:248
  296.9 181.4 %reduce-scatter.7.cloned.1.call-start = ((), (), s32[]{:S(2)}) async-start(), calls=%async_computation.8 | async-start | bytes 4718592 | tf_op jit(solution)/shard_map/reduce_scatter | solution.py:248
  306.4 40.1 %collective-permute-start.19 = (bf16[256,2048]{1,0:T(8,128)(2,1)}, bf16[256,2048]{1,0:T(8,128)(2,1)}, u32[]{:S(2)}, u32[]{:S(2)}) collective-permute-start(bf16[256,2048]{1,0:T(8,128)(2,1)} %slice.257), channel_id=1, source_target_pairs={{0,8},{8,0},{16,24},{24,16},{1,9},{9,1},{17,25},{25,17},{2,10},{10... | collective-permute-start | bytes 3145736 | tf_op jit(solution)/shard_map/ppermute | solution.py:21
  310.3 37.4 %collective-permute-start.20 = (bf16[256,2048]{1,0:T(8,128)(2,1)}, bf16[256,2048]{1,0:T(8,128)(2,1)}, u32[]{:S(2)}, u32[]{:S(2)}) collective-permute-start(bf16[256,2048]{1,0:T(8,128)(2,1)} %slice.258), channel_id=1, source_target_pairs={{0,16},{8,24},{16,0},{24,8},{1,17},{9,25},{17,1},{25,9},{2,18},{10... | collective-permute-start | bytes 3145736 | tf_op jit(solution)/shard_map/ppermute | solution.py:21
  350.6 51.3 %collective-permute-start.24 = (bf16[256,2048]{1,0:T(8,128)(2,1)}, bf16[256,2048]{1,0:T(8,128)(2,1)}, u32[]{:S(2)}, u32[]{:S(2)}) collective-permute-start(bf16[256,2048]{1,0:T(8,128)(2,1)} %add_convert_fusion.4), channel_id=1, source_target_pairs={{0,8},{8,0},{16,24},{24,16},{1,9},{9,1},{17,25},{25,17},{2,10},{10... | collective-permute-start | bytes 3145736 | tf_op jit(solution)/shard_map/ppermute | solution.py:21
  353.7 48.2 %collective-permute-start.25 = (bf16[256,2048]{1,0:T(8,128)(2,1)}, bf16[256,2048]{1,0:T(8,128)(2,1)}, u32[]{:S(2)}, u32[]{:S(2)}) collective-permute-start(bf16[256,2048]{1,0:T(8,128)(2,1)} %add_convert_fusion.3), channel_id=1, source_target_pairs={{0,16},{8,24},{16,0},{24,8},{1,17},{9,25},{17,1},{25,9},{2,18},{10... | collective-permute-start | bytes 3145736 | tf_op jit(solution)/shard_map/ppermute | solution.py:21
  356.6 150.7 %reduce-scatter.9.cloned.1.call-start = ((), (), s32[]{:S(2)}) async-start(), calls=%async_computation.9 | async-start | bytes 2359296 | tf_op jit(solution)/shard_map/reduce_scatter | solution.py:248
  361.7 38.7 %collective-permute-start.22 = (bf16[128,2048]{1,0:T(8,128)(2,1)S(1)}, bf16[128,2048]{1,0:T(8,128)(2,1)}, u32[]{:S(2)}, u32[]{:S(2)}) collective-permute-start(bf16[128,2048]{1,0:T(8,128)(2,1)S(1)} %fusion.51), channel_id=1, source_target_pairs={{0,16},{8,24},{16,0},{24,8},{1,17},{9,25},{17,1},{25,9},{2,18},{10... | collective-permute-start | bytes 1572872 | tf_op jit(solution)/shard_map/ppermute | solution.py:21
  363.2 37.3 %collective-permute-start.21 = (bf16[128,2048]{1,0:T(8,128)(2,1)S(1)}, bf16[128,2048]{1,0:T(8,128)(2,1)}, u32[]{:S(2)}, u32[]{:S(2)}) collective-permute-start(bf16[128,2048]{1,0:T(8,128)(2,1)S(1)} %fusion.51), channel_id=1, source_target_pairs={{0,8},{8,0},{16,24},{24,16},{1,9},{9,1},{17,25},{25,17},{2,10},{10... | collective-permute-start | bytes 1572872 | tf_op jit(solution)/shard_map/ppermute | solution.py:21
  428.1 38.2 %collective-permute-start.30 = (bf16[256,2048]{1,0:T(8,128)(2,1)}, bf16[256,2048]{1,0:T(8,128)(2,1)}, u32[]{:S(2)}, u32[]{:S(2)}) collective-permute-start(bf16[256,2048]{1,0:T(8,128)(2,1)} %pad_maximum_fusion.7), channel_id=1, source_target_pairs={{0,8},{8,0},{16,24},{24,16},{1,9},{9,1},{17,25},{25,17},{2,10},{10... | collective-permute-start | bytes 3145736 | tf_op jit(solution)/shard_map/ppermute | solution.py:21
  430.9 35.4 %collective-permute-start.31 = (bf16[256,2048]{1,0:T(8,128)(2,1)}, bf16[256,2048]{1,0:T(8,128)(2,1)}, u32[]{:S(2)}, u32[]{:S(2)}) collective-permute-start(bf16[256,2048]{1,0:T(8,128)(2,1)} %pad_maximum_fusion.8), channel_id=1, source_target_pairs={{0,16},{8,24},{16,0},{24,8},{1,17},{9,25},{17,1},{25,9},{2,18},{10... | collective-permute-start | bytes 3145736 | tf_op jit(solution)/shard_map/ppermute | solution.py:21
  432.4 33.9 %collective-permute-start.32 = (bf16[2,64,2048]{2,1,0:T(8,128)(2,1)}, bf16[2,64,2048]{2,1,0:T(8,128)(2,1)}, u32[]{:S(2)}, u32[]{:S(2)}) collective-permute-start(bf16[2,64,2048]{2,1,0:T(8,128)(2,1)} %get-tuple-element.153), channel_id=1, source_target_pairs={{0,6},{1,7},{2,4},{3,5},{4,2},{5,3},{6,0},{7,1},{8,14},{9,15},{10,... | collective-permute-start | bytes 1572872 | tf_op jit(solution)/shard_map/ppermute | solution.py:21
  439.3 139.9 %reduce-scatter.11.cloned.1.call-start = ((), (), s32[]{:S(2)}) async-start(), calls=%async_computation.10 | async-start | bytes 7077888 | tf_op jit(solution)/shard_map/reduce_scatter | solution.py:248
  511.2 139.7 %all-gather.16.cloned.1.call-start = ((), (), s32[]{:S(2)}) async-start(), calls=%async_computation.12 | async-start | bytes 3932160 | tf_op jit(solution)/shard_map/all_gather | solution.py:500
  517.8 34.3 %collective-permute-start.44 = (bf16[4,64,2048]{2,1,0:T(8,128)(2,1)}, bf16[4,64,2048]{2,1,0:T(8,128)(2,1)}, u32[]{:S(2)}, u32[]{:S(2)}) collective-permute-start(bf16[4,64,2048]{2,1,0:T(8,128)(2,1)} %collective-permute-done.33.piece_ref), channel_id=1, source_target_pairs={{0,16},{8,24},{16,0},{24,8},{1,17},{9,25},{17,1},{25,9},{2,18},{10... | collective-permute-start | bytes 3145736 | tf_op jit(solution)/shard_map/ppermute | solution.py:21
  524.3 46.8 %collective-permute-start.41 = (bf16[4,64,2048]{2,1,0:T(8,128)(2,1)}, bf16[4,64,2048]{2,1,0:T(8,128)(2,1)}, u32[]{:S(2)}, u32[]{:S(2)}) collective-permute-start(bf16[4,64,2048]{2,1,0:T(8,128)(2,1)} %constant_dynamic-update-slice_fusion.6.piece_ref), channel_id=1, source_target_pairs={{0,16},{8,24},{16,0},{24,8},{1,17},{9,25},{17,1},{25,9},{2,18},{10... | collective-permute-start | bytes 3145736 | tf_op jit(solution)/shard_map/ppermute | solution.py:21
  579.2 56.9 %collective-permute-start.45 = (bf16[4,64,2048]{2,1,0:T(8,128)(2,1)}, bf16[4,64,2048]{2,1,0:T(8,128)(2,1)S(1)}, u32[]{:S(2)}, u32[]{:S(2)}) collective-permute-start(bf16[4,64,2048]{2,1,0:T(8,128)(2,1)} %collective-permute-done.41.piece_ref), channel_id=1, source_target_pairs={{0,8},{8,0},{16,24},{24,16},{1,9},{9,1},{17,25},{25,17},{2,10},{10... | collective-permute-start | bytes 3145736 | tf_op jit(solution)/shard_map/ppermute | solution.py:21
  581.9 40.6 %collective-permute-start.46 = (bf16[128,2048]{1,0:T(8,128)(2,1)S(1)}, bf16[128,2048]{1,0:T(8,128)(2,1)S(1)}, u32[]{:S(2)}, u32[]{:S(2)}) collective-permute-start(bf16[128,2048]{1,0:T(8,128)(2,1)S(1)} %slice.233), channel_id=1, source_target_pairs={{0,16},{8,24},{16,0},{24,8},{1,17},{9,25},{17,1},{25,9},{2,18},{10... | collective-permute-start | bytes 1572872 | tf_op jit(solution)/shard_map/ppermute | solution.py:21
  584.5 51.7 %collective-permute-start.47 = (bf16[128,2048]{1,0:T(8,128)(2,1)S(1)}, bf16[128,2048]{1,0:T(8,128)(2,1)S(1)}, u32[]{:S(2)}, u32[]{:S(2)}) collective-permute-start(bf16[128,2048]{1,0:T(8,128)(2,1)S(1)} %slice.234), channel_id=1, source_target_pairs={{0,8},{8,0},{16,24},{24,16},{1,9},{9,1},{17,25},{25,17},{2,10},{10... | collective-permute-start | bytes 1572872 | tf_op jit(solution)/shard_map/ppermute | solution.py:21
  (100 other events, 1431.2 us)
Sparse Core Ops, SparseCore 0:
  14.2 109.7 all-gather.7
  126.1 27.0 all-gather.9
  154.8 46.6 all-gather.13
  203.5 45.8 all-gather.11
  297.0 48.7 reduce-scatter.4
  356.7 47.7 reduce-scatter.6
  439.4 38.2 reduce-scatter.8
  511.3 67.8 reduce-scatter.10
  581.1 66.6 all-gather.15

commit v5 on v4

--- a/solution.py
+++ b/solution.py
@@ -131,6 +131,12 @@
     return jnp.concatenate(
         [plus(own[:half], arrived[2], late[1]), plus(own[half:], arrived[3], late[0])], 0
     )
+
+
+def paired_sum(terms):
+    while len(terms) > 1:
+        terms = [terms[i] + terms[i + 1] for i in range(0, len(terms), 2)]
+    return terms[0]
 
 
 def plus(*terms):
@@ -553,7 +559,7 @@
         grad_out = stacked([(piece, k, 0) for k, piece in enumerate(out_pieces)], w_out.shape)
     else:
         grad_out = out_pieces[0].astype(jnp.float32)
-    grad_gains = butterfly(grad_gains, "ctx")
+    grad_gains = paired_sum(gathered(grad_gains, "ctx"))
     grad_gains = lax.dynamic_slice_in_dim(grad_gains, lax.axis_index("fsdp") * shard, shard, 1)
     if strided:
         grad_w_qkv = pl.pallas_call(

time: 677 us -> 676 us (level)
    ppermute x56 -> x57, waiting for transfers between devices: 206 us -> 203 us  [swapped(): return lax.ppermute(array, axis, [(i, i ^ by) for i in range(size)])]
    ppermute x56 -> x57, starting transfers between devices: 63 us -> 64.4 us  [swapped(): return lax.ppermute(array, axis, [(i, i ^ by) for i in range(size)])]
  transfers between devices with their start and end apart: 65 -> 66, of which waited for: 31 -> 30; matrix products, arithmetic and copies ran while one was open for 25% -> 25% of each run, Pallas kernels for 10% -> 10%
where the time goes in v5:
time: 676 us; the launch traced here: 670 us
  waiting for transfers between devices  239 us (35%)
  matrix products  113 us (17%)
  Pallas kernels  66.2 us (10%)
  starting transfers between devices  65.3 us (10%)
  local copies, waits for them, and re-layouts  64.5 us (10%)
  blocking collectives  53.6 us (8%)
  other arithmetic  52.8 us (8%)
  between operations  15.3 us (2%)
    ppermute x57, waiting for transfers between devices, swapped(): return lax.ppermute(array, axis, [(i, i ^ by) for i in range(size)])  203 us
    dot_general x15, matrix products, product(): lax.dot_general(left, right, (((left_dim,), (right_dim,)), ((), ())), pre...  91.5 us
    ppermute x57, starting transfers between devices, swapped(): return lax.ppermute(array, axis, [(i, i ^ by) for i in range(size)])  64.4 us
    all_gather x1, blocking collectives, per_device(): lax.all_gather(gains, 'fsdp', axis=1, tiled=True).astype(jnp.float32)  53.6 us
    pallas_call x13, Pallas kernels, placed(): pl.pallas_call(body, grid_spec=pltpu.PrefetchScalarGridSpec(num_scalar_pr...  50.3 us
    all_gather x4, waiting for transfers between devices, gather_rows(): return lax.all_gather(array, axis, axis=0, tiled=True)  27.1 us
    unnamed x141, local copies, waits for them, and re-layouts  26.3 us
    convert_element_type x12, other arithmetic, low(): return values.astype(jnp.bfloat16)  24.8 us
  transfers between devices with their start and end apart: 66, of which 30 were waited for; matrix products, arithmetic and copies ran while one was open for 25% of the time, Pallas kernels for 10%

profile of v5, /device:TPU:0, one launch (start us, length us, event | category | flops | bytes accessed | tf_op | source)
XLA Modules:
  0.0 669.9 jit_solution(17731501937011772873)
XLA Ops:
  7.2 4.7 copy.64
  15.0 7.8 %shard_map.161 = bf16[8,64,2048]{2,1,0:T(8,128)(2,1)} custom-call(s32[1]{0:T(128)} %bitcast.1.own_ref, bf16[256,2,8192]{2,1,0:T(2,128)(2,1)} %in_ref.1), custom_call_target="tpu_custom_call" | custom-call | flops 1 | bytes 1 | tf_op jit(solution)/shard_map/pallas_call | solution.py:314
  37.8 53.6 %all_gather.21 = bf16[2,2048]{1,0:T(2,128)(2,1)S(1)} all-gather(bf16[2,256]{1,0:T(2,128)(2,1)S(1)} %pad_maximum_fusion.29), channel_id=1, replica_groups=mesh['ctx'=4,'fsdp'=8] {'fsdp'}, dimensions={1}, use_global_device_ids=true | all-gather | bytes 9216 | tf_op jit(solution)/shard_map/all_gather | solution.py:333
  98.4 15.5 %collective-permute-done.6 = bf16[2,64,2048]{2,1,0:T(8,128)(2,1)S(1)} collective-permute-done((bf16[2,64,2048]{2,1,0:T(8,128)(2,1)S(1)}, bf16[2,64,2048]{2,1,0:T(8,128)(2,1)S(1)}, u32[]{:S(2)}, u32[]{:S(2)}) %collective-permute-start.6) | collective-permute-done | bytes 524320 | tf_op jit(solution)/shard_map/ppermute | solution.py:21
  116.3 7.7 %all-gather.8.cloned.1.call-done = bf16[2048,1536]{0,1:T(8,128)(2,1)} async-done(((bf16[256,1536]{0,1:T(8,128)(2,1)}), bf16[2048,1536]{0,1:T(8,128)(2,1)}) %all-gather.8.cloned.1.call-update) | async-done | bytes 6291472 | tf_op jit(solution)/shard_map/all_gather | solution.py:250
  126.7 6.0 fusion.23
  134.6 8.3 %fusion.62 = (f32[8,512]{1,0:T(8,128)S(1)}, f32[8,512,512]{1,2,0:T(8,128)}) fusion(pred[512,512]{0,1:T(8,128)(4,1)} %broadcast_compare_fusion, bf16[512,8,32]{0,2,1:T(8,128)(2,1)S(1)} %get-tuple-element.272, bf16[512,8,32]{0,2,1:T(8,128)(2,1)} %get-tuple-element.273, bf16[512,8,32]{0,2,1:T(8,128)(2,1)} %get-tuple-element.253, ...), kind=kOutput, calls=%fused_computation.205 | convolution fusion | flops 281018880 | bytes 9715712 | tf_op jit(solution)/shard_map/sub | solution.py:380
  142.9 4.7 fusion.6
  153.2 4.9 fusion.64
  163.3 21.3 %collective-permute-done.12 = bf16[128,2048]{1,0:T(8,128)(2,1)S(1)} collective-permute-done((bf16[128,2048]{1,0:T(8,128)(2,1)}, bf16[128,2048]{1,0:T(8,128)(2,1)S(1)}, u32[]{:S(2)}, u32[]{:S(2)}) %collective-permute-start.12) | collective-permute-done | bytes 524320 | tf_op jit(solution)/shard_map/ppermute | solution.py:21
  184.6 10.7 %collective-permute-done.11 = bf16[128,2048]{1,0:T(8,128)(2,1)S(1)} collective-permute-done((bf16[128,2048]{1,0:T(8,128)(2,1)}, bf16[128,2048]{1,0:T(8,128)(2,1)S(1)}, u32[]{:S(2)}, u32[]{:S(2)}) %collective-permute-start.11) | collective-permute-done | bytes 524320 | tf_op jit(solution)/shard_map/ppermute | solution.py:21
  216.8 11.4 %collective-permute-done.15 = bf16[256,2048]{1,0:T(8,128)(2,1)S(1)} collective-permute-done((bf16[256,2048]{1,0:T(8,128)(2,1)S(1)}, bf16[256,2048]{1,0:T(8,128)(2,1)S(1)}, u32[]{:S(2)}, u32[]{:S(2)}) %collective-permute-start.15) | collective-permute-done | bytes 1048608 | tf_op jit(solution)/shard_map/ppermute | solution.py:21
  231.8 17.6 %all-gather.12.cloned.1.call-done = bf16[1024,2048]{1,0:T(8,128)(2,1)} async-done(((bf16[128,2048]{1,0:T(8,128)(2,1)}), bf16[1024,2048]{1,0:T(8,128)(2,1)}) %all-gather.12.cloned.1.call-update) | async-done | bytes 4194320 | tf_op jit(solution)/shard_map/all_gather | solution.py:250
  249.4 15.4 %fusion.65 = f32[1024,2048]{0,1:T(8,128)} fusion(bf16[1024,2048]{1,0:T(8,128)(2,1)} %all-gather.12.cloned.1.call-done, bf16[2048,2048]{1,0:T(8,128)(2,1)} %constant_dynamic-update-slice_fusion.1), kind=kOutput, calls=%fused_computation.208 | convolution fusion | flops 8589934592 | bytes 20971520 | tf_op jit(solution)/shard_map/dot_general | solution.py:236
  264.8 9.3 %multiply_convert_fusion.3 = (bf16[1024,1024]{0,1:T(8,128)(2,1)S(1)}, bf16[1024,1024]{0,1:T(8,128)(2,1)S(1)}, bf16[1024,1024]{0,1:T(8,128)(2,1)}) fusion(f32[1024,2048]{0,1:T(8,128)} %fusion.65, bf16[1024,2048]{1,0:T(8,128)(2,1)S(1)} %bitcast.222, bf16[1024,2048]{1,0:T(8,128)(2,1)S(1)} %copy-done.53), kind=kOutput, calls=%fused_computation.10 | convolution fusion | flops 4310695936 | bytes 23068672 | tf_op jit(solution)/shard_map/dot_general | solution.py:236
  275.5 12.8 %convolution_convert_fusion.1 = bf16[1024,2048]{1,0:T(8,128)(2,1)} fusion(bf16[2048,2048]{1,0:T(8,128)(2,1)} %constant_dynamic-update-slice_fusion.1, bf16[1024,1024]{0,1:T(8,128)(2,1)S(1)} %get-tuple-element.217, bf16[1024,1024]{0,1:T(8,128)(2,1)S(1)} %get-tuple-element.216), kind=kOutput, calls=%fused_computation.19 | convolution fusion | flops 8600420352 | bytes 16777216 | tf_op jit(solution)/shard_map/dot_general | solution.py:236
  315.3 4.9 convolution_convert_fusion.2
  323.9 6.3 convolution_convert_fusion.3
  330.2 16.3 %collective-permute-done.19 = bf16[256,2048]{1,0:T(8,128)(2,1)} collective-permute-done((bf16[256,2048]{1,0:T(8,128)(2,1)}, bf16[256,2048]{1,0:T(8,128)(2,1)}, u32[]{:S(2)}, u32[]{:S(2)}) %collective-permute-start.19) | collective-permute-done | bytes 1048608 | tf_op jit(solution)/shard_map/ppermute | solution.py:21
  363.8 25.3 %collective-permute-done.23 = bf16[128,2048]{1,0:T(8,128)(2,1)S(1)} collective-permute-done((bf16[128,2048]{1,0:T(8,128)(2,1)S(1)}, bf16[128,2048]{1,0:T(8,128)(2,1)S(1)}, u32[]{:S(2)}, u32[]{:S(2)}) %collective-permute-start.23) | collective-permute-done | bytes 524320 | tf_op jit(solution)/shard_map/ppermute | solution.py:21
  389.1 11.4 %collective-permute-done.22 = bf16[128,2048]{1,0:T(8,128)(2,1)} collective-permute-done((bf16[128,2048]{1,0:T(8,128)(2,1)S(1)}, bf16[128,2048]{1,0:T(8,128)(2,1)}, u32[]{:S(2)}, u32[]{:S(2)}) %collective-permute-start.22) | collective-permute-done | bytes 524320 | tf_op jit(solution)/shard_map/ppermute | solution.py:21
  452.0 5.5 broadcast_multiply_fusion
  457.5 5.9 convolution_convert_fusion
  466.4 9.4 %collective-permute-done.33.piece_ref = bf16[4,64,2048]{2,1,0:T(8,128)(2,1)} collective-permute-done((bf16[4,64,2048]{2,1,0:T(8,128)(2,1)S(1)}, bf16[4,64,2048]{2,1,0:T(8,128)(2,1)}, u32[]{:S(2)}, u32[]{:S(2)}) %collective-permute-start.33) | collective-permute-done | bytes 1048608 | tf_op jit(solution)/shard_map/ppermute | solution.py:21
  487.3 20.0 %collective-permute-done.37 = bf16[2,64,2048]{2,1,0:T(8,128)(2,1)} collective-permute-done((bf16[2,64,2048]{2,1,0:T(8,128)(2,1)}, bf16[2,64,2048]{2,1,0:T(8,128)(2,1)}, u32[]{:S(2)}, u32[]{:S(2)}) %collective-permute-start.37) | collective-permute-done | bytes 524320 | tf_op jit(solution)/shard_map/ppermute | solution.py:21
  525.1 4.5 collective-permute-done.43
  540.6 4.5 shard_map.164.refs_0_
  552.2 18.9 %collective-permute-done.41.piece_ref = bf16[4,64,2048]{2,1,0:T(8,128)(2,1)} collective-permute-done((bf16[4,64,2048]{2,1,0:T(8,128)(2,1)}, bf16[4,64,2048]{2,1,0:T(8,128)(2,1)}, u32[]{:S(2)}, u32[]{:S(2)}) %collective-permute-start.41) | collective-permute-done | bytes 1048608 | tf_op jit(solution)/shard_map/ppermute | solution.py:21
  571.1 8.1 %reduce-scatter.11.cloned.1.call-done = bf16[256,1536]{1,0:T(8,128)(2,1)} async-done(((bf16[2048,1536]{1,0:T(8,128)(2,1)}), bf16[256,1536]{1,0:T(8,128)(2,1)}) %reduce-scatter.11.cloned.1.call-update) | async-done | bytes 786448 | tf_op jit(solution)/shard_map/reduce_scatter | solution.py:254
  585.1 4.5 shard_map.165.refs_0_
  624.9 11.3 %collective-permute-done.47 = bf16[128,2048]{1,0:T(8,128)(2,1)S(1)} collective-permute-done((bf16[128,2048]{1,0:T(8,128)(2,1)S(1)}, bf16[128,2048]{1,0:T(8,128)(2,1)S(1)}, u32[]{:S(2)}, u32[]{:S(2)}) %collective-permute-start.47) | collective-permute-done | bytes 524320 | tf_op jit(solution)/shard_map/ppermute | solution.py:21
  654.4 5.4 shard_map.175
  (397 shorter events, 280.4 us)
Async XLA Ops:
  7.2 116.8 %all-gather.8.cloned.1.call-start = ((), (), s32[]{:S(2)}) async-start(), calls=%async_computation.4 | async-start | bytes 7077888 | tf_op jit(solution)/shard_map/all_gather | solution.py:250
  14.1 139.1 %all-gather.10.cloned.1.call-start = ((), (), s32[]{:S(2)}) async-start(), calls=%async_computation.5 | async-start | bytes 2359296 | tf_op jit(solution)/shard_map/all_gather | solution.py:250
  14.9 186.6 %all-gather.14.cloned.1.call-start = ((), (), s32[]{:S(2)}) async-start(), calls=%async_computation.11 | async-start | bytes 4718592 | tf_op jit(solution)/shard_map/all_gather | solution.py:250
  24.8 224.6 %all-gather.12.cloned.1.call-start = ((), (), s32[]{:S(2)}) async-start(), calls=%async_computation.6 | async-start | bytes 4718592 | tf_op jit(solution)/shard_map/all_gather | solution.py:250
  28.6 64.4 %collective-permute-start.3 = (bf16[128,2048]{1,0:T(8,128)(2,1)S(1)}, bf16[128,2048]{1,0:T(8,128)(2,1)S(1)}, u32[]{:S(2)}, u32[]{:S(2)}) collective-permute-start(bf16[128,2048]{1,0:T(8,128)(2,1)S(1)} %bitcast.204), channel_id=1, source_target_pairs={{0,24},{8,16},{16,8},{24,0},{1,25},{9,17},{17,9},{25,1},{2,26},{10... | collective-permute-start | bytes 1572872 | tf_op jit(solution)/shard_map/ppermute | solution.py:21
  32.8 60.2 %collective-permute-start.2 = (bf16[128,2048]{1,0:T(8,128)(2,1)S(1)}, bf16[128,2048]{1,0:T(8,128)(2,1)S(1)}, u32[]{:S(2)}, u32[]{:S(2)}) collective-permute-start(bf16[128,2048]{1,0:T(8,128)(2,1)S(1)} %bitcast.205), channel_id=1, source_target_pairs={{0,16},{8,24},{16,0},{24,8},{1,17},{9,25},{17,1},{25,9},{2,18},{10... | collective-permute-start | bytes 1572872 | tf_op jit(solution)/shard_map/ppermute | solution.py:21
  33.3 59.6 %collective-permute-start.1 = (bf16[128,2048]{1,0:T(8,128)(2,1)S(1)}, bf16[128,2048]{1,0:T(8,128)(2,1)S(1)}, u32[]{:S(2)}, u32[]{:S(2)}) collective-permute-start(bf16[128,2048]{1,0:T(8,128)(2,1)S(1)} %bitcast.206), channel_id=1, source_target_pairs={{0,8},{8,0},{16,24},{24,16},{1,9},{9,1},{17,25},{25,17},{2,10},{10... | collective-permute-start | bytes 1572872 | tf_op jit(solution)/shard_map/ppermute | solution.py:21
  33.4 63.0 %collective-permute-start.4 = (bf16[2,64,2048]{2,1,0:T(8,128)(2,1)S(1)}, bf16[2,64,2048]{2,1,0:T(8,128)(2,1)S(1)}, u32[]{:S(2)}, u32[]{:S(2)}) collective-permute-start(bf16[2,64,2048]{2,1,0:T(8,128)(2,1)S(1)} %get-tuple-element.113), channel_id=1, source_target_pairs={{0,2},{1,3},{2,0},{3,1},{4,6},{5,7},{6,4},{7,5},{8,10},{9,11},{10,... | collective-permute-start | bytes 1572872 | tf_op jit(solution)/shard_map/ppermute | solution.py:21
  35.4 62.2 %collective-permute-start.5 = (bf16[2,64,2048]{2,1,0:T(8,128)(2,1)S(1)}, bf16[2,64,2048]{2,1,0:T(8,128)(2,1)S(1)}, u32[]{:S(2)}, u32[]{:S(2)}) collective-permute-start(bf16[2,64,2048]{2,1,0:T(8,128)(2,1)S(1)} %get-tuple-element.114), channel_id=1, source_target_pairs={{0,4},{1,5},{2,6},{3,7},{4,0},{5,1},{6,2},{7,3},{8,12},{9,13},{10,... | collective-permute-start | bytes 1572872 | tf_op jit(solution)/shard_map/ppermute | solution.py:21
  124.0 77.5 %collective-permute-start.13 = (bf16[512,2048]{1,0:T(8,128)(2,1)}, bf16[512,2048]{1,0:T(8,128)(2,1)}, u32[]{:S(2)}, u32[]{:S(2)}) collective-permute-start(bf16[512,2048]{1,0:T(8,128)(2,1)} %bitcast.16), channel_id=1, source_target_pairs={{0,8},{8,0},{16,24},{24,16},{1,9},{9,1},{17,25},{25,17},{2,10},{10... | collective-permute-start | bytes 6291464 | tf_op jit(solution)/shard_map/ppermute | solution.py:21
  125.2 76.3 %collective-permute-start.14 = (bf16[512,2048]{1,0:T(8,128)(2,1)}, bf16[512,2048]{1,0:T(8,128)(2,1)}, u32[]{:S(2)}, u32[]{:S(2)}) collective-permute-start(bf16[512,2048]{1,0:T(8,128)(2,1)} %bitcast.16), channel_id=1, source_target_pairs={{0,16},{8,24},{16,0},{24,8},{1,17},{9,25},{17,1},{25,9},{2,18},{10... | collective-permute-start | bytes 6291464 | tf_op jit(solution)/shard_map/ppermute | solution.py:21
  161.6 33.7 %collective-permute-start.11 = (bf16[128,2048]{1,0:T(8,128)(2,1)}, bf16[128,2048]{1,0:T(8,128)(2,1)S(1)}, u32[]{:S(2)}, u32[]{:S(2)}) collective-permute-start(bf16[128,2048]{1,0:T(8,128)(2,1)} %get-tuple-element.244), channel_id=1, source_target_pairs={{0,16},{8,24},{16,0},{24,8},{1,17},{9,25},{17,1},{25,9},{2,18},{10... | collective-permute-start | bytes 1572872 | tf_op jit(solution)/shard_map/ppermute | solution.py:21
  162.2 33.2 %collective-permute-start.10 = (bf16[128,2048]{1,0:T(8,128)(2,1)}, bf16[128,2048]{1,0:T(8,128)(2,1)}, u32[]{:S(2)}, u32[]{:S(2)}) collective-permute-start(bf16[128,2048]{1,0:T(8,128)(2,1)} %get-tuple-element.242), channel_id=1, source_target_pairs={{0,8},{8,0},{16,24},{24,16},{1,9},{9,1},{17,25},{25,17},{2,10},{10... | collective-permute-start | bytes 1572872 | tf_op jit(solution)/shard_map/ppermute | solution.py:21
  201.5 153.7 %reduce-scatter.5.cloned.1.call-start = ((), (), s32[]{:S(2)}) async-start(), calls=%async_computation.7 | async-start | bytes 4718592 | tf_op jit(solution)/shard_map/reduce_scatter | solution.py:254
  296.9 181.4 %reduce-scatter.7.cloned.1.call-start = ((), (), s32[]{:S(2)}) async-start(), calls=%async_computation.8 | async-start | bytes 4718592 | tf_op jit(solution)/shard_map/reduce_scatter | solution.py:254
  306.5 40.1 %collective-permute-start.19 = (bf16[256,2048]{1,0:T(8,128)(2,1)}, bf16[256,2048]{1,0:T(8,128)(2,1)}, u32[]{:S(2)}, u32[]{:S(2)}) collective-permute-start(bf16[256,2048]{1,0:T(8,128)(2,1)} %slice.257), channel_id=1, source_target_pairs={{0,8},{8,0},{16,24},{24,16},{1,9},{9,1},{17,25},{25,17},{2,10},{10... | collective-permute-start | bytes 3145736 | tf_op jit(solution)/shard_map/ppermute | solution.py:21
  310.3 37.4 %collective-permute-start.20 = (bf16[256,2048]{1,0:T(8,128)(2,1)}, bf16[256,2048]{1,0:T(8,128)(2,1)}, u32[]{:S(2)}, u32[]{:S(2)}) collective-permute-start(bf16[256,2048]{1,0:T(8,128)(2,1)} %slice.258), channel_id=1, source_target_pairs={{0,16},{8,24},{16,0},{24,8},{1,17},{9,25},{17,1},{25,9},{2,18},{10... | collective-permute-start | bytes 3145736 | tf_op jit(solution)/shard_map/ppermute | solution.py:21
  350.6 51.3 %collective-permute-start.24 = (bf16[256,2048]{1,0:T(8,128)(2,1)}, bf16[256,2048]{1,0:T(8,128)(2,1)}, u32[]{:S(2)}, u32[]{:S(2)}) collective-permute-start(bf16[256,2048]{1,0:T(8,128)(2,1)} %add_convert_fusion.4), channel_id=1, source_target_pairs={{0,8},{8,0},{16,24},{24,16},{1,9},{9,1},{17,25},{25,17},{2,10},{10... | collective-permute-start | bytes 3145736 | tf_op jit(solution)/shard_map/ppermute | solution.py:21
  353.8 48.2 %collective-permute-start.25 = (bf16[256,2048]{1,0:T(8,128)(2,1)}, bf16[256,2048]{1,0:T(8,128)(2,1)}, u32[]{:S(2)}, u32[]{:S(2)}) collective-permute-start(bf16[256,2048]{1,0:T(8,128)(2,1)} %add_convert_fusion.3), channel_id=1, source_target_pairs={{0,16},{8,24},{16,0},{24,8},{1,17},{9,25},{17,1},{25,9},{2,18},{10... | collective-permute-start | bytes 3145736 | tf_op jit(solution)/shard_map/ppermute | solution.py:21
  356.6 150.7 %reduce-scatter.9.cloned.1.call-start = ((), (), s32[]{:S(2)}) async-start(), calls=%async_computation.9 | async-start | bytes 2359296 | tf_op jit(solution)/shard_map/reduce_scatter | solution.py:254
  361.8 38.7 %collective-permute-start.22 = (bf16[128,2048]{1,0:T(8,128)(2,1)S(1)}, bf16[128,2048]{1,0:T(8,128)(2,1)}, u32[]{:S(2)}, u32[]{:S(2)}) collective-permute-start(bf16[128,2048]{1,0:T(8,128)(2,1)S(1)} %fusion.53), channel_id=1, source_target_pairs={{0,16},{8,24},{16,0},{24,8},{1,17},{9,25},{17,1},{25,9},{2,18},{10... | collective-permute-start | bytes 1572872 | tf_op jit(solution)/shard_map/ppermute | solution.py:21
  363.2 37.3 %collective-permute-start.21 = (bf16[128,2048]{1,0:T(8,128)(2,1)S(1)}, bf16[128,2048]{1,0:T(8,128)(2,1)}, u32[]{:S(2)}, u32[]{:S(2)}) collective-permute-start(bf16[128,2048]{1,0:T(8,128)(2,1)S(1)} %fusion.53), channel_id=1, source_target_pairs={{0,8},{8,0},{16,24},{24,16},{1,9},{9,1},{17,25},{25,17},{2,10},{10... | collective-permute-start | bytes 1572872 | tf_op jit(solution)/shard_map/ppermute | solution.py:21
  428.1 38.2 %collective-permute-start.30 = (bf16[256,2048]{1,0:T(8,128)(2,1)}, bf16[256,2048]{1,0:T(8,128)(2,1)}, u32[]{:S(2)}, u32[]{:S(2)}) collective-permute-start(bf16[256,2048]{1,0:T(8,128)(2,1)} %pad_maximum_fusion.7), channel_id=1, source_target_pairs={{0,8},{8,0},{16,24},{24,16},{1,9},{9,1},{17,25},{25,17},{2,10},{10... | collective-permute-start | bytes 3145736 | tf_op jit(solution)/shard_map/ppermute | solution.py:21
  431.0 35.4 %collective-permute-start.31 = (bf16[256,2048]{1,0:T(8,128)(2,1)}, bf16[256,2048]{1,0:T(8,128)(2,1)}, u32[]{:S(2)}, u32[]{:S(2)}) collective-permute-start(bf16[256,2048]{1,0:T(8,128)(2,1)} %pad_maximum_fusion.8), channel_id=1, source_target_pairs={{0,16},{8,24},{16,0},{24,8},{1,17},{9,25},{17,1},{25,9},{2,18},{10... | collective-permute-start | bytes 3145736 | tf_op jit(solution)/shard_map/ppermute | solution.py:21
  432.4 33.9 %collective-permute-start.32 = (bf16[2,64,2048]{2,1,0:T(8,128)(2,1)}, bf16[2,64,2048]{2,1,0:T(8,128)(2,1)}, u32[]{:S(2)}, u32[]{:S(2)}) collective-permute-start(bf16[2,64,2048]{2,1,0:T(8,128)(2,1)} %get-tuple-element.153), channel_id=1, source_target_pairs={{0,6},{1,7},{2,4},{3,5},{4,2},{5,3},{6,0},{7,1},{8,14},{9,15},{10,... | collective-permute-start | bytes 1572872 | tf_op jit(solution)/shard_map/ppermute | solution.py:21
  439.3 139.9 %reduce-scatter.11.cloned.1.call-start = ((), (), s32[]{:S(2)}) async-start(), calls=%async_computation.10 | async-start | bytes 7077888 | tf_op jit(solution)/shard_map/reduce_scatter | solution.py:254
  511.3 139.7 %all-gather.16.cloned.1.call-start = ((), (), s32[]{:S(2)}) async-start(), calls=%async_computation.12 | async-start | bytes 3932160 | tf_op jit(solution)/shard_map/all_gather | solution.py:506
  517.8 34.3 %collective-permute-start.44 = (bf16[4,64,2048]{2,1,0:T(8,128)(2,1)}, bf16[4,64,2048]{2,1,0:T(8,128)(2,1)}, u32[]{:S(2)}, u32[]{:S(2)}) collective-permute-start(bf16[4,64,2048]{2,1,0:T(8,128)(2,1)} %collective-permute-done.33.piece_ref), channel_id=1, source_target_pairs={{0,16},{8,24},{16,0},{24,8},{1,17},{9,25},{17,1},{25,9},{2,18},{10... | collective-permute-start | bytes 3145736 | tf_op jit(solution)/shard_map/ppermute | solution.py:21
  524.3 46.8 %collective-permute-start.41 = (bf16[4,64,2048]{2,1,0:T(8,128)(2,1)}, bf16[4,64,2048]{2,1,0:T(8,128)(2,1)}, u32[]{:S(2)}, u32[]{:S(2)}) collective-permute-start(bf16[4,64,2048]{2,1,0:T(8,128)(2,1)} %constant_dynamic-update-slice_fusion.6.piece_ref), channel_id=1, source_target_pairs={{0,16},{8,24},{16,0},{24,8},{1,17},{9,25},{17,1},{25,9},{2,18},{10... | collective-permute-start | bytes 3145736 | tf_op jit(solution)/shard_map/ppermute | solution.py:21
  579.3 56.9 %collective-permute-start.45 = (bf16[4,64,2048]{2,1,0:T(8,128)(2,1)}, bf16[4,64,2048]{2,1,0:T(8,128)(2,1)S(1)}, u32[]{:S(2)}, u32[]{:S(2)}) collective-permute-start(bf16[4,64,2048]{2,1,0:T(8,128)(2,1)} %collective-permute-done.41.piece_ref), channel_id=1, source_target_pairs={{0,8},{8,0},{16,24},{24,16},{1,9},{9,1},{17,25},{25,17},{2,10},{10... | collective-permute-start | bytes 3145736 | tf_op jit(solution)/shard_map/ppermute | solution.py:21
  581.9 40.6 %collective-permute-start.46 = (bf16[128,2048]{1,0:T(8,128)(2,1)S(1)}, bf16[128,2048]{1,0:T(8,128)(2,1)S(1)}, u32[]{:S(2)}, u32[]{:S(2)}) collective-permute-start(bf16[128,2048]{1,0:T(8,128)(2,1)S(1)} %slice.233), channel_id=1, source_target_pairs={{0,16},{8,24},{16,0},{24,8},{1,17},{9,25},{17,1},{25,9},{2,18},{10... | collective-permute-start | bytes 1572872 | tf_op jit(solution)/shard_map/ppermute | solution.py:21
  584.5 51.6 %collective-permute-start.47 = (bf16[128,2048]{1,0:T(8,128)(2,1)S(1)}, bf16[128,2048]{1,0:T(8,128)(2,1)S(1)}, u32[]{:S(2)}, u32[]{:S(2)}) collective-permute-start(bf16[128,2048]{1,0:T(8,128)(2,1)S(1)} %slice.234), channel_id=1, source_target_pairs={{0,8},{8,0},{16,24},{24,16},{1,9},{9,1},{17,25},{25,17},{2,10},{10... | collective-permute-start | bytes 1572872 | tf_op jit(solution)/shard_map/ppermute | solution.py:21
  (101 other events, 1449.1 us)
Sparse Core Ops, SparseCore 0:
  14.2 109.7 all-gather.7
  126.2 26.9 all-gather.9
  154.8 46.6 all-gather.13
  203.5 45.8 all-gather.11
  297.0 48.7 reduce-scatter.4
  356.8 47.7 reduce-scatter.6
  439.5 38.3 reduce-scatter.8
  511.4 67.7 reduce-scatter.10
  581.1 66.6 all-gather.15
